TPU v7x, 128 devices: a whole 4x4x4 slice. The times are simulated.
128 devices in a mesh: list: 32 (over x, z, core), help: 4 (over y).
Axes of the slice: x: 4, y: 4, z: 4, core: 2. Of those that a mesh axis runs over, the one named last changes fastest.
Arguments:
- members: bfloat16 [524288, 768], P(('list', 'help')), may hold values from -6 to 6
- owner: int32 [524288, 1], P(('list', 'help')), may hold values from 0 to 63; in each aligned block of 4096 rows (0 to 4095, 4096 to 8191, ...) at most 128 rows name the same one
- seed_label: int32 [524288], P(('list', 'help')), may hold values from 0 to 7
Outputs:
- assignments: float32 [8, 524288], P(None, ('list', 'help'))
- centroids: float32 [64, 8, 768], P('list')
Inputs may be any that keep to these rules, and one draw needn't show every extreme that they name: `owner`: in each device's block of 4096 members no list is named by more than 128 of them, a bound that some block reaches; every list has members.
All inputs are finite; a program needn't handle non-finite values.
Results may differ from a plain program's by a relative error of at most 0.012.
The roundings to bfloat16 on the way count: a program that leaves them out, or rounds other values in their place, can miss the bound.
Values may be sent and summed in bfloat16 or wider, within the bound.
No kernel may reach another device: no remote copies, remote signals or barrier semaphores. Data moves between devices by JAX's collectives and lax.ppermute only.
A program may use at most 128 MiB of HBM per device.

v0:
```python
import jax
import jax.numpy as jnp
from jax import lax
from jax.sharding import PartitionSpec as P

K = 8
ITERS = 3
LIST_DEV = 2


smoothing_heat_factor = 2.0


def local(members, owner, seed_label):
    row_count, width = members.shape
    n_list = lax.axis_size("list")
    lists_all = n_list * LIST_DEV
    owner_ids = owner[:, 0]
    list_iota = jnp.arange(lists_all, dtype=jnp.int32)
    group_iota = jnp.arange(K, dtype=jnp.int32)
    capacity = max(2, (2 * row_count + lists_all - 1) // lists_all)
    per_index = LIST_DEV * capacity
    list_hot_int = (owner_ids[:, None] == list_iota[None, :]).astype(jnp.int32)
    rank_in = jnp.sum(jnp.cumsum(list_hot_int, axis=0) * list_hot_int, axis=1) - 1
    slot_pos = owner_ids * capacity + rank_in
    outgoing = jnp.zeros((lists_all * capacity, width), jnp.bfloat16).at[slot_pos].set(members)
    tags = (
        jnp.zeros((lists_all * capacity,), jnp.bfloat16)
        .at[slot_pos]
        .set((seed_label + 1).astype(jnp.bfloat16))
    )
    shipped = outgoing.reshape(n_list, per_index, width)
    shipped_tags = tags.reshape(n_list, per_index)
    arrived, received_labels_list = (
        lax.all_to_all(shipped, "list", split_axis=0, concat_axis=0, tiled=True),
        lax.all_to_all(shipped_tags, "list", split_axis=0, concat_axis=0, tiled=True),
    )
    arrived = arrived.reshape(n_list, LIST_DEV, capacity, width)
    tag_vals = received_labels_list.astype(jnp.float32).reshape(n_list, LIST_DEV, capacity)
    present = (tag_vals > 0.5).astype(jnp.float32)
    labels = tag_vals - 1.0

    def group_update(weights_bf):
        sums = jnp.einsum("sqck,sqcd->qkd", weights_bf, arrived, preferred_element_type=jnp.float32)
        totals = jnp.sum(weights_bf.astype(jnp.float32), axis=(0, 2))
        sums, totals = lax.psum((sums, totals), "help")
        return sums / (totals + 1.0)[:, :, None]

    def holder_mapping(centers):
        separation_measures = jnp.einsum(
            "sqcd,qkd->sqck",
            arrived,
            centers.astype(jnp.bfloat16),
            preferred_element_type=jnp.float32,
        )
        centroid_magnitude_power = jnp.sum(centers * centers, axis=-1)[None, :, None, :]
        membership_raw_preference = (
            2.0 * separation_measures - centroid_magnitude_power
        ) / smoothing_heat_factor
        return jax.nn.softmax(membership_raw_preference, axis=-1)

    init_weights = (labels[..., None] == group_iota.astype(jnp.float32)).astype(jnp.bfloat16)
    centers = group_update(init_weights)
    for turn in range(ITERS):
        weights = (holder_mapping(centers) * present[..., None]).astype(jnp.bfloat16)
        centers = group_update(weights)
    final = holder_mapping(centers)
    going_back = jnp.transpose(final, (3, 0, 1, 2)).reshape(K, n_list, per_index)
    returned = lax.all_to_all(going_back, "list", split_axis=1, concat_axis=1, tiled=True)
    assignments = returned.reshape(K, n_list * per_index)[:, slot_pos]
    return (assignments, centers)


def solution(mesh):
    placed = (P(("list", "help"), None), P(("list", "help"), None), P(("list", "help")))
    return jax.shard_map(
        local,
        mesh=mesh,
        in_specs=placed,
        out_specs=(P(None, ("list", "help")), P("list", None, None)),
        check_vma=False,
    )
```

profile of v0, /device:TPU:1, one launch (start us, length us, event | category | flops | bytes accessed | tf_op | source)
XLA Modules:
  0.0 440.3 jit_solution(8046842960267865049)
XLA Ops:
  0.6 0.8 fusion.80
  1.5 18.4 %reduce-window.6 = s32[64,32,128]{2,1,0:T(8,128)S(1)} reduce-window(s32[64,32,128]{2,1,0:T(8,128)S(1)} %fusion.80, s32[]{:T(128)} %constant.14.clone.1), window={size=1x1x128 pad=0_0x0_0x127_0}, to_apply=%region_0.0 | reduce-window | flops 33292288 | bytes 2097156 | tf_op jit(solution)/shard_map/reduce-window
  20.3 0.4 copy.46
  21.2 1.4 fusion.79
  22.7 0.7 compare_select_fusion
  23.4 0.7 add_convert_fusion
  24.1 28.6 %scatter_custom_fusion = bf16[8192]{0:T(1024)(128)(2,1)S(1)} fusion(s32[4096]{0:T(1024)S(1)} %bitcast.117, bf16[4096]{0:T(1024)(128)(2,1)S(1)} %add_convert_fusion, bf16[]{:T(256)} %constant.12.clone.1), kind=kCustom, calls=%fused_computation.99 | custom fusion | bytes 16386 | tf_op jit(solution)/shard_map/scatter | solution.py:30
  52.7 0.5 broadcast.153
  53.3 0.7 reduce
  54.0 0.6 reshape.128
  54.6 9.4 %all-to-all-start = ((bf16[32,2,128]{2,1,0:T(2,128)(2,1)}), bf16[32,2,128]{2,1,0:T(2,128)(2,1)S(1)}, u32[]{:S(2)}, u32[]{:S(2)}) async-start(bf16[32,2,128]{2,1,0:T(2,128)(2,1)} %reshape.128), calls=%async_computation | async-start | bytes 32768 | tf_op jit(solution)/shard_map/all_to_all | solution.py:36
  64.0 26.0 %scatter_custom_fusion.1 = bf16[8192,768]{1,0:T(8,128)(2,1)} fusion(s32[4096]{0:T(1024)S(1)} %bitcast.118, bf16[4096,768]{1,0:T(8,128)(2,1)} %param.3, bf16[]{:T(256)} %constant.12.clone.1), kind=kCustom, calls=%fused_computation.6 | custom fusion | bytes 12583424 | tf_op jit(solution)/shard_map/scatter | solution.py:26
  90.1 7.4 %all-to-all-start.1 = ((bf16[32,256,768]{2,1,0:T(8,128)(2,1)}), bf16[32,256,768]{2,1,0:T(8,128)(2,1)}, u32[]{:S(2)}, u32[]{:S(2)}) async-start(bf16[32,256,768]{2,1,0:T(8,128)(2,1)} %bitcast.107), calls=%async_computation.1 | async-start | bytes 25165824 | tf_op jit(solution)/shard_map/all_to_all | solution.py:35
  97.8 174.8 %all-to-all-done.1 = bf16[32,256,768]{2,1,0:T(8,128)(2,1)} async-done(((bf16[32,256,768]{2,1,0:T(8,128)(2,1)}), bf16[32,256,768]{2,1,0:T(8,128)(2,1)}, u32[]{:S(2)}, u32[]{:S(2)}) %all-to-all-start.1) | async-done | bytes 12582944 | tf_op jit(solution)/shard_map/all_to_all | solution.py:35
  272.6 5.6 %fusion.66 = f32[2,8,768]{2,1,0:T(8,128)S(1)} fusion(bf16[32,2,128,768]{3,2,1,0:T(8,128)(2,1)} %bitcast.9, f32[32,2,128]{2,0,1:T(8,128)S(1)} %copy.24, f32[8]{0:T(128)S(1)} %iota_convert_fusion), kind=kOutput, calls=%fused_computation.43 | convolution fusion | flops 100728832 | bytes 12664864 | tf_op jit(solution)/shard_map/sqck,sqcd->qkd/dot_general | solution.py:44
  278.2 14.0 %all-reduce.3 = (f32[2,8,768]{2,1,0:T(8,128)S(1)}, f32[2,8]{1,0:T(2,128)S(1)}) all-reduce(f32[2,8,768]{2,1,0:T(8,128)S(1)} %fusion.66, f32[2,8]{1,0:T(2,128)S(1)} %convert_reduce_fusion.3), channel_id=1, replica_groups=mesh['list'=32,'help'=4] {'help'}, use_global_device_ids=true, to_apply=%region_5.6 | all-reduce | flops 12304 | bytes 98432 | tf_op jit(solution)/shard_map/psum | solution.py:46
  292.4 6.4 %fusion.101 = (f32[32,2,128]{2,0,1:T(8,128)S(1)}, f32[32,2,128,8]{2,3,0,1:T(8,128)S(1)}) fusion(bf16[32,2,128,768]{3,2,1,0:T(8,128)(2,1)} %bitcast.9, f32[2,8]{1,0:T(2,128)S(1)} %multiply_reduce_fusion.3, f32[2,8,768]{2,1,0:T(8,128)S(1)} %get-tuple-element.14, f32[2,8]{1,0:T(2,128)S(1)} %broadcast_add_fusion.5), kind=kOutput, calls=%fused_computation.106 | convolution fusion | flops 101015560 | bytes 12927104 | tf_op jit(solution)/shard_map/sub | solution.py:60
  299.0 5.5 %fusion.69 = f32[2,8,768]{2,1,0:T(8,128)S(1)} fusion(bf16[32,2,128,8]{2,3,0,1:T(8,128)(2,1)S(1)} %get-tuple-element.23, bf16[32,2,128,768]{3,2,1,0:T(8,128)(2,1)} %bitcast.9), kind=kOutput, calls=%fused_computation.44 | convolution fusion | flops 100663296 | bytes 12763136 | tf_op jit(solution)/shard_map/sqck,sqcd->qkd/dot_general | solution.py:44
  304.5 11.3 %all-reduce.2 = (f32[2,8,768]{2,1,0:T(8,128)S(1)}, f32[2,8]{1,0:T(2,128)S(1)}) all-reduce(f32[2,8,768]{2,1,0:T(8,128)S(1)} %fusion.69, f32[2,8]{1,0:T(2,128)S(1)} %get-tuple-element.22), channel_id=1, replica_groups=mesh['list'=32,'help'=4] {'help'}, use_global_device_ids=true, to_apply=%region_11.12 | all-reduce | flops 12304 | bytes 98432 | tf_op jit(solution)/shard_map/psum | solution.py:46
  316.0 6.4 %fusion.102 = (f32[32,2,128]{2,0,1:T(8,128)S(1)}, f32[32,2,128,8]{2,3,0,1:T(8,128)S(1)}) fusion(bf16[32,2,128,768]{3,2,1,0:T(8,128)(2,1)} %bitcast.9, f32[2,8]{1,0:T(2,128)S(1)} %multiply_reduce_fusion.2, f32[2,8,768]{2,1,0:T(8,128)S(1)} %get-tuple-element.12, f32[2,8]{1,0:T(2,128)S(1)} %broadcast_add_fusion.4), kind=kOutput, calls=%fused_computation.107 | convolution fusion | flops 101015560 | bytes 12927104 | tf_op jit(solution)/shard_map/sub | solution.py:60
  322.6 5.5 %fusion.72 = f32[2,8,768]{2,1,0:T(8,128)S(1)} fusion(bf16[32,2,128,8]{2,3,0,1:T(8,128)(2,1)S(1)} %get-tuple-element.21, bf16[32,2,128,768]{3,2,1,0:T(8,128)(2,1)} %bitcast.9), kind=kOutput, calls=%fused_computation.45 | convolution fusion | flops 100663296 | bytes 12763136 | tf_op jit(solution)/shard_map/sqck,sqcd->qkd/dot_general | solution.py:44
  328.1 12.7 %all-reduce.1 = (f32[2,8,768]{2,1,0:T(8,128)S(1)}, f32[2,8]{1,0:T(2,128)S(1)}) all-reduce(f32[2,8,768]{2,1,0:T(8,128)S(1)} %fusion.72, f32[2,8]{1,0:T(2,128)S(1)} %get-tuple-element.20), channel_id=1, replica_groups=mesh['list'=32,'help'=4] {'help'}, use_global_device_ids=true, to_apply=%region_17.18 | all-reduce | flops 12304 | bytes 98432 | tf_op jit(solution)/shard_map/psum | solution.py:46
  341.0 6.4 %fusion.103 = (f32[32,2,128]{2,0,1:T(8,128)S(1)}, f32[32,2,128,8]{2,3,0,1:T(8,128)S(1)}) fusion(bf16[32,2,128,768]{3,2,1,0:T(8,128)(2,1)} %bitcast.9, f32[2,8]{1,0:T(2,128)S(1)} %multiply_reduce_fusion.1, f32[2,8,768]{2,1,0:T(8,128)S(1)} %get-tuple-element.10, f32[2,8]{1,0:T(2,128)S(1)} %broadcast_add_fusion.3), kind=kOutput, calls=%fused_computation.108 | convolution fusion | flops 101015560 | bytes 12927104 | tf_op jit(solution)/shard_map/sub | solution.py:60
  347.5 5.5 %fusion.75 = f32[2,8,768]{2,1,0:T(8,128)S(1)} fusion(bf16[32,2,128,8]{2,3,0,1:T(8,128)(2,1)S(1)} %get-tuple-element.19, bf16[32,2,128,768]{3,2,1,0:T(8,128)(2,1)} %bitcast.9), kind=kOutput, calls=%fused_computation.46 | convolution fusion | flops 100663296 | bytes 12763136 | tf_op jit(solution)/shard_map/sqck,sqcd->qkd/dot_general | solution.py:44
  353.1 11.6 %all-reduce = (f32[2,8,768]{2,1,0:T(8,128)S(1)}, f32[2,8]{1,0:T(2,128)S(1)}) all-reduce(f32[2,8,768]{2,1,0:T(8,128)S(1)} %fusion.75, f32[2,8]{1,0:T(2,128)S(1)} %get-tuple-element.18), channel_id=1, replica_groups=mesh['list'=32,'help'=4] {'help'}, use_global_device_ids=true, to_apply=%region_23.24 | all-reduce | flops 12304 | bytes 98432 | tf_op jit(solution)/shard_map/psum | solution.py:46
  364.8 6.4 %bitcast_reduce_fusion = (f32[32,2,128]{2,0,1:T(8,128)S(1)}, f32[2,8,32,128]{3,1,2,0:T(8,128)S(1)}) fusion(f32[2,8]{1,0:T(2,128)S(1)} %get-tuple-element.16, bf16[32,2,128,768]{3,2,1,0:T(8,128)(2,1)} %bitcast.9, f32[2,8,768]{2,1,0:T(8,128)S(1)} %get-tuple-element.17), kind=kOutput, calls=%fused_computation.58 | convolution fusion | flops 100929536 | bytes 12927040 | tf_op jit(solution)/shard_map/sqcd,qkd->sqck/dot_general | solution.py:50
  371.4 0.8 copy_bitcast_fusion
  372.2 42.3 %all-to-all-start.2 = ((f32[8,32,256]{2,0,1:T(8,128)}), f32[8,32,256]{2,0,1:T(8,128)S(1)}, u32[]{:S(2)}, u32[]{:S(2)}) async-start(f32[8,32,256]{2,0,1:T(8,128)} %copy_bitcast_fusion), calls=%async_computation.2 | async-start | bytes 524288 | tf_op jit(solution)/shard_map/all_to_all | solution.py:69
  414.6 8.9 %all-to-all-done.2 = f32[8,32,256]{2,0,1:T(8,128)S(1)} async-done(((f32[8,32,256]{2,0,1:T(8,128)}), f32[8,32,256]{2,0,1:T(8,128)S(1)}, u32[]{:S(2)}, u32[]{:S(2)}) %all-to-all-start.2) | async-done | bytes 262176 | tf_op jit(solution)/shard_map/all_to_all | solution.py:69
  423.5 2.6 copy.36
  426.1 13.0 %gather_fusion = f32[4096,8]{1,0:T(8,128)S(1)} fusion(f32[8,8192]{0,1:T(8,128)} %bitcast.108, s32[4096]{0:T(1024)S(1)} %broadcast_clamp_fusion), kind=kCustom, calls=%fused_computation | custom fusion | bytes 278528 | tf_op jit(solution)/shard_map/gather | solution.py:70
  439.1 1.2 copy.37
  (28 shorter events, 2.5 us)
Async XLA Ops:
  54.6 35.4 %all-to-all-start = ((bf16[32,2,128]{2,1,0:T(2,128)(2,1)}), bf16[32,2,128]{2,1,0:T(2,128)(2,1)S(1)}, u32[]{:S(2)}, u32[]{:S(2)}) async-start(bf16[32,2,128]{2,1,0:T(2,128)(2,1)} %reshape.128), calls=%async_computation | async-start | bytes 32768 | tf_op jit(solution)/shard_map/all_to_all | solution.py:36
  90.1 182.6 %all-to-all-start.1 = ((bf16[32,256,768]{2,1,0:T(8,128)(2,1)}), bf16[32,256,768]{2,1,0:T(8,128)(2,1)}, u32[]{:S(2)}, u32[]{:S(2)}) async-start(bf16[32,256,768]{2,1,0:T(8,128)(2,1)} %bitcast.107), calls=%async_computation.1 | async-start | bytes 25165824 | tf_op jit(solution)/shard_map/all_to_all | solution.py:35
  364.8 75.5 %copy-start = (f32[2,8,768]{2,1,0:T(8,128)}, f32[2,8,768]{2,1,0:T(8,128)S(1)}, u32[]{:S(2)}) copy-start(f32[2,8,768]{2,1,0:T(8,128)S(1)} %get-tuple-element.17) | copy-start | bytes 147460
  372.2 51.3 %all-to-all-start.2 = ((f32[8,32,256]{2,0,1:T(8,128)}), f32[8,32,256]{2,0,1:T(8,128)S(1)}, u32[]{:S(2)}, u32[]{:S(2)}) async-start(f32[8,32,256]{2,0,1:T(8,128)} %copy_bitcast_fusion), calls=%async_computation.2 | async-start | bytes 524288 | tf_op jit(solution)/shard_map/all_to_all | solution.py:69
where the time goes:
time: 441 us; the launch traced here: 440 us
  waiting for transfers between devices  184 us (42%)
  local copies, waits for them, and re-layouts  73.3 us (17%)
  starting transfers between devices  59.2 us (13%)
  blocking collectives  49.6 us (11%)
  matrix products  47.8 us (11%)
  other arithmetic  25.8 us (6%)
    all_to_all x1, waiting for transfers between devices, local(): lax.all_to_all(shipped, 'list', split_axis=0, concat_axis=0, tiled=True)  175 us
    psum x4, blocking collectives, group_update(): sums, totals = lax.psum((sums, totals), 'help')  49.6 us
    all_to_all x1, starting transfers between devices, local(): lax.all_to_all(going_back, 'list', split_axis=1, concat_axis=1, tiled=True)  42.3 us
    scatter x1, local copies, waits for them, and re-layouts, local(): tags = jnp.zeros((lists_all * capacity,), jnp.bfloat16).at[slot_pos].set(...  28.6 us
    scatter x1, local copies, waits for them, and re-layouts, local(): jnp.zeros((lists_all * capacity, width), jnp.bfloat16).at[slot_pos]  26 us
    dot_general x4, matrix products, group_update(): jnp.einsum('sqck,sqcd->qkd', weights_bf, arrived, preferred_element_type=...  22.1 us
    sub x3, matrix products, holder_mapping(): return jax.nn.softmax(membership_raw_preference, axis=-1)  19.2 us
    another operation x3, other arithmetic  19 us
  transfers between devices with their start and end apart: 3, of which 2 were waited for; matrix products, arithmetic and copies ran while one was open for 6% of the time, Pallas kernels for 0%

commit v1 on v0

v1 whole, which is shorter than its diff:
```python
import jax
import jax.numpy as jnp
from jax import lax
from jax.experimental import pallas as pl
from jax.experimental.pallas import tpu as pltpu
from jax.sharding import Mesh, PartitionSpec as P

K = 8
D = 768
ITERS = 3
HALF_D = D // 2
LANES = 128
CHUNK = HALF_D + LANES
OWN_LISTS = 32
SEATS = 64
TILE = 512
f32 = jnp.float32
bf16 = jnp.bfloat16


def lane_fold(block):
    total = block[:, :LANES]
    for at in range(LANES, block.shape[1], LANES):
        total = total + block[:, at : at + LANES]
    return total


def store_sums(out, acc, tot, base):
    for seat in range(SEATS):
        row, half = base + (seat // 2) * K, seat % 2
        out[seat, :, :HALF_D] = acc[row : row + K, half * HALF_D : (half + 1) * HALF_D]
        out[seat, :, HALF_D:] = tot[row : row + K, :]


def seed_kernel(members, code, mine, theirs, acc, tot):
    step = pl.program_id(0)

    @pl.when(step == 0)
    def _():
        acc[...] = jnp.zeros_like(acc)
        tot[...] = jnp.zeros_like(tot)

    groups = lax.broadcasted_iota(jnp.int32, (K, TILE), 0)
    shifted = jnp.broadcast_to(code[...], (K, TILE)) - groups
    rows = []
    for name in range(2 * OWN_LISTS):
        hot = jnp.where(shifted == name * K, 1.0, 0.0).astype(f32)
        tot[name * K : (name + 1) * K, :] += lane_fold(hot)
        rows.append(hot)
    hots = jnp.concatenate(rows, axis=0).astype(bf16)
    acc[...] += jnp.dot(hots, members[...], preferred_element_type=f32)

    @pl.when(step == pl.num_programs(0) - 1)
    def _():
        store_sums(mine, acc, tot, 0)
        store_sums(theirs, acc, tot, OWN_LISTS * K)


def seed_sums(members, code):
    rows = members.shape[0]
    part = jax.ShapeDtypeStruct((SEATS, K, CHUNK), f32)
    whole = pl.BlockSpec((SEATS, K, CHUNK), lambda i: (0, 0, 0))
    return pl.pallas_call(
        seed_kernel,
        grid=(rows // TILE,),
        in_specs=[
            pl.BlockSpec((TILE, D), lambda i: (i, 0)),
            pl.BlockSpec((1, TILE), lambda i: (0, i)),
        ],
        out_specs=[whole, whole],
        out_shape=[part, part],
        scratch_shapes=[
            pltpu.VMEM((2 * OWN_LISTS * K, D), f32),
            pltpu.VMEM((2 * OWN_LISTS * K, LANES), f32),
        ],
        name="seed_sums",
    )(members, code)


def finish_kernel(parts, out):
    total = parts[0]
    for seat in range(1, SEATS):
        total = total + parts[seat]
    count = jnp.sum(total[:, HALF_D:], axis=1, keepdims=True)
    centers = total[:, :HALF_D] / (count + 1.0)
    norm = jnp.sum(centers * centers, axis=1, keepdims=True)
    lane = lax.broadcasted_iota(jnp.int32, (K, LANES), 1)
    norms = jnp.broadcast_to(norm, (K, LANES))
    if out.dtype == bf16:
        high = norms.astype(bf16).astype(f32)
        middle = (norms - high).astype(bf16).astype(f32)
        low = norms - high - middle
        tail = jnp.where(lane == 0, high, jnp.where(lane == 1, middle, jnp.where(lane == 2, low, 0.0)))
    else:
        tail = jnp.where(lane == 0, norms, 0.0)
    block = jnp.concatenate([centers, tail], axis=1).astype(out.dtype)
    for seat in range(SEATS):
        out[seat] = block


def finish(parts, dtype):
    return pl.pallas_call(
        finish_kernel,
        out_shape=jax.ShapeDtypeStruct((SEATS, K, CHUNK), dtype),
        name="finish_" + jnp.dtype(dtype).name,
    )(parts)


def unpack_centers(packed, cen, nrm):
    for pair in range(OWN_LISTS // 2):
        for half in range(2):
            blocks = [packed[4 * pair + 2 * i + half].astype(f32) for i in range(2)]
            cen[pair * 16 : pair * 16 + 16, half * HALF_D : (half + 1) * HALF_D] = jnp.concatenate(
                [b[:, :HALF_D] for b in blocks], axis=0
            ).astype(bf16)
        for i in range(2):
            name = 2 * pair + i
            tails = packed[2 * name][:, HALF_D:].astype(f32) + packed[2 * name + 1][:, HALF_D:].astype(f32)
            nrm[name * K : (name + 1) * K, :] = jnp.broadcast_to(
                jnp.sum(tails, axis=1, keepdims=True), (K, LANES)
            )


def soft_weights(members, owner, cen, nrm):
    dots = lax.dot_general(
        cen[...], members[...], (((1,), (1,)), ((), ())), preferred_element_type=f32
    )
    names = jnp.broadcast_to(owner[...], (K, TILE))
    dot = jnp.zeros((K, TILE), f32)
    norm = jnp.zeros((K, TILE), f32)
    for name in range(OWN_LISTS):
        here = names == name
        rows = slice(name * K, (name + 1) * K)
        dot = jnp.where(here, dots[rows, :], dot)
        norm = jnp.where(here, jnp.concatenate([nrm[rows, :]] * (TILE // LANES), axis=1), norm)
    logits = (2.0 * dot - norm) / 2.0
    exps = jnp.exp(logits - jnp.max(logits, axis=0, keepdims=True))
    return exps / jnp.sum(exps, axis=0, keepdims=True), names


def round_kernel(packed, own, own_owner, other, other_owner, out, cen, nrm, acc, tot):
    step = pl.program_id(0)
    steps = pl.num_programs(0)

    @pl.when(step == 0)
    def _():
        unpack_centers(packed, cen, nrm)
        acc[...] = jnp.zeros_like(acc)
        tot[...] = jnp.zeros_like(tot)

    def work(members, owner):
        weights, names = soft_weights(members, owner, cen, nrm)
        weights = weights.astype(bf16).astype(f32)
        rows = []
        for name in range(OWN_LISTS):
            here = jnp.where(names == name, weights, 0.0)
            tot[name * K : (name + 1) * K, :] += lane_fold(here)
            rows.append(here)
        spread = jnp.concatenate(rows, axis=0).astype(bf16)
        acc[...] += jnp.dot(spread, members[...], preferred_element_type=f32)

    @pl.when(step < steps // 2)
    def _():
        work(own, own_owner)

    @pl.when(step >= steps // 2)
    def _():
        work(other, other_owner)

    @pl.when(step == steps - 1)
    def _():
        store_sums(out, acc, tot, 0)


def round_sums(packed, own, own_owner, other, other_owner):
    half = own.shape[0] // TILE
    first = lambda i: jnp.minimum(i, half - 1)
    second = lambda i: jnp.maximum(i - half, 0)
    whole = pl.BlockSpec((SEATS, K, CHUNK), lambda i: (0, 0, 0))
    return pl.pallas_call(
        round_kernel,
        grid=(2 * half,),
        in_specs=[
            whole,
            pl.BlockSpec((TILE, D), lambda i: (first(i), 0)),
            pl.BlockSpec((1, TILE), lambda i: (0, first(i))),
            pl.BlockSpec((TILE, D), lambda i: (second(i), 0)),
            pl.BlockSpec((1, TILE), lambda i: (0, second(i))),
        ],
        out_specs=whole,
        out_shape=jax.ShapeDtypeStruct((SEATS, K, CHUNK), f32),
        scratch_shapes=[
            pltpu.VMEM((OWN_LISTS * K, D), bf16),
            pltpu.VMEM((OWN_LISTS * K, LANES), f32),
            pltpu.VMEM((OWN_LISTS * K, D), f32),
            pltpu.VMEM((OWN_LISTS * K, LANES), f32),
        ],
        name="round_sums",
    )(packed, own, own_owner, other, other_owner)


def assign_kernel(packed, members, owner, out, cen, nrm):
    @pl.when(pl.program_id(0) == 0)
    def _():
        unpack_centers(packed, cen, nrm)

    out[...] = soft_weights(members, owner, cen, nrm)[0]


def assign(packed, members, owner):
    rows = members.shape[0]
    return pl.pallas_call(
        assign_kernel,
        grid=(rows // TILE,),
        in_specs=[
            pl.BlockSpec((SEATS, K, CHUNK), lambda i: (0, 0, 0)),
            pl.BlockSpec((TILE, D), lambda i: (i, 0)),
            pl.BlockSpec((1, TILE), lambda i: (0, i)),
        ],
        out_specs=pl.BlockSpec((K, TILE), lambda i: (0, i)),
        out_shape=jax.ShapeDtypeStruct((K, rows), f32),
        scratch_shapes=[
            pltpu.VMEM((OWN_LISTS * K, D), bf16),
            pltpu.VMEM((OWN_LISTS * K, LANES), f32),
        ],
        name="assign",
    )(packed, members, owner)


SWAP = [(0, 1), (1, 0)]
SEAT_AXES = ("x", "z", "y")


def local(members, owner, seed_label):
    core = lax.axis_index("c")
    owner = owner.reshape(1, -1)

    def relative(names):
        away = ((names >> 1) & 1) ^ core
        return (names >> 2) * 2 + (names & 1) + OWN_LISTS * away

    other = lax.ppermute(members, "c", SWAP)
    other_owner = relative(lax.ppermute(owner, "c", SWAP))
    own_owner = relative(owner)

    def exchange(parts):
        return lax.all_to_all(parts, SEAT_AXES, split_axis=0, concat_axis=0, tiled=True)

    mine, theirs = seed_sums(members, own_owner * K + seed_label.reshape(1, -1))
    parts = mine + lax.ppermute(theirs, "c", SWAP)
    for turn in range(ITERS):
        packed = exchange(finish(exchange(parts), bf16))
        parts = round_sums(packed, members, own_owner, other, other_owner)
    packed = exchange(finish(exchange(parts), f32))
    theirs = assign(packed, other, other_owner)
    swapped = lax.ppermute(theirs, "c", SWAP)
    mine = assign(packed, members, own_owner)
    assignments = jnp.where(own_owner < OWN_LISTS, mine, swapped)
    place = lax.axis_index(("x", "z")) * 4
    held = lax.dynamic_slice_in_dim(packed, place, 4, axis=0)[:, :, :HALF_D]
    centers = held.reshape(2, 2, K, HALF_D).transpose(0, 2, 1, 3).reshape(2, K, D)
    return assignments, centers


def solution(mesh):
    fine = Mesh(mesh.devices.reshape(4, 4, 2, 4), ("x", "z", "c", "y"))
    every = ("x", "z", "c", "y")
    return jax.shard_map(
        local,
        mesh=fine,
        in_specs=(P(every, None), P(every, None), P(every)),
        out_specs=(P(None, every), P(("x", "z", "c"), None, None)),
        check_vma=False,
    )
```

time: 441 us -> 274 us (0.62)
  waiting for transfers between devices: 184 us -> 29.5 us
  Pallas kernels: 0 us -> 92.6 us
  local copies, waits for them, and re-layouts: 73.3 us -> 3.22 us
  blocking collectives: 49.6 us -> 111 us
  matrix products: 47.8 us -> 0 us
  starting transfers between devices: 59.2 us -> 26.8 us
  other arithmetic: 25.8 us -> 7.48 us
    all_to_all x3 -> x2, waiting for transfers between devices: 184 us -> 26.7 us  [exchange(): lax.all_to_all(parts, SEAT_AXES, split_axis=0, concat_axis=0, tiled=True)]
    all_to_all x0 -> x6, blocking collectives: none -> 111 us  [exchange(): lax.all_to_all(parts, SEAT_AXES, split_axis=0, concat_axis=0, tiled=True)]
    pallas_call x0 -> x10, Pallas kernels: none -> 92.6 us  [the longest x3 57.5 us: round_sums(): pl.pallas_call(round_kernel, grid=(2 * half,), in_specs=[whole, pl.BlockS...]
    scatter x2 -> x0, local copies, waits for them, and re-layouts: 54.6 us -> none  [the longest x1 28.6 us: local(): tags = jnp.zeros((lists_all * capacity,), jnp.bfloat16).at[slot_pos].set(...]
    psum x4 -> x0, blocking collectives: 49.6 us -> none  [group_update(): sums, totals = lax.psum((sums, totals), 'help')]
    all_to_all x3 -> x2, starting transfers between devices: 59.2 us -> 16.6 us  [exchange(): lax.all_to_all(parts, SEAT_AXES, split_axis=0, concat_axis=0, tiled=True)]
    dot_general x5 -> x0, matrix products: 28.6 us -> none  [the longest x4 22.1 us: group_update(): jnp.einsum('sqck,sqcd->qkd', weights_bf, arrived, preferred_element_type=...]
    sub x3 -> x0, matrix products: 19.2 us -> none  [holder_mapping(): return jax.nn.softmax(membership_raw_preference, axis=-1)]
  transfers between devices with their start and end apart: 3 -> 6, of which waited for: 2 -> 3; matrix products, arithmetic and copies ran while one was open for 6% -> 3% of each run, Pallas kernels for 0% -> 7%
where the time goes in v1:
time: 274 us; the launch traced here: 271 us
  blocking collectives  111 us (41%)
  Pallas kernels  92.6 us (34%)
  waiting for transfers between devices  29.5 us (11%)
  starting transfers between devices  26.8 us (10%)
  other arithmetic  7.48 us (3%)
  local copies, waits for them, and re-layouts  3.22 us (1%)
    all_to_all x6, blocking collectives, exchange(): lax.all_to_all(parts, SEAT_AXES, split_axis=0, concat_axis=0, tiled=True)  111 us
    pallas_call x3, Pallas kernels, round_sums(): pl.pallas_call(round_kernel, grid=(2 * half,), in_specs=[whole, pl.BlockS...  57.5 us
    all_to_all x2, waiting for transfers between devices, exchange(): lax.all_to_all(parts, SEAT_AXES, split_axis=0, concat_axis=0, tiled=True)  26.7 us
    all_to_all x2, starting transfers between devices, exchange(): lax.all_to_all(parts, SEAT_AXES, split_axis=0, concat_axis=0, tiled=True)  16.6 us
    pallas_call x2, Pallas kernels, assign(): pl.pallas_call(assign_kernel, grid=(rows // TILE,), in_specs=[pl.BlockSpe...  16.2 us
    pallas_call x1, Pallas kernels, seed_sums(): pl.pallas_call(seed_kernel, grid=(rows // TILE,), in_specs=[pl.BlockSpec(...  9.48 us
    pallas_call x4, Pallas kernels, finish(): pl.pallas_call(finish_kernel, out_shape=jax.ShapeDtypeStruct((SEATS, K, C...  9.42 us
    ppermute x1, starting transfers between devices, local(): swapped = lax.ppermute(theirs, 'c', SWAP)  8.17 us
  transfers between devices with their start and end apart: 6, of which 3 were waited for; matrix products, arithmetic and copies ran while one was open for 3% of the time, Pallas kernels for 7%

profile of v1, /device:TPU:1, one launch (start us, length us, event | category | flops | bytes accessed | tf_op | source)
XLA Modules:
  0.0 271.3 jit_solution(15863092340681722707)
XLA Ops:
  0.6 1.5 collective-permute-start.1
  2.1 0.8 compare_reduce_fusion
  2.9 1.3 add.47
  4.3 9.5 %seed_sums.1 = (f32[64,8,512]{2,1,0:T(8,128)}, f32[64,8,512]{2,1,0:T(8,128)}) custom-call(bf16[4096,768]{1,0:T(8,128)(2,1)} %members.3, s32[1,4096]{1,0:T(1,128)} %bitcast.9), custom_call_target="tpu_custom_call" | custom-call | tf_op jit(solution)/shard_map/seed_sums/pallas_call | solution.py:63
  13.8 2.8 %collective-permute-done = f32[64,8,512]{2,1,0:T(8,128)S(1)} collective-permute-done((f32[64,8,512]{2,1,0:T(8,128)}, f32[64,8,512]{2,1,0:T(8,128)S(1)}, u32[]{:S(2)}, u32[]{:S(2)}) %collective-permute-start) | collective-permute-done | bytes 1048608 | tf_op jit(solution)/shard_map/ppermute | solution.py:250
  16.6 2.5 add.49
  19.1 11.2 %all-to-all-start = ((f32[64,8,512]{2,1,0:T(8,128)}), f32[64,8,512]{2,1,0:T(8,128)S(1)}, u32[]{:S(2)}, u32[]{:S(2)}) async-start(f32[64,8,512]{2,1,0:T(8,128)} %add.49), calls=%async_computation | async-start | bytes 2097152 | tf_op jit(solution)/shard_map/all_to_all | solution.py:247
  30.8 0.6 multiply_add_fusion.1.own_owner.owner
  31.5 16.1 %all-to-all-done.parts = f32[64,8,512]{2,1,0:T(8,128)S(1)} async-done(((f32[64,8,512]{2,1,0:T(8,128)}), f32[64,8,512]{2,1,0:T(8,128)S(1)}, u32[]{:S(2)}, u32[]{:S(2)}) %all-to-all-start) | async-done | bytes 1048608 | tf_op jit(solution)/shard_map/all_to_all | solution.py:247
  47.6 1.0 copy-done
  48.6 2.3 finish_bfloat16.3
  50.9 5.4 %all-to-all-start.1 = ((bf16[64,8,512]{2,1,0:T(8,128)(2,1)}), bf16[64,8,512]{2,1,0:T(8,128)(2,1)S(1)}, u32[]{:S(2)}, u32[]{:S(2)}) async-start(bf16[64,8,512]{2,1,0:T(8,128)(2,1)} %finish_bfloat16.3), calls=%async_computation.1 | async-start | bytes 1048576 | tf_op jit(solution)/shard_map/all_to_all | solution.py:247
  56.3 0.6 multiply_add_fusion.other_owner.owner
  56.9 10.6 %all-to-all-done.1.packed = bf16[64,8,512]{2,1,0:T(8,128)(2,1)S(1)} async-done(((bf16[64,8,512]{2,1,0:T(8,128)(2,1)}), bf16[64,8,512]{2,1,0:T(8,128)(2,1)S(1)}, u32[]{:S(2)}, u32[]{:S(2)}) %all-to-all-start.1) | async-done | bytes 524320 | tf_op jit(solution)/shard_map/all_to_all | solution.py:247
  67.5 0.8 copy-done.1
  68.3 19.1 %round_sums.3 = f32[64,8,512]{2,1,0:T(8,128)} custom-call(bf16[64,8,512]{2,1,0:T(8,128)(2,1)} %copy-done.1, bf16[4096,768]{1,0:T(8,128)(2,1)} %members.3, s32[1,4096]{1,0:T(1,128)} %multiply_add_fusion.1.own_owner.owner, bf16[4096,768]{1,0:T(8,128)(2,1)} %collective-permute-done.1.other.members, s32[1,4096]{1,0:T(1,128)} %multiply_add_fusion.other_owner.owner), custom_call_target="tpu_custom_call" | custom-call | tf_op jit(solution)/shard_map/round_sums/pallas_call | solution.py:180
  87.4 21.5 %all_to_all.40.parts = f32[64,8,512]{2,1,0:T(8,128)} all-to-all(f32[64,8,512]{2,1,0:T(8,128)} %round_sums.3), channel_id=1, replica_groups=mesh['x'=4,'z'=4,'c'=2,'y'=4] {'x','z','y'}, dimensions={0} | all-to-all | bytes 2097152 | tf_op jit(solution)/shard_map/all_to_all | solution.py:247
  109.0 2.3 finish_bfloat16.4
  111.3 16.1 %all_to_all.41.packed = bf16[64,8,512]{2,1,0:T(8,128)(2,1)} all-to-all(bf16[64,8,512]{2,1,0:T(8,128)(2,1)} %finish_bfloat16.4), channel_id=1, replica_groups=mesh['x'=4,'z'=4,'c'=2,'y'=4] {'x','z','y'}, dimensions={0} | all-to-all | bytes 1048576 | tf_op jit(solution)/shard_map/all_to_all | solution.py:247
  127.4 19.1 %round_sums.4 = f32[64,8,512]{2,1,0:T(8,128)} custom-call(bf16[64,8,512]{2,1,0:T(8,128)(2,1)} %all_to_all.41.packed, bf16[4096,768]{1,0:T(8,128)(2,1)} %members.3, s32[1,4096]{1,0:T(1,128)} %multiply_add_fusion.1.own_owner.owner, bf16[4096,768]{1,0:T(8,128)(2,1)} %collective-permute-done.1.other.members, s32[1,4096]{1,0:T(1,128)} %multiply_add_fusion.other_owner.owner), custom_call_target="tpu_custom_call" | custom-call | tf_op jit(solution)/shard_map/round_sums/pallas_call | solution.py:180
  146.5 19.4 %all_to_all.42.parts = f32[64,8,512]{2,1,0:T(8,128)} all-to-all(f32[64,8,512]{2,1,0:T(8,128)} %round_sums.4), channel_id=1, replica_groups=mesh['x'=4,'z'=4,'c'=2,'y'=4] {'x','z','y'}, dimensions={0} | all-to-all | bytes 2097152 | tf_op jit(solution)/shard_map/all_to_all | solution.py:247
  166.0 2.3 finish_bfloat16.5
  168.3 16.0 %all_to_all.43.packed = bf16[64,8,512]{2,1,0:T(8,128)(2,1)} all-to-all(bf16[64,8,512]{2,1,0:T(8,128)(2,1)} %finish_bfloat16.5), channel_id=1, replica_groups=mesh['x'=4,'z'=4,'c'=2,'y'=4] {'x','z','y'}, dimensions={0} | all-to-all | bytes 1048576 | tf_op jit(solution)/shard_map/all_to_all | solution.py:247
  184.2 19.2 %round_sums.5 = f32[64,8,512]{2,1,0:T(8,128)} custom-call(bf16[64,8,512]{2,1,0:T(8,128)(2,1)} %all_to_all.43.packed, bf16[4096,768]{1,0:T(8,128)(2,1)} %members.3, s32[1,4096]{1,0:T(1,128)} %multiply_add_fusion.1.own_owner.owner, bf16[4096,768]{1,0:T(8,128)(2,1)} %collective-permute-done.1.other.members, s32[1,4096]{1,0:T(1,128)} %multiply_add_fusion.other_owner.owner), custom_call_target="tpu_custom_call" | custom-call | tf_op jit(solution)/shard_map/round_sums/pallas_call | solution.py:180
  203.4 19.2 %all_to_all.44.parts = f32[64,8,512]{2,1,0:T(8,128)} all-to-all(f32[64,8,512]{2,1,0:T(8,128)} %round_sums.5), channel_id=1, replica_groups=mesh['x'=4,'z'=4,'c'=2,'y'=4] {'x','z','y'}, dimensions={0} | all-to-all | bytes 2097152 | tf_op jit(solution)/shard_map/all_to_all | solution.py:247
  222.6 2.6 finish_float32.1
  225.1 18.8 %all_to_all.45.packed = f32[64,8,512]{2,1,0:T(8,128)} all-to-all(f32[64,8,512]{2,1,0:T(8,128)} %finish_float32.1), channel_id=1, replica_groups=mesh['x'=4,'z'=4,'c'=2,'y'=4] {'x','z','y'}, dimensions={0} | all-to-all | bytes 2097152 | tf_op jit(solution)/shard_map/all_to_all | solution.py:247
  243.9 8.1 %assign.3 = f32[8,4096]{1,0:T(8,128)} custom-call(f32[64,8,512]{2,1,0:T(8,128)} %all_to_all.45.packed, bf16[4096,768]{1,0:T(8,128)(2,1)} %collective-permute-done.1.other.members, s32[1,4096]{1,0:T(1,128)} %multiply_add_fusion.other_owner.owner), custom_call_target="tpu_custom_call" | custom-call | tf_op jit(solution)/shard_map/assign/pallas_call | solution.py:212
  252.0 8.2 %collective-permute-start.3 = (f32[8,4096]{1,0:T(8,128)}, f32[8,4096]{1,0:T(8,128)S(1)}, u32[]{:S(2)}, u32[]{:S(2)}) collective-permute-start(f32[8,4096]{1,0:T(8,128)} %assign.3), channel_id=1, source_target_pairs={{0,4},{4,0},{1,5},{5,1},{2,6},{6,2},{3,7},{7,3},{8,12},{12,8},{9,1... | collective-permute-start | bytes 393224 | tf_op jit(solution)/shard_map/ppermute | solution.py:256
  260.2 8.1 %assign.2 = f32[8,4096]{1,0:T(8,128)} custom-call(f32[64,8,512]{2,1,0:T(8,128)} %all_to_all.45.packed, bf16[4096,768]{1,0:T(8,128)(2,1)} %members.3, s32[1,4096]{1,0:T(1,128)} %multiply_add_fusion.1.own_owner.owner), custom_call_target="tpu_custom_call" | custom-call | tf_op jit(solution)/shard_map/assign/pallas_call | solution.py:212
  268.3 1.4 constant_dynamic-slice_fusion
  269.7 1.6 broadcast_select_fusion
  (10 shorter events, 0.6 us)
Async XLA Ops:
  0.6 29.7 %copy-start.2 = (s32[4096,1]{0,1:T(1,128)S(1)}, s32[4096,1]{0,1:T(1,128)}, u32[]{:S(2)}) copy-start(s32[4096,1]{0,1:T(1,128)} %param.4) | copy-start | bytes 49156
  0.6 66.8 %collective-permute-start.1 = (bf16[4096,768]{1,0:T(8,128)(2,1)}, bf16[4096,768]{1,0:T(8,128)(2,1)}, u32[]{:S(2)}, u32[]{:S(2)}) collective-permute-start(bf16[4096,768]{1,0:T(8,128)(2,1)} %members.3), channel_id=1, source_target_pairs={{0,4},{4,0},{1,5},{5,1},{2,6},{6,2},{3,7},{7,3},{8,12},{12,8},{9,1... | collective-permute-start | bytes 18874376 | tf_op jit(solution)/shard_map/ppermute | solution.py:242
  13.7 2.9 %collective-permute-start = (f32[64,8,512]{2,1,0:T(8,128)}, f32[64,8,512]{2,1,0:T(8,128)S(1)}, u32[]{:S(2)}, u32[]{:S(2)}) collective-permute-start(f32[64,8,512]{2,1,0:T(8,128)} %get-tuple-element.5), channel_id=1, source_target_pairs={{0,4},{4,0},{1,5},{5,1},{2,6},{6,2},{3,7},{7,3},{8,12},{12,8},{9,1... | collective-permute-start | bytes 3145736 | tf_op jit(solution)/shard_map/ppermute | solution.py:250
  19.1 28.5 %all-to-all-start = ((f32[64,8,512]{2,1,0:T(8,128)}), f32[64,8,512]{2,1,0:T(8,128)S(1)}, u32[]{:S(2)}, u32[]{:S(2)}) async-start(f32[64,8,512]{2,1,0:T(8,128)} %add.49), calls=%async_computation | async-start | bytes 2097152 | tf_op jit(solution)/shard_map/all_to_all | solution.py:247
  30.3 25.9 %collective-permute-start.2 = (s32[1,4096]{1,0:T(1,128)S(1)}, s32[1,4096]{1,0:T(1,128)S(1)}, u32[]{:S(2)}, u32[]{:S(2)}) collective-permute-start(s32[1,4096]{1,0:T(1,128)S(1)} %bitcast.11), channel_id=1, source_target_pairs={{0,4},{4,0},{1,5},{5,1},{2,6},{6,2},{3,7},{7,3},{8,12},{12,8},{9,1... | collective-permute-start | bytes 49160 | tf_op jit(solution)/shard_map/ppermute | solution.py:243
  47.6 1.0 copy-start
  50.9 16.6 %all-to-all-start.1 = ((bf16[64,8,512]{2,1,0:T(8,128)(2,1)}), bf16[64,8,512]{2,1,0:T(8,128)(2,1)S(1)}, u32[]{:S(2)}, u32[]{:S(2)}) async-start(bf16[64,8,512]{2,1,0:T(8,128)(2,1)} %finish_bfloat16.3), calls=%async_computation.1 | async-start | bytes 1048576 | tf_op jit(solution)/shard_map/all_to_all | solution.py:247
  67.5 0.8 copy-start.1
  252.0 17.7 %collective-permute-start.3 = (f32[8,4096]{1,0:T(8,128)}, f32[8,4096]{1,0:T(8,128)S(1)}, u32[]{:S(2)}, u32[]{:S(2)}) collective-permute-start(f32[8,4096]{1,0:T(8,128)} %assign.3), channel_id=1, source_target_pairs={{0,4},{4,0},{1,5},{5,1},{2,6},{6,2},{3,7},{7,3},{8,12},{12,8},{9,1... | collective-permute-start | bytes 393224 | tf_op jit(solution)/shard_map/ppermute | solution.py:256

commit v2 on v1

v2 whole, which is shorter than its diff:
```python
import jax
import jax.numpy as jnp
from jax import lax
from jax.experimental import pallas as pl
from jax.experimental.pallas import tpu as pltpu
from jax.sharding import Mesh, PartitionSpec as P

K = 8
D = 768
ITERS = 3
HALF_D = D // 2
LANES = 128
CHUNK = HALF_D + LANES
OWN_LISTS = 32
SEATS = 64
TILE = 512
UNROLL = 4
COPIES = 4
SEED_COPIES = 4
f32 = jnp.float32
bf16 = jnp.bfloat16


def lane_fold(block):
    total = block[:, :LANES]
    for at in range(LANES, block.shape[1], LANES):
        total = total + block[:, at : at + LANES]
    return total


def store_sums(out, acc, tot, base):
    for seat in range(SEATS):
        row, half = base + (seat // 2) * K, seat % 2
        out[seat, :, :HALF_D] = acc[row : row + K, half * HALF_D : (half + 1) * HALF_D]
        out[seat, :, HALF_D:] = tot[row : row + K, :]


def relative(names, core):
    away = ((names >> 1) & 1) ^ core
    return (names >> 2) * 2 + (names & 1) + OWN_LISTS * away


def start_copies(sources, buf, sems, copies):
    rows = sources[0].shape[0] // copies
    for number in range(len(sources) * copies):
        source = sources[number // copies].at[pl.ds(number % copies * rows, rows), :]
        pltpu.make_async_copy(source, buf.at[pl.ds(number * rows, rows), :], sems.at[number]).start()


def wait_copy(source, buf, sems, copies, number):
    rows = source.shape[0] // copies
    pltpu.make_async_copy(
        source.at[pl.ds(0, rows), :], buf.at[pl.ds(number * rows, rows), :], sems.at[number]
    ).wait()


def at_tile(tile):
    return pl.ds(pl.multiple_of(tile * TILE, TILE), TILE)


def seed_kernel(core, members, owner, seeds, mine, theirs, acc, tot, code, buf, sems):
    start_copies([members], buf, sems, SEED_COPIES)
    code[...] = relative(owner[...], core[0]) * K + seeds[...]
    acc[...] = jnp.zeros_like(acc)
    tot[...] = jnp.zeros_like(tot)
    groups = lax.broadcasted_iota(jnp.int32, (K, TILE), 0)
    unroll = buf.shape[0] // TILE // SEED_COPIES

    def work(turn, carry):
        wait_copy(members, buf, sems, SEED_COPIES, turn)
        for part in range(unroll):
            spot = at_tile(turn * unroll + part)
            shifted = jnp.broadcast_to(code[:, spot], (K, TILE)) - groups
            rows = []
            for name in range(2 * OWN_LISTS):
                hot = jnp.where(shifted == name * K, 1.0, 0.0).astype(f32)
                tot[name * K : (name + 1) * K, :] += lane_fold(hot)
                rows.append(hot)
            hots = jnp.concatenate(rows, axis=0).astype(bf16)
            acc[...] += jnp.dot(hots, buf[spot, :], preferred_element_type=f32)
        return carry

    lax.fori_loop(0, SEED_COPIES, work, 0)
    store_sums(mine, acc, tot, 0)
    store_sums(theirs, acc, tot, OWN_LISTS * K)


IN_VMEM = pl.BlockSpec(memory_space=pltpu.VMEM)
IN_SMEM = pl.BlockSpec(memory_space=pltpu.SMEM)
IN_PLACE = pl.BlockSpec(memory_space=pl.ANY)


def seed_sums(core, members, owner, seeds):
    part = jax.ShapeDtypeStruct((SEATS, K, CHUNK), f32)
    rows = members.shape[0]
    return pl.pallas_call(
        seed_kernel,
        in_specs=[IN_SMEM, IN_PLACE, IN_VMEM, IN_VMEM],
        out_specs=[IN_VMEM, IN_VMEM],
        out_shape=[part, part],
        scratch_shapes=[
            pltpu.VMEM((2 * OWN_LISTS * K, D), f32),
            pltpu.VMEM((2 * OWN_LISTS * K, LANES), f32),
            pltpu.VMEM((1, rows), jnp.int32),
            pltpu.VMEM((rows, D), bf16),
            pltpu.SemaphoreType.DMA((SEED_COPIES,)),
        ],
        name="seed_sums",
    )(core, members, owner, seeds)


def finish_kernel(parts, out):
    total = parts[0]
    for seat in range(1, SEATS):
        total = total + parts[seat]
    count = jnp.sum(total[:, HALF_D:], axis=1, keepdims=True)
    centers = total[:, :HALF_D] / (count + 1.0)
    norm = jnp.sum(centers * centers, axis=1, keepdims=True)
    lane = lax.broadcasted_iota(jnp.int32, (K, LANES), 1)
    norms = jnp.broadcast_to(norm, (K, LANES))
    if out.dtype == bf16:
        high = norms.astype(bf16).astype(f32)
        middle = (norms - high).astype(bf16).astype(f32)
        low = norms - high - middle
        tail = jnp.where(lane == 0, high, jnp.where(lane == 1, middle, jnp.where(lane == 2, low, 0.0)))
    else:
        tail = jnp.where(lane == 0, norms, 0.0)
    block = jnp.concatenate([centers, tail], axis=1).astype(out.dtype)
    for seat in range(SEATS):
        out[seat] = block


def finish(parts, dtype):
    return pl.pallas_call(
        finish_kernel,
        in_specs=[IN_VMEM],
        out_specs=IN_VMEM,
        out_shape=jax.ShapeDtypeStruct((SEATS, K, CHUNK), dtype),
        name="finish_" + jnp.dtype(dtype).name,
    )(parts)


def unpack_centers(packed, cen, nrm):
    for pair in range(OWN_LISTS // 2):
        for half in range(2):
            blocks = [packed[4 * pair + 2 * i + half].astype(f32) for i in range(2)]
            cen[pair * 16 : pair * 16 + 16, half * HALF_D : (half + 1) * HALF_D] = jnp.concatenate(
                [b[:, :HALF_D] for b in blocks], axis=0
            ).astype(bf16)
        for i in range(2):
            name = 2 * pair + i
            tails = packed[2 * name][:, HALF_D:].astype(f32) + packed[2 * name + 1][:, HALF_D:].astype(f32)
            nrm[name * K : (name + 1) * K, :] = jnp.broadcast_to(
                jnp.sum(tails, axis=1, keepdims=True), (K, LANES)
            )


def dots_of(tile, cen, buf):
    return lax.dot_general(
        cen[...], buf[at_tile(tile), :], (((1,), (1,)), ((), ())), preferred_element_type=f32
    )


def soft_weights(dots, slot, nrm, names):
    dot = jnp.zeros((K, TILE), f32)
    norm = jnp.zeros((K, TILE), f32)
    for name in range(OWN_LISTS):
        here = names == name
        rows = slice(name * K, (name + 1) * K)
        dot = jnp.where(here, dots[slot, rows, :], dot)
        norm = jnp.where(here, jnp.concatenate([nrm[rows, :]] * (TILE // LANES), axis=1), norm)
    logits = (2.0 * dot - norm) / 2.0
    exps = jnp.exp(logits - jnp.max(logits, axis=0, keepdims=True))
    return exps / jnp.sum(exps, axis=0, keepdims=True)


def both_owners(core, own_owner, other_owner, owners):
    rows = own_owner.shape[1]
    owners[:, :rows] = relative(own_owner[...], core)
    owners[:, rows:] = relative(other_owner[...], core)


def both_waits(own, buf, sems, turn):
    for number in range(2):
        wait_copy(own, buf, sems, COPIES, turn * 2 + number)


def round_kernel(
    core, packed, own, own_owner, other, other_owner, out, cen, nrm, acc, tot, owners, dots, buf, sems
):
    start_copies([own, other], buf, sems, COPIES)
    unpack_centers(packed, cen, nrm)
    both_owners(core[0], own_owner, other_owner, owners)
    acc[...] = jnp.zeros_like(acc)
    tot[...] = jnp.zeros_like(tot)

    def work(turn, carry):
        both_waits(own, buf, sems, turn)
        for part in range(UNROLL):
            dots[part] = dots_of(turn * UNROLL + part, cen, buf)
        for part in range(UNROLL):
            spot = at_tile(turn * UNROLL + part)
            names = jnp.broadcast_to(owners[:, spot], (K, TILE))
            weights = soft_weights(dots, part, nrm, names).astype(bf16).astype(f32)
            rows = []
            for name in range(OWN_LISTS):
                here = jnp.where(names == name, weights, 0.0)
                tot[name * K : (name + 1) * K, :] += lane_fold(here)
                rows.append(here)
            spread = jnp.concatenate(rows, axis=0).astype(bf16)
            acc[...] += jnp.dot(spread, buf[spot, :], preferred_element_type=f32)
        return carry

    lax.fori_loop(0, COPIES, work, 0)
    store_sums(out, acc, tot, 0)


def round_sums(core, packed, own, own_owner, other, other_owner):
    rows = 2 * own.shape[0]
    return pl.pallas_call(
        round_kernel,
        in_specs=[IN_SMEM, IN_VMEM, IN_PLACE, IN_VMEM, IN_PLACE, IN_VMEM],
        out_specs=IN_VMEM,
        out_shape=jax.ShapeDtypeStruct((SEATS, K, CHUNK), f32),
        scratch_shapes=[
            pltpu.VMEM((OWN_LISTS * K, D), bf16),
            pltpu.VMEM((OWN_LISTS * K, LANES), f32),
            pltpu.VMEM((OWN_LISTS * K, D), f32),
            pltpu.VMEM((OWN_LISTS * K, LANES), f32),
            pltpu.VMEM((1, rows), jnp.int32),
            pltpu.VMEM((UNROLL, OWN_LISTS * K, TILE), f32),
            pltpu.VMEM((rows, D), bf16),
            pltpu.SemaphoreType.DMA((2 * COPIES,)),
        ],
        name="round_sums",
    )(core, packed, own, own_owner, other, other_owner)


def assign_kernel(
    core, packed, own, own_owner, other, other_owner, out, held, cen, nrm, owners, dots, buf, sems
):
    start_copies([own, other], buf, sems, COPIES)
    unpack_centers(packed, cen, nrm)
    both_owners(core[0], own_owner, other_owner, owners)
    for name in range(2):
        for half in range(2):
            block = packed[core[1] + 2 * name + half]
            held[name, :, half * HALF_D : (half + 1) * HALF_D] = block[:, :HALF_D]

    def work(turn, carry):
        both_waits(own, buf, sems, turn)
        for part in range(UNROLL):
            dots[part] = dots_of(turn * UNROLL + part, cen, buf)
        for part in range(UNROLL):
            spot = at_tile(turn * UNROLL + part)
            names = jnp.broadcast_to(owners[:, spot], (K, TILE))
            out[:, spot] = jnp.where(names < OWN_LISTS, soft_weights(dots, part, nrm, names), 0.0)
        return carry

    lax.fori_loop(0, COPIES, work, 0)


def assign(core, packed, own, own_owner, other, other_owner):
    rows = 2 * own.shape[0]
    return pl.pallas_call(
        assign_kernel,
        in_specs=[IN_SMEM, IN_VMEM, IN_PLACE, IN_VMEM, IN_PLACE, IN_VMEM],
        out_specs=[IN_VMEM, IN_VMEM],
        out_shape=[jax.ShapeDtypeStruct((K, rows), f32), jax.ShapeDtypeStruct((2, K, D), f32)],
        scratch_shapes=[
            pltpu.VMEM((OWN_LISTS * K, D), bf16),
            pltpu.VMEM((OWN_LISTS * K, LANES), f32),
            pltpu.VMEM((1, rows), jnp.int32),
            pltpu.VMEM((UNROLL, OWN_LISTS * K, TILE), f32),
            pltpu.VMEM((rows, D), bf16),
            pltpu.SemaphoreType.DMA((2 * COPIES,)),
        ],
        name="assign",
    )(core, packed, own, own_owner, other, other_owner)


SWAP = [(0, 1), (1, 0)]
SEAT_AXES = ("x", "z", "y")


def local(members, owner, seed_label):
    place = jnp.stack([lax.axis_index("c"), lax.axis_index(("x", "z")) * 4]).astype(jnp.int32)
    owner = owner.reshape(1, -1)
    other = lax.ppermute(members, "c", SWAP)
    other_owner = lax.ppermute(owner, "c", SWAP)
    both = (members, owner, other, other_owner)

    def exchange(parts):
        return lax.all_to_all(parts, SEAT_AXES, split_axis=0, concat_axis=0, tiled=True)

    mine, theirs = seed_sums(place, members, owner, seed_label.reshape(1, -1))
    parts = mine + lax.ppermute(theirs, "c", SWAP)
    for turn in range(ITERS):
        packed = exchange(finish(exchange(parts), bf16))
        parts = round_sums(place, packed, *both)
    packed = exchange(finish(exchange(parts), f32))
    weights, centers = assign(place, packed, *both)
    rows = members.shape[0]
    swapped = lax.ppermute(weights[:, rows:], "c", SWAP)
    return weights[:, :rows] + swapped, centers


def solution(mesh):
    fine = Mesh(mesh.devices.reshape(4, 4, 2, 4), ("x", "z", "c", "y"))
    every = ("x", "z", "c", "y")
    return jax.shard_map(
        local,
        mesh=fine,
        in_specs=(P(every, None), P(every, None), P(every)),
        out_specs=(P(None, every), P(("x", "z", "c"), None, None)),
        check_vma=False,
    )
```

time: 274 us -> 238 us (0.87)
  Pallas kernels: 92.6 us -> 60.9 us
  blocking collectives: 111 us -> 140 us
  waiting for transfers between devices: 29.5 us -> 13.3 us
  starting transfers between devices: 26.8 us -> 17.2 us
  other arithmetic: 7.48 us -> 3.59 us
    pallas_call x10 -> x9, Pallas kernels: 92.6 us -> 60.9 us  [the longest x3 35.7 us: round_sums(): pl.pallas_call(round_kernel, in_specs=[IN_SMEM, IN_VMEM, IN_PLACE, IN_VME...]
    all_to_all x6 -> x7, blocking collectives: 111 us -> 140 us  [exchange(): lax.all_to_all(parts, SEAT_AXES, split_axis=0, concat_axis=0, tiled=True)]
    all_to_all x2 -> x1, waiting for transfers between devices: 26.7 us -> 8.32 us  [exchange(): lax.all_to_all(parts, SEAT_AXES, split_axis=0, concat_axis=0, tiled=True)]
    all_to_all x2 -> x1, starting transfers between devices: 16.6 us -> 5.6 us  [exchange(): lax.all_to_all(parts, SEAT_AXES, split_axis=0, concat_axis=0, tiled=True)]
  transfers between devices with their start and end apart: 6 -> 5, of which waited for: 3 -> 4; matrix products, arithmetic and copies ran while one was open for 3% -> 1% of each run, Pallas kernels for 7% -> 4%
where the time goes in v2:
time: 238 us; the launch traced here: 237 us
  blocking collectives  140 us (59%)
  Pallas kernels  60.9 us (26%)
  starting transfers between devices  17.2 us (7%)
  waiting for transfers between devices  13.3 us (6%)
  other arithmetic  3.59 us (2%)
    all_to_all x7, blocking collectives, exchange(): lax.all_to_all(parts, SEAT_AXES, split_axis=0, concat_axis=0, tiled=True)  140 us
    pallas_call x3, Pallas kernels, round_sums(): pl.pallas_call(round_kernel, in_specs=[IN_SMEM, IN_VMEM, IN_PLACE, IN_VME...  35.7 us
    pallas_call x4, Pallas kernels, finish(): pl.pallas_call(finish_kernel, in_specs=[IN_VMEM], out_specs=IN_VMEM, out_...  9.42 us
    all_to_all x1, waiting for transfers between devices, exchange(): lax.all_to_all(parts, SEAT_AXES, split_axis=0, concat_axis=0, tiled=True)  8.32 us
    ppermute x1, starting transfers between devices, local(): swapped = lax.ppermute(weights[:, rows:], 'c', SWAP)  8.26 us
    pallas_call x1, Pallas kernels, assign(): pl.pallas_call(assign_kernel, in_specs=[IN_SMEM, IN_VMEM, IN_PLACE, IN_VM...  8.08 us
    pallas_call x1, Pallas kernels, seed_sums(): pl.pallas_call(seed_kernel, in_specs=[IN_SMEM, IN_PLACE, IN_VMEM, IN_VMEM...  7.67 us
    all_to_all x1, starting transfers between devices, exchange(): lax.all_to_all(parts, SEAT_AXES, split_axis=0, concat_axis=0, tiled=True)  5.6 us
  transfers between devices with their start and end apart: 5, of which 4 were waited for; matrix products, arithmetic and copies ran while one was open for 1% of the time, Pallas kernels for 4%

profile of v2, /device:TPU:1, one launch (start us, length us, event | category | flops | bytes accessed | tf_op | source)
XLA Modules:
  0.0 237.0 jit_solution(18021949033162481000)
XLA Ops:
  0.6 1.5 collective-permute-start.1
  2.1 0.6 pad_add_fusion.core
  2.7 7.7 %seed_sums.1 = (f32[64,8,512]{2,1,0:T(8,128)}, f32[64,8,512]{2,1,0:T(8,128)}) custom-call(s32[2]{0:T(128)} %pad_add_fusion.core, bf16[4096,768]{1,0:T(8,128)(2,1)} %own.7, s32[1,4096]{1,0:T(1,128)} %bitcast.4, s32[1,4096]{1,0:T(1,128)} %bitcast.10), custom_call_target="tpu_custom_call" | custom-call | tf_op jit(solution)/shard_map/seed_sums/pallas_call | solution.py:96
  10.3 0.1 collective-permute-start
  10.5 3.1 %collective-permute-done = f32[64,8,512]{2,1,0:T(8,128)S(1)} collective-permute-done((f32[64,8,512]{2,1,0:T(8,128)}, f32[64,8,512]{2,1,0:T(8,128)S(1)}, u32[]{:S(2)}, u32[]{:S(2)}) %collective-permute-start) | collective-permute-done | bytes 1048608 | tf_op jit(solution)/shard_map/ppermute | solution.py:297
  13.6 1.4 add.10
  15.0 28.2 %all_to_all.40.parts = f32[64,8,512]{2,1,0:T(8,128)} all-to-all(f32[64,8,512]{2,1,0:T(8,128)S(1)} %add.10), channel_id=1, replica_groups=mesh['x'=4,'z'=4,'c'=2,'y'=4] {'x','z','y'}, dimensions={0} | all-to-all | bytes 2097152 | tf_op jit(solution)/shard_map/all_to_all | solution.py:294
  43.2 2.3 finish_bfloat16.3
  45.5 5.6 %all-to-all-start.1 = ((bf16[64,8,512]{2,1,0:T(8,128)(2,1)}), bf16[64,8,512]{2,1,0:T(8,128)(2,1)S(1)}, u32[]{:S(2)}, u32[]{:S(2)}) async-start(bf16[64,8,512]{2,1,0:T(8,128)(2,1)} %finish_bfloat16.3), calls=%async_computation.1 | async-start | bytes 1048576 | tf_op jit(solution)/shard_map/all_to_all | solution.py:294
  51.1 0.0 copy-done.1
  51.1 1.8 collective-permute-start.2
  52.9 0.8 collective-permute-done.2.other_owner
  53.7 8.3 %all-to-all-done.1.packed = bf16[64,8,512]{2,1,0:T(8,128)(2,1)S(1)} async-done(((bf16[64,8,512]{2,1,0:T(8,128)(2,1)}), bf16[64,8,512]{2,1,0:T(8,128)(2,1)S(1)}, u32[]{:S(2)}, u32[]{:S(2)}) %all-to-all-start.1) | async-done | bytes 524320 | tf_op jit(solution)/shard_map/all_to_all | solution.py:294
  62.0 0.0 collective-permute-done.1.other
  62.0 0.8 copy-done
  62.8 11.9 %round_sums.3 = f32[64,8,512]{2,1,0:T(8,128)} custom-call(s32[2]{0:T(128)} %pad_add_fusion.core, bf16[64,8,512]{2,1,0:T(8,128)(2,1)} %copy-done, bf16[4096,768]{1,0:T(8,128)(2,1)} %own.7, s32[1,4096]{1,0:T(1,128)} %bitcast.5, bf16[4096,768]{1,0:T(8,128)(2,1)} %collective-permute-done.1.other, s32[1,4096]{1,0:T(1,128)} %copy-done.2), custom_call_target="tpu_custom_call" | custom-call | tf_op jit(solution)/shard_map/round_sums/pallas_call | solution.py:220
  74.7 21.8 %all_to_all.41.parts = f32[64,8,512]{2,1,0:T(8,128)} all-to-all(f32[64,8,512]{2,1,0:T(8,128)} %round_sums.3), channel_id=1, replica_groups=mesh['x'=4,'z'=4,'c'=2,'y'=4] {'x','z','y'}, dimensions={0} | all-to-all | bytes 2097152 | tf_op jit(solution)/shard_map/all_to_all | solution.py:294
  96.6 2.3 finish_bfloat16.4
  98.9 16.1 %all_to_all.42.packed = bf16[64,8,512]{2,1,0:T(8,128)(2,1)} all-to-all(bf16[64,8,512]{2,1,0:T(8,128)(2,1)} %finish_bfloat16.4), channel_id=1, replica_groups=mesh['x'=4,'z'=4,'c'=2,'y'=4] {'x','z','y'}, dimensions={0} | all-to-all | bytes 1048576 | tf_op jit(solution)/shard_map/all_to_all | solution.py:294
  115.0 11.9 %round_sums.4 = f32[64,8,512]{2,1,0:T(8,128)} custom-call(s32[2]{0:T(128)} %pad_add_fusion.core, bf16[64,8,512]{2,1,0:T(8,128)(2,1)} %all_to_all.42.packed, bf16[4096,768]{1,0:T(8,128)(2,1)} %own.7, s32[1,4096]{1,0:T(1,128)} %bitcast.6, bf16[4096,768]{1,0:T(8,128)(2,1)} %collective-permute-done.1.other, s32[1,4096]{1,0:T(1,128)} %copy-done.2), custom_call_target="tpu_custom_call" | custom-call | tf_op jit(solution)/shard_map/round_sums/pallas_call | solution.py:220
  126.9 19.4 %all_to_all.43.parts = f32[64,8,512]{2,1,0:T(8,128)} all-to-all(f32[64,8,512]{2,1,0:T(8,128)} %round_sums.4), channel_id=1, replica_groups=mesh['x'=4,'z'=4,'c'=2,'y'=4] {'x','z','y'}, dimensions={0} | all-to-all | bytes 2097152 | tf_op jit(solution)/shard_map/all_to_all | solution.py:294
  146.3 2.3 finish_bfloat16.5
  148.6 16.1 %all_to_all.44.packed = bf16[64,8,512]{2,1,0:T(8,128)(2,1)} all-to-all(bf16[64,8,512]{2,1,0:T(8,128)(2,1)} %finish_bfloat16.5), channel_id=1, replica_groups=mesh['x'=4,'z'=4,'c'=2,'y'=4] {'x','z','y'}, dimensions={0} | all-to-all | bytes 1048576 | tf_op jit(solution)/shard_map/all_to_all | solution.py:294
  164.7 11.9 %round_sums.5 = f32[64,8,512]{2,1,0:T(8,128)} custom-call(s32[2]{0:T(128)} %pad_add_fusion.core, bf16[64,8,512]{2,1,0:T(8,128)(2,1)} %all_to_all.44.packed, bf16[4096,768]{1,0:T(8,128)(2,1)} %own.7, s32[1,4096]{1,0:T(1,128)} %bitcast.7, bf16[4096,768]{1,0:T(8,128)(2,1)} %collective-permute-done.1.other, s32[1,4096]{1,0:T(1,128)} %copy-done.2), custom_call_target="tpu_custom_call" | custom-call | tf_op jit(solution)/shard_map/round_sums/pallas_call | solution.py:220
  176.6 19.2 %all_to_all.45.parts = f32[64,8,512]{2,1,0:T(8,128)} all-to-all(f32[64,8,512]{2,1,0:T(8,128)} %round_sums.5), channel_id=1, replica_groups=mesh['x'=4,'z'=4,'c'=2,'y'=4] {'x','z','y'}, dimensions={0} | all-to-all | bytes 2097152 | tf_op jit(solution)/shard_map/all_to_all | solution.py:294
  195.9 2.6 %finish_float32.1 = f32[64,8,512]{2,1,0:T(8,128)} custom-call(f32[64,8,512]{2,1,0:T(8,128)} %all_to_all.45.parts), custom_call_target="tpu_custom_call" | custom-call | tf_op jit(solution)/shard_map/finish_float32/pallas_call | solution.py:134
  198.4 18.8 %all_to_all.46.packed = f32[64,8,512]{2,1,0:T(8,128)} all-to-all(f32[64,8,512]{2,1,0:T(8,128)} %finish_float32.1), channel_id=1, replica_groups=mesh['x'=4,'z'=4,'c'=2,'y'=4] {'x','z','y'}, dimensions={0} | all-to-all | bytes 2097152 | tf_op jit(solution)/shard_map/all_to_all | solution.py:294
  217.2 8.1 %assign.1 = (f32[8,8192]{1,0:T(8,128)}, f32[2,8,768]{2,1,0:T(8,128)}) custom-call(s32[2]{0:T(128)} %pad_add_fusion.core, f32[64,8,512]{2,1,0:T(8,128)} %all_to_all.46.packed, bf16[4096,768]{1,0:T(8,128)(2,1)} %own.7, s32[1,4096]{1,0:T(1,128)} %bitcast.8, bf16[4096,768]{1,0:T(8,128)(2,1)} %collective-permute-done.1.other, s32[1,4096]{1,0:T(1,128)} %copy-done.2), custom_call_target="tpu_custom_call" | custom-call | tf_op jit(solution)/shard_map/assign/pallas_call | solution.py:265
  225.3 0.9 slice.7
  226.2 8.3 %collective-permute-start.3 = (f32[8,4096]{1,0:T(8,128)S(1)}, f32[8,4096]{1,0:T(8,128)S(1)}, u32[]{:S(2)}, u32[]{:S(2)}) collective-permute-start(f32[8,4096]{1,0:T(8,128)S(1)} %slice.7), channel_id=1, source_target_pairs={{0,4},{4,0},{1,5},{5,1},{2,6},{6,2},{3,7},{7,3},{8,12},{12,8},{9,1... | collective-permute-start | bytes 393224 | tf_op jit(solution)/shard_map/ppermute | solution.py:304
  234.5 1.0 collective-permute-done.3
  235.4 1.6 slice_add_fusion
  (4 shorter events, 0.0 us)
Async XLA Ops:
  0.6 61.4 %collective-permute-start.1 = (bf16[4096,768]{1,0:T(8,128)(2,1)}, bf16[4096,768]{1,0:T(8,128)(2,1)}, u32[]{:S(2)}, u32[]{:S(2)}) collective-permute-start(bf16[4096,768]{1,0:T(8,128)(2,1)} %own.7), channel_id=1, source_target_pairs={{0,4},{4,0},{1,5},{5,1},{2,6},{6,2},{3,7},{7,3},{8,12},{12,8},{9,1... | collective-permute-start | bytes 18874376 | tf_op jit(solution)/shard_map/ppermute | solution.py:289
  2.7 48.4 %copy-start.1 = (s32[4096,1]{0,1:T(1,128)S(1)}, s32[4096,1]{0,1:T(1,128)}, u32[]{:S(2)}) copy-start(s32[4096,1]{0,1:T(1,128)} %param.4) | copy-start | bytes 49156
  10.3 3.2 %collective-permute-start = (f32[64,8,512]{2,1,0:T(8,128)}, f32[64,8,512]{2,1,0:T(8,128)S(1)}, u32[]{:S(2)}, u32[]{:S(2)}) collective-permute-start(f32[64,8,512]{2,1,0:T(8,128)} %get-tuple-element.7), channel_id=1, source_target_pairs={{0,4},{4,0},{1,5},{5,1},{2,6},{6,2},{3,7},{7,3},{8,12},{12,8},{9,1... | collective-permute-start | bytes 3145736 | tf_op jit(solution)/shard_map/ppermute | solution.py:297
  45.5 16.5 %all-to-all-start.1 = ((bf16[64,8,512]{2,1,0:T(8,128)(2,1)}), bf16[64,8,512]{2,1,0:T(8,128)(2,1)S(1)}, u32[]{:S(2)}, u32[]{:S(2)}) async-start(bf16[64,8,512]{2,1,0:T(8,128)(2,1)} %finish_bfloat16.3), calls=%async_computation.1 | async-start | bytes 1048576 | tf_op jit(solution)/shard_map/all_to_all | solution.py:294
  51.1 2.6 %collective-permute-start.2 = (s32[1,4096]{1,0:T(1,128)S(1)}, s32[1,4096]{1,0:T(1,128)S(1)}, u32[]{:S(2)}, u32[]{:S(2)}) collective-permute-start(s32[1,4096]{1,0:T(1,128)S(1)} %bitcast.9), channel_id=1, source_target_pairs={{0,4},{4,0},{1,5},{5,1},{2,6},{6,2},{3,7},{7,3},{8,12},{12,8},{9,1... | collective-permute-start | bytes 49160 | tf_op jit(solution)/shard_map/ppermute | solution.py:290
  53.7 8.3 %copy-start.2 = (s32[1,4096]{1,0:T(1,128)}, s32[1,4096]{1,0:T(1,128)S(1)}, u32[]{:S(2)}) copy-start(s32[1,4096]{1,0:T(1,128)S(1)} %collective-permute-done.2.other_owner) | copy-start | bytes 49156
  62.0 0.8 copy-start
  226.2 9.2 %collective-permute-start.3 = (f32[8,4096]{1,0:T(8,128)S(1)}, f32[8,4096]{1,0:T(8,128)S(1)}, u32[]{:S(2)}, u32[]{:S(2)}) collective-permute-start(f32[8,4096]{1,0:T(8,128)S(1)} %slice.7), channel_id=1, source_target_pairs={{0,4},{4,0},{1,5},{5,1},{2,6},{6,2},{3,7},{7,3},{8,12},{12,8},{9,1... | collective-permute-start | bytes 393224 | tf_op jit(solution)/shard_map/ppermute | solution.py:304

commit v3 on v2

--- a/solution.py
+++ b/solution.py
@@ -87,7 +87,7 @@
 
 IN_VMEM = pl.BlockSpec(memory_space=pltpu.VMEM)
 IN_SMEM = pl.BlockSpec(memory_space=pltpu.SMEM)
-IN_PLACE = pl.BlockSpec(memory_space=pl.ANY)
+IN_PLACE = pl.BlockSpec(memory_space=pltpu.HBM)
 
 
 def seed_sums(core, members, owner, seeds):
@@ -105,38 +105,41 @@
             pltpu.VMEM((rows, D), bf16),
             pltpu.SemaphoreType.DMA((SEED_COPIES,)),
         ],
+        compiler_params=pltpu.CompilerParams(vmem_limit_bytes=59 << 20),
         name="seed_sums",
     )(core, members, owner, seeds)
 
 
-def finish_kernel(parts, out):
+def finish_kernel(parts, out, exact):
     total = parts[0]
     for seat in range(1, SEATS):
         total = total + parts[seat]
     count = jnp.sum(total[:, HALF_D:], axis=1, keepdims=True)
     centers = total[:, :HALF_D] / (count + 1.0)
+    exact[...] = centers
     norm = jnp.sum(centers * centers, axis=1, keepdims=True)
     lane = lax.broadcasted_iota(jnp.int32, (K, LANES), 1)
     norms = jnp.broadcast_to(norm, (K, LANES))
-    if out.dtype == bf16:
-        high = norms.astype(bf16).astype(f32)
-        middle = (norms - high).astype(bf16).astype(f32)
-        low = norms - high - middle
-        tail = jnp.where(lane == 0, high, jnp.where(lane == 1, middle, jnp.where(lane == 2, low, 0.0)))
-    else:
-        tail = jnp.where(lane == 0, norms, 0.0)
-    block = jnp.concatenate([centers, tail], axis=1).astype(out.dtype)
+    high = norms.astype(bf16).astype(f32)
+    middle = (norms - high).astype(bf16).astype(f32)
+    low = norms - high - middle
+    tail = jnp.where(lane == 0, high, jnp.where(lane == 1, middle, jnp.where(lane == 2, low, 0.0)))
+    block = jnp.concatenate([centers, tail], axis=1).astype(bf16)
     for seat in range(SEATS):
         out[seat] = block
 
 
-def finish(parts, dtype):
+def finish(parts):
     return pl.pallas_call(
         finish_kernel,
         in_specs=[IN_VMEM],
-        out_specs=IN_VMEM,
-        out_shape=jax.ShapeDtypeStruct((SEATS, K, CHUNK), dtype),
-        name="finish_" + jnp.dtype(dtype).name,
+        out_specs=[IN_VMEM, IN_VMEM],
+        out_shape=[
+            jax.ShapeDtypeStruct((SEATS, K, CHUNK), bf16),
+            jax.ShapeDtypeStruct((K, HALF_D), f32),
+        ],
+        compiler_params=pltpu.CompilerParams(vmem_limit_bytes=4 << 20),
+        name="finish",
     )(parts)
 
 
@@ -232,51 +235,60 @@
             pltpu.VMEM((rows, D), bf16),
             pltpu.SemaphoreType.DMA((2 * COPIES,)),
         ],
+        compiler_params=pltpu.CompilerParams(vmem_limit_bytes=59 << 20),
         name="round_sums",
     )(core, packed, own, own_owner, other, other_owner)
 
 
 def assign_kernel(
-    core, packed, own, own_owner, other, other_owner, out, held, cen, nrm, owners, dots, buf, sems
+    core, packed, own, own_owner, other, other_owner, mine, near, far, wide,
+    kept, given, held, cen, nrm, owners, dots, blocks, buf, sems,
 ):
     start_copies([own, other], buf, sems, COPIES)
     unpack_centers(packed, cen, nrm)
     both_owners(core[0], own_owner, other_owner, owners)
-    for name in range(2):
-        for half in range(2):
-            block = packed[core[1] + 2 * name + half]
-            held[name, :, half * HALF_D : (half + 1) * HALF_D] = block[:, :HALF_D]
-
-    def work(turn, carry):
-        both_waits(own, buf, sems, turn)
-        for part in range(UNROLL):
-            dots[part] = dots_of(turn * UNROLL + part, cen, buf)
-        for part in range(UNROLL):
-            spot = at_tile(turn * UNROLL + part)
-            names = jnp.broadcast_to(owners[:, spot], (K, TILE))
-            out[:, spot] = jnp.where(names < OWN_LISTS, soft_weights(dots, part, nrm, names), 0.0)
-        return carry
-
-    lax.fori_loop(0, COPIES, work, 0)
-
-
-def assign(core, packed, own, own_owner, other, other_owner):
-    rows = 2 * own.shape[0]
+    for shift, block in enumerate((mine, near, far, wide)):
+        blocks[shift] = block[...]
+    for seat in range(4):
+        held[seat // 2, :, seat % 2 * HALF_D : (seat % 2 + 1) * HALF_D] = blocks[(core[1] - seat) & 3]
+
+    def work_on(out, first):
+        def work(turn, carry):
+            both_waits(own, buf, sems, turn + first)
+            for part in range(UNROLL):
+                dots[part] = dots_of((turn + first) * UNROLL + part, cen, buf)
+            for part in range(UNROLL):
+                names = jnp.broadcast_to(owners[:, at_tile((turn + first) * UNROLL + part)], (K, TILE))
+                weights = soft_weights(dots, part, nrm, names)
+                out[:, at_tile(turn * UNROLL + part)] = jnp.where(names < OWN_LISTS, weights, 0.0)
+            return carry
+
+        lax.fori_loop(0, COPIES // 2, work, 0)
+
+    work_on(kept, 0)
+    work_on(given, COPIES // 2)
+
+
+def assign(core, packed, own, own_owner, other, other_owner, *blocks):
+    rows = own.shape[0]
+    part = jax.ShapeDtypeStruct((K, rows), f32)
     return pl.pallas_call(
         assign_kernel,
-        in_specs=[IN_SMEM, IN_VMEM, IN_PLACE, IN_VMEM, IN_PLACE, IN_VMEM],
-        out_specs=[IN_VMEM, IN_VMEM],
-        out_shape=[jax.ShapeDtypeStruct((K, rows), f32), jax.ShapeDtypeStruct((2, K, D), f32)],
+        in_specs=[IN_SMEM, IN_VMEM, IN_PLACE, IN_VMEM, IN_PLACE, IN_VMEM] + [IN_VMEM] * 4,
+        out_specs=[IN_VMEM, IN_VMEM, IN_VMEM],
+        out_shape=[part, part, jax.ShapeDtypeStruct((2, K, D), f32)],
         scratch_shapes=[
             pltpu.VMEM((OWN_LISTS * K, D), bf16),
             pltpu.VMEM((OWN_LISTS * K, LANES), f32),
-            pltpu.VMEM((1, rows), jnp.int32),
+            pltpu.VMEM((1, 2 * rows), jnp.int32),
             pltpu.VMEM((UNROLL, OWN_LISTS * K, TILE), f32),
-            pltpu.VMEM((rows, D), bf16),
+            pltpu.VMEM((4, K, HALF_D), f32),
+            pltpu.VMEM((2 * rows, D), bf16),
             pltpu.SemaphoreType.DMA((2 * COPIES,)),
         ],
+        compiler_params=pltpu.CompilerParams(vmem_limit_bytes=59 << 20),
         name="assign",
-    )(core, packed, own, own_owner, other, other_owner)
+    )(core, packed, own, own_owner, other, other_owner, *blocks)
 
 
 SWAP = [(0, 1), (1, 0)]
@@ -284,7 +296,7 @@
 
 
 def local(members, owner, seed_label):
-    place = jnp.stack([lax.axis_index("c"), lax.axis_index(("x", "z")) * 4]).astype(jnp.int32)
+    place = jnp.stack([lax.axis_index("c"), lax.axis_index("y")]).astype(jnp.int32)
     owner = owner.reshape(1, -1)
     other = lax.ppermute(members, "c", SWAP)
     other_owner = lax.ppermute(owner, "c", SWAP)
@@ -296,13 +308,14 @@
     mine, theirs = seed_sums(place, members, owner, seed_label.reshape(1, -1))
     parts = mine + lax.ppermute(theirs, "c", SWAP)
     for turn in range(ITERS):
-        packed = exchange(finish(exchange(parts), bf16))
+        packed = exchange(finish(exchange(parts))[0])
         parts = round_sums(place, packed, *both)
-    packed = exchange(finish(exchange(parts), f32))
-    weights, centers = assign(place, packed, *both)
-    rows = members.shape[0]
-    swapped = lax.ppermute(weights[:, rows:], "c", SWAP)
-    return weights[:, :rows] + swapped, centers
+    packed, exact = finish(exchange(parts))
+    blocks = [exact] + [
+        lax.ppermute(exact, "y", [(seat, (seat + shift) % 4) for seat in range(4)]) for shift in (1, 2, 3)
+    ]
+    kept, given, centers = assign(place, exchange(packed), *both, *blocks)
+    return kept + lax.ppermute(given, "c", SWAP), centers
 
 
 def solution(mesh):

time: 238 us -> 226 us (0.950)
  blocking collectives: 140 us -> 118 us
  starting transfers between devices: 17.2 us -> 25.5 us
  waiting for transfers between devices: 13.3 us -> 20.7 us
  Pallas kernels: 60.9 us -> 54.8 us
    all_to_all x7 -> x6, blocking collectives: 140 us -> 118 us  [exchange(): lax.all_to_all(parts, SEAT_AXES, split_axis=0, concat_axis=0, tiled=True)]
    pallas_call x4, Pallas kernels: 9.42 us -> 3.62 us  [finish(): pl.pallas_call(finish_kernel, in_specs=[IN_VMEM], out_specs=[IN_VMEM, IN_...]
    all_to_all x1 -> x2, starting transfers between devices: 5.6 us -> 10.2 us  [exchange(): lax.all_to_all(parts, SEAT_AXES, split_axis=0, concat_axis=0, tiled=True)]
    ppermute x1 -> x4, waiting for transfers between devices: 0.99 us -> 4.99 us  [the longest x3 3.8 us: local(): lax.ppermute(exact, 'y', [(seat, (seat + shift) % 4) for seat in range(4)])]
    ppermute x1 -> x4, starting transfers between devices: 8.26 us -> 12 us  [the longest x1 8.63 us: local(): return (kept + lax.ppermute(given, 'c', SWAP), centers)]
    all_to_all x1 -> x2, waiting for transfers between devices: 8.32 us -> 11.7 us  [exchange(): lax.all_to_all(parts, SEAT_AXES, split_axis=0, concat_axis=0, tiled=True)]
  transfers between devices with their start and end apart: 5 -> 9, of which waited for: 4 -> 7; matrix products, arithmetic and copies ran while one was open for 1% -> 1% of each run, Pallas kernels for 4% -> 4%
where the time goes in v3:
time: 226 us; the launch traced here: 225 us
  blocking collectives  118 us (52%)
  Pallas kernels  54.8 us (24%)
  starting transfers between devices  25.5 us (11%)
  waiting for transfers between devices  20.7 us (9%)
  other arithmetic  3.59 us (2%)
    all_to_all x6, blocking collectives, exchange(): lax.all_to_all(parts, SEAT_AXES, split_axis=0, concat_axis=0, tiled=True)  118 us
    pallas_call x3, Pallas kernels, round_sums(): pl.pallas_call(round_kernel, in_specs=[IN_SMEM, IN_VMEM, IN_PLACE, IN_VME...  35.6 us
    all_to_all x2, waiting for transfers between devices, exchange(): lax.all_to_all(parts, SEAT_AXES, split_axis=0, concat_axis=0, tiled=True)  11.7 us
    all_to_all x2, starting transfers between devices, exchange(): lax.all_to_all(parts, SEAT_AXES, split_axis=0, concat_axis=0, tiled=True)  10.2 us
    ppermute x1, starting transfers between devices, local(): return (kept + lax.ppermute(given, 'c', SWAP), centers)  8.63 us
    pallas_call x1, Pallas kernels, assign(): pl.pallas_call(assign_kernel, in_specs=[IN_SMEM, IN_VMEM, IN_PLACE, IN_VM...  7.91 us
    pallas_call x1, Pallas kernels, seed_sums(): pl.pallas_call(seed_kernel, in_specs=[IN_SMEM, IN_PLACE, IN_VMEM, IN_VMEM...  7.7 us
  transfers between devices with their start and end apart: 9, of which 7 were waited for; matrix products, arithmetic and copies ran while one was open for 1% of the time, Pallas kernels for 4%

profile of v3, /device:TPU:1, one launch (start us, length us, event | category | flops | bytes accessed | tf_op | source)
XLA Modules:
  0.0 225.2 jit_solution(5129560183171166298)
XLA Ops:
  0.6 1.5 collective-permute-start.1
  2.7 7.7 %seed_sums.1 = (f32[64,8,512]{2,1,0:T(8,128)}, f32[64,8,512]{2,1,0:T(8,128)}) custom-call(s32[2]{0:T(128)} %pad_add_fusion.core, bf16[4096,768]{1,0:T(8,128)(2,1)} %own.7, s32[1,4096]{1,0:T(1,128)} %bitcast.4, s32[1,4096]{1,0:T(1,128)} %bitcast.10), custom_call_target="tpu_custom_call" | custom-call | tf_op jit(solution)/shard_map/seed_sums/pallas_call | solution.py:96
  10.5 3.1 %collective-permute-done = f32[64,8,512]{2,1,0:T(8,128)S(1)} collective-permute-done((f32[64,8,512]{2,1,0:T(8,128)}, f32[64,8,512]{2,1,0:T(8,128)S(1)}, u32[]{:S(2)}, u32[]{:S(2)}) %collective-permute-start) | collective-permute-done | bytes 1048608 | tf_op jit(solution)/shard_map/ppermute | solution.py:309
  13.6 1.4 add.6
  15.0 28.1 %all_to_all.40.parts = f32[64,8,512]{2,1,0:T(8,128)S(1)} all-to-all(f32[64,8,512]{2,1,0:T(8,128)S(1)} %add.6), channel_id=1, replica_groups=mesh['x'=4,'z'=4,'c'=2,'y'=4] {'x','z','y'}, dimensions={0} | all-to-all | bytes 2097152 | tf_op jit(solution)/shard_map/all_to_all | solution.py:306
  43.1 1.1 finish.4
  44.2 5.6 %all-to-all-start.1 = ((bf16[64,8,512]{2,1,0:T(8,128)(2,1)}), bf16[64,8,512]{2,1,0:T(8,128)(2,1)S(1)}, u32[]{:S(2)}, u32[]{:S(2)}) async-start(bf16[64,8,512]{2,1,0:T(8,128)(2,1)} %get-tuple-element.14), calls=%async_computation.1 | async-start | bytes 1048576 | tf_op jit(solution)/shard_map/all_to_all | solution.py:306
  49.8 1.8 collective-permute-start.2
  51.6 0.8 collective-permute-done.2.other_owner
  52.4 8.3 %all-to-all-done.1.packed = bf16[64,8,512]{2,1,0:T(8,128)(2,1)S(1)} async-done(((bf16[64,8,512]{2,1,0:T(8,128)(2,1)}), bf16[64,8,512]{2,1,0:T(8,128)(2,1)S(1)}, u32[]{:S(2)}, u32[]{:S(2)}) %all-to-all-start.1) | async-done | bytes 524320 | tf_op jit(solution)/shard_map/all_to_all | solution.py:306
  60.7 0.8 copy-done.2
  61.5 11.9 %round_sums.3 = f32[64,8,512]{2,1,0:T(8,128)} custom-call(s32[2]{0:T(128)} %pad_add_fusion.core, bf16[64,8,512]{2,1,0:T(8,128)(2,1)} %copy-done.2, bf16[4096,768]{1,0:T(8,128)(2,1)} %own.7, s32[1,4096]{1,0:T(1,128)} %bitcast.5, bf16[4096,768]{1,0:T(8,128)(2,1)} %collective-permute-done.1.other, s32[1,4096]{1,0:T(1,128)} %copy-done.4), custom_call_target="tpu_custom_call" | custom-call | tf_op jit(solution)/shard_map/round_sums/pallas_call | solution.py:223
  73.4 22.0 %all_to_all.41.parts = f32[64,8,512]{2,1,0:T(8,128)S(1)} all-to-all(f32[64,8,512]{2,1,0:T(8,128)} %round_sums.3), channel_id=1, replica_groups=mesh['x'=4,'z'=4,'c'=2,'y'=4] {'x','z','y'}, dimensions={0} | all-to-all | bytes 2097152 | tf_op jit(solution)/shard_map/all_to_all | solution.py:306
  95.4 0.8 finish.5
  96.2 15.3 %all_to_all.42.packed = bf16[64,8,512]{2,1,0:T(8,128)(2,1)} all-to-all(bf16[64,8,512]{2,1,0:T(8,128)(2,1)S(1)} %get-tuple-element.15), channel_id=1, replica_groups=mesh['x'=4,'z'=4,'c'=2,'y'=4] {'x','z','y'}, dimensions={0} | all-to-all | bytes 1048576 | tf_op jit(solution)/shard_map/all_to_all | solution.py:306
  111.5 11.9 %round_sums.4 = f32[64,8,512]{2,1,0:T(8,128)} custom-call(s32[2]{0:T(128)} %pad_add_fusion.core, bf16[64,8,512]{2,1,0:T(8,128)(2,1)} %all_to_all.42.packed, bf16[4096,768]{1,0:T(8,128)(2,1)} %own.7, s32[1,4096]{1,0:T(1,128)} %bitcast.6, bf16[4096,768]{1,0:T(8,128)(2,1)} %collective-permute-done.1.other, s32[1,4096]{1,0:T(1,128)} %copy-done.4), custom_call_target="tpu_custom_call" | custom-call | tf_op jit(solution)/shard_map/round_sums/pallas_call | solution.py:223
  123.3 18.9 %all_to_all.43.parts = f32[64,8,512]{2,1,0:T(8,128)S(1)} all-to-all(f32[64,8,512]{2,1,0:T(8,128)} %round_sums.4), channel_id=1, replica_groups=mesh['x'=4,'z'=4,'c'=2,'y'=4] {'x','z','y'}, dimensions={0} | all-to-all | bytes 2097152 | tf_op jit(solution)/shard_map/all_to_all | solution.py:306
  142.2 0.8 finish.6
  143.0 15.5 %all_to_all.44.packed = bf16[64,8,512]{2,1,0:T(8,128)(2,1)} all-to-all(bf16[64,8,512]{2,1,0:T(8,128)(2,1)S(1)} %get-tuple-element.16), channel_id=1, replica_groups=mesh['x'=4,'z'=4,'c'=2,'y'=4] {'x','z','y'}, dimensions={0} | all-to-all | bytes 1048576 | tf_op jit(solution)/shard_map/all_to_all | solution.py:306
  158.4 11.9 %round_sums.5 = f32[64,8,512]{2,1,0:T(8,128)} custom-call(s32[2]{0:T(128)} %pad_add_fusion.core, bf16[64,8,512]{2,1,0:T(8,128)(2,1)} %all_to_all.44.packed, bf16[4096,768]{1,0:T(8,128)(2,1)} %own.7, s32[1,4096]{1,0:T(1,128)} %bitcast.7, bf16[4096,768]{1,0:T(8,128)(2,1)} %collective-permute-done.1.other, s32[1,4096]{1,0:T(1,128)} %copy-done.4), custom_call_target="tpu_custom_call" | custom-call | tf_op jit(solution)/shard_map/round_sums/pallas_call | solution.py:223
  170.3 18.4 %all_to_all.45.parts = f32[64,8,512]{2,1,0:T(8,128)S(1)} all-to-all(f32[64,8,512]{2,1,0:T(8,128)} %round_sums.5), channel_id=1, replica_groups=mesh['x'=4,'z'=4,'c'=2,'y'=4] {'x','z','y'}, dimensions={0} | all-to-all | bytes 2097152 | tf_op jit(solution)/shard_map/all_to_all | solution.py:306
  188.8 1.1 finish.7
  189.8 4.6 %all-to-all-start.7 = ((bf16[64,8,512]{2,1,0:T(8,128)(2,1)}), bf16[64,8,512]{2,1,0:T(8,128)(2,1)S(1)}, u32[]{:S(2)}, u32[]{:S(2)}) async-start(bf16[64,8,512]{2,1,0:T(8,128)(2,1)} %get-tuple-element.17), calls=%async_computation.7 | async-start | bytes 1048576 | tf_op jit(solution)/shard_map/all_to_all | solution.py:306
  194.5 2.2 collective-permute-start.5
  197.2 0.6 collective-permute-start.3
  197.8 3.4 %collective-permute-done.4.far = f32[8,384]{1,0:T(8,128)S(1)} collective-permute-done((f32[8,384]{1,0:T(8,128)S(1)}, f32[8,384]{1,0:T(8,128)S(1)}, u32[]{:S(2)}, u32[]{:S(2)}) %collective-permute-start.4) | collective-permute-done | bytes 12320 | tf_op jit(solution)/shard_map/ppermute | solution.py:315
  201.6 3.4 %all-to-all-done.7.packed = bf16[64,8,512]{2,1,0:T(8,128)(2,1)S(1)} async-done(((bf16[64,8,512]{2,1,0:T(8,128)(2,1)}), bf16[64,8,512]{2,1,0:T(8,128)(2,1)S(1)}, u32[]{:S(2)}, u32[]{:S(2)}) %all-to-all-start.7) | async-done | bytes 524320 | tf_op jit(solution)/shard_map/all_to_all | solution.py:306
  205.0 0.8 copy-done.1
  205.8 7.9 %assign.1 = (f32[8,4096]{1,0:T(8,128)}, f32[8,4096]{1,0:T(8,128)}, f32[2,8,768]{2,1,0:T(8,128)}) custom-call(s32[2]{0:T(128)} %pad_add_fusion.core, bf16[64,8,512]{2,1,0:T(8,128)(2,1)} %copy-done.1, bf16[4096,768]{1,0:T(8,128)(2,1)} %own.7, s32[1,4096]{1,0:T(1,128)} %bitcast.8, bf16[4096,768]{1,0:T(8,128)(2,1)} %collective-permute-done.1.other, ...), custom_call_target="tpu_custom_call" | custom-call | tf_op jit(solution)/shard_map/assign/pallas_call | solution.py:275
  213.8 8.6 %collective-permute-start.6 = (f32[8,4096]{1,0:T(8,128)}, f32[8,4096]{1,0:T(8,128)S(1)}, u32[]{:S(2)}, u32[]{:S(2)}) collective-permute-start(f32[8,4096]{1,0:T(8,128)} %get-tuple-element.20), channel_id=1, source_target_pairs={{0,4},{4,0},{1,5},{5,1},{2,6},{6,2},{3,7},{7,3},{8,12},{12,8},{9,1... | collective-permute-start | bytes 393224 | tf_op jit(solution)/shard_map/ppermute | solution.py:318
  222.4 1.2 collective-permute-done.6
  223.6 1.6 add.7
  (20 shorter events, 1.7 us)
Async XLA Ops:
  0.6 60.1 %collective-permute-start.1 = (bf16[4096,768]{1,0:T(8,128)(2,1)}, bf16[4096,768]{1,0:T(8,128)(2,1)}, u32[]{:S(2)}, u32[]{:S(2)}) collective-permute-start(bf16[4096,768]{1,0:T(8,128)(2,1)} %own.7), channel_id=1, source_target_pairs={{0,4},{4,0},{1,5},{5,1},{2,6},{6,2},{3,7},{7,3},{8,12},{12,8},{9,1... | collective-permute-start | bytes 18874376 | tf_op jit(solution)/shard_map/ppermute | solution.py:301
  2.7 47.1 %copy-start.3 = (s32[4096,1]{0,1:T(1,128)S(1)}, s32[4096,1]{0,1:T(1,128)}, u32[]{:S(2)}) copy-start(s32[4096,1]{0,1:T(1,128)} %param.4) | copy-start | bytes 49156
  10.4 3.2 %collective-permute-start = (f32[64,8,512]{2,1,0:T(8,128)}, f32[64,8,512]{2,1,0:T(8,128)S(1)}, u32[]{:S(2)}, u32[]{:S(2)}) collective-permute-start(f32[64,8,512]{2,1,0:T(8,128)} %get-tuple-element.13), channel_id=1, source_target_pairs={{0,4},{4,0},{1,5},{5,1},{2,6},{6,2},{3,7},{7,3},{8,12},{12,8},{9,1... | collective-permute-start | bytes 3145736 | tf_op jit(solution)/shard_map/ppermute | solution.py:309
  44.2 16.5 %all-to-all-start.1 = ((bf16[64,8,512]{2,1,0:T(8,128)(2,1)}), bf16[64,8,512]{2,1,0:T(8,128)(2,1)S(1)}, u32[]{:S(2)}, u32[]{:S(2)}) async-start(bf16[64,8,512]{2,1,0:T(8,128)(2,1)} %get-tuple-element.14), calls=%async_computation.1 | async-start | bytes 1048576 | tf_op jit(solution)/shard_map/all_to_all | solution.py:306
  49.8 2.6 %collective-permute-start.2 = (s32[1,4096]{1,0:T(1,128)S(1)}, s32[1,4096]{1,0:T(1,128)S(1)}, u32[]{:S(2)}, u32[]{:S(2)}) collective-permute-start(s32[1,4096]{1,0:T(1,128)S(1)} %bitcast.9), channel_id=1, source_target_pairs={{0,4},{4,0},{1,5},{5,1},{2,6},{6,2},{3,7},{7,3},{8,12},{12,8},{9,1... | collective-permute-start | bytes 49160 | tf_op jit(solution)/shard_map/ppermute | solution.py:302
  52.4 8.3 %copy-start.4 = (s32[1,4096]{1,0:T(1,128)}, s32[1,4096]{1,0:T(1,128)S(1)}, u32[]{:S(2)}) copy-start(s32[1,4096]{1,0:T(1,128)S(1)} %collective-permute-done.2.other_owner) | copy-start | bytes 49156
  60.7 0.8 copy-start.2
  189.8 15.2 %copy-start = (f32[8,384]{1,0:T(8,128)}, f32[8,384]{1,0:T(8,128)S(1)}, u32[]{:S(2)}) copy-start(f32[8,384]{1,0:T(8,128)S(1)} %get-tuple-element.18.mine) | copy-start | bytes 36868
  189.8 15.2 %all-to-all-start.7 = ((bf16[64,8,512]{2,1,0:T(8,128)(2,1)}), bf16[64,8,512]{2,1,0:T(8,128)(2,1)S(1)}, u32[]{:S(2)}, u32[]{:S(2)}) async-start(bf16[64,8,512]{2,1,0:T(8,128)(2,1)} %get-tuple-element.17), calls=%async_computation.7 | async-start | bytes 1048576 | tf_op jit(solution)/shard_map/all_to_all | solution.py:306
  194.5 3.3 %collective-permute-start.5 = (f32[8,384]{1,0:T(8,128)S(1)}, f32[8,384]{1,0:T(8,128)S(1)}, u32[]{:S(2)}, u32[]{:S(2)}) collective-permute-start(f32[8,384]{1,0:T(8,128)S(1)} %get-tuple-element.18.mine), channel_id=1, source_target_pairs={{0,3},{1,0},{2,1},{3,2},{4,7},{5,4},{6,5},{7,6},{8,11},{9,8},{10,9... | collective-permute-start | bytes 36872 | tf_op jit(solution)/shard_map/ppermute | solution.py:315
  196.6 4.5 %collective-permute-start.4 = (f32[8,384]{1,0:T(8,128)S(1)}, f32[8,384]{1,0:T(8,128)S(1)}, u32[]{:S(2)}, u32[]{:S(2)}) collective-permute-start(f32[8,384]{1,0:T(8,128)S(1)} %get-tuple-element.18.mine), channel_id=1, source_target_pairs={{0,2},{1,3},{2,0},{3,1},{4,6},{5,7},{6,4},{7,5},{8,10},{9,11},{10,... | collective-permute-start | bytes 36872 | tf_op jit(solution)/shard_map/ppermute | solution.py:315
  197.2 4.4 %collective-permute-start.3 = (f32[8,384]{1,0:T(8,128)S(1)}, f32[8,384]{1,0:T(8,128)S(1)}, u32[]{:S(2)}, u32[]{:S(2)}) collective-permute-start(f32[8,384]{1,0:T(8,128)S(1)} %get-tuple-element.18.mine), channel_id=1, source_target_pairs={{0,1},{1,2},{2,3},{3,0},{4,5},{5,6},{6,7},{7,4},{8,9},{9,10},{10,1... | collective-permute-start | bytes 36872 | tf_op jit(solution)/shard_map/ppermute | solution.py:315
  197.8 7.2 %copy-start.5 = (f32[8,384]{1,0:T(8,128)}, f32[8,384]{1,0:T(8,128)S(1)}, u32[]{:S(2)}) copy-start(f32[8,384]{1,0:T(8,128)S(1)} %collective-permute-done.5.wide) | copy-start | bytes 36868
  201.2 3.8 %copy-start.6 = (f32[8,384]{1,0:T(8,128)}, f32[8,384]{1,0:T(8,128)S(1)}, u32[]{:S(2)}) copy-start(f32[8,384]{1,0:T(8,128)S(1)} %collective-permute-done.4.far) | copy-start | bytes 36868
  201.6 3.4 %copy-start.7 = (f32[8,384]{1,0:T(8,128)}, f32[8,384]{1,0:T(8,128)S(1)}, u32[]{:S(2)}) copy-start(f32[8,384]{1,0:T(8,128)S(1)} %collective-permute-done.3.near) | copy-start | bytes 36868
  205.0 0.8 copy-start.1
  213.8 9.8 %collective-permute-start.6 = (f32[8,4096]{1,0:T(8,128)}, f32[8,4096]{1,0:T(8,128)S(1)}, u32[]{:S(2)}, u32[]{:S(2)}) collective-permute-start(f32[8,4096]{1,0:T(8,128)} %get-tuple-element.20), channel_id=1, source_target_pairs={{0,4},{4,0},{1,5},{5,1},{2,6},{6,2},{3,7},{7,3},{8,12},{12,8},{9,1... | collective-permute-start | bytes 393224 | tf_op jit(solution)/shard_map/ppermute | solution.py:318

commit v4 on v3

v4 whole, which is shorter than its diff:
```python
import jax
import jax.numpy as jnp
from jax import lax
from jax.experimental import pallas as pl
from jax.experimental.pallas import tpu as pltpu
from jax.sharding import Mesh, PartitionSpec as P

K = 8
D = 768
ITERS = 3
HALF_D = D // 2
LANES = 128
CHUNK = HALF_D + LANES
OWN_LISTS = 32
SEATS = 64
TILE = 512
UNROLL = 8
COPIES = 4
SEED_COPIES = 4
f32 = jnp.float32
bf16 = jnp.bfloat16


def lane_fold(block):
    total = block[:, :LANES]
    for at in range(LANES, block.shape[1], LANES):
        total = total + block[:, at : at + LANES]
    return total


def store_sums(out, acc, tot, base):
    for seat in range(SEATS):
        row, half = base + (seat // 2) * K, seat % 2
        out[seat, :, :HALF_D] = acc[row : row + K, half * HALF_D : (half + 1) * HALF_D]
        out[seat, :, HALF_D:] = tot[row : row + K, :]


def relative(names, core):
    away = ((names >> 1) & 1) ^ core
    return (names >> 2) * 2 + (names & 1) + OWN_LISTS * away


def start_copies(sources, buf, sems, copies):
    rows = sources[0].shape[0] // copies
    for number in range(len(sources) * copies):
        source = sources[number // copies].at[pl.ds(number % copies * rows, rows), :]
        pltpu.make_async_copy(source, buf.at[pl.ds(number * rows, rows), :], sems.at[number]).start()


def wait_copy(source, buf, sems, copies, number):
    rows = source.shape[0] // copies
    pltpu.make_async_copy(
        source.at[pl.ds(0, rows), :], buf.at[pl.ds(number * rows, rows), :], sems.at[number]
    ).wait()


def at_tile(tile):
    return pl.ds(pl.multiple_of(tile * TILE, TILE), TILE)


def seed_kernel(core, members, owner, seeds, mine, theirs, ids, held, acc, tot, code, buf, sems, pair):
    start_copies([members], held, sems, SEED_COPIES)
    pltpu.make_async_copy(owner, ids, pair.at[0]).start()
    pltpu.make_async_copy(seeds, buf, pair.at[1]).start()
    acc[...] = jnp.zeros_like(acc)
    tot[...] = jnp.zeros_like(tot)
    pltpu.make_async_copy(owner, ids, pair.at[0]).wait()
    pltpu.make_async_copy(seeds, buf, pair.at[1]).wait()
    ids[...] = relative(ids[...], core[0])
    code[...] = ids[...] * K + buf[...]
    groups = lax.broadcasted_iota(jnp.int32, (K, TILE), 0)
    unroll = members.shape[0] // TILE // SEED_COPIES

    def work(turn, carry):
        wait_copy(members, held, sems, SEED_COPIES, turn)
        for part in range(unroll):
            spot = at_tile(turn * unroll + part)
            shifted = jnp.broadcast_to(code[:, spot], (K, TILE)) - groups
            rows = []
            for name in range(2 * OWN_LISTS):
                hot = jnp.where(shifted == name * K, 1.0, 0.0).astype(f32)
                tot[name * K : (name + 1) * K, :] += lane_fold(hot)
                rows.append(hot)
            hots = jnp.concatenate(rows, axis=0).astype(bf16)
            acc[...] += jnp.dot(hots, held[spot, :], preferred_element_type=f32)
        return carry

    lax.fori_loop(0, SEED_COPIES, work, 0)
    store_sums(mine, acc, tot, 0)
    store_sums(theirs, acc, tot, OWN_LISTS * K)


IN_VMEM = pl.BlockSpec(memory_space=pltpu.VMEM)
IN_SMEM = pl.BlockSpec(memory_space=pltpu.SMEM)
IN_PLACE = pl.BlockSpec(memory_space=pltpu.HBM)


def seed_sums(core, members, owner, seeds):
    part = jax.ShapeDtypeStruct((SEATS, K, CHUNK), f32)
    rows = members.shape[0]
    return pl.pallas_call(
        seed_kernel,
        in_specs=[IN_SMEM, IN_PLACE, IN_PLACE, IN_PLACE],
        out_specs=[IN_VMEM] * 4,
        out_shape=[
            part,
            part,
            jax.ShapeDtypeStruct((1, rows), jnp.int32),
            pltpu.VMEM((2 * rows, D), bf16),
        ],
        scratch_shapes=[
            pltpu.VMEM((2 * OWN_LISTS * K, D), f32),
            pltpu.VMEM((2 * OWN_LISTS * K, LANES), f32),
            pltpu.VMEM((1, rows), jnp.int32),
            pltpu.VMEM((1, rows), jnp.int32),
            pltpu.SemaphoreType.DMA((SEED_COPIES,)),
            pltpu.SemaphoreType.DMA((2,)),
        ],
        compiler_params=pltpu.CompilerParams(vmem_limit_bytes=24 << 20),
        name="seed_sums",
    )(core, members, owner, seeds)


def finish_kernel(parts, out, exact):
    total = parts[0]
    for seat in range(1, SEATS):
        total = total + parts[seat]
    count = jnp.sum(total[:, HALF_D:], axis=1, keepdims=True)
    centers = total[:, :HALF_D] / (count + 1.0)
    exact[...] = centers
    norm = jnp.sum(centers * centers, axis=1, keepdims=True)
    lane = lax.broadcasted_iota(jnp.int32, (K, LANES), 1)
    norms = jnp.broadcast_to(norm, (K, LANES))
    high = norms.astype(bf16).astype(f32)
    middle = (norms - high).astype(bf16).astype(f32)
    low = norms - high - middle
    tail = jnp.where(lane == 0, high, jnp.where(lane == 1, middle, jnp.where(lane == 2, low, 0.0)))
    block = jnp.concatenate([centers, tail], axis=1).astype(bf16)
    for seat in range(SEATS):
        out[seat] = block


def finish(parts):
    return pl.pallas_call(
        finish_kernel,
        in_specs=[IN_VMEM],
        out_specs=[IN_VMEM, IN_VMEM],
        out_shape=[
            jax.ShapeDtypeStruct((SEATS, K, CHUNK), bf16),
            jax.ShapeDtypeStruct((K, HALF_D), f32),
        ],
        compiler_params=pltpu.CompilerParams(vmem_limit_bytes=4 << 20),
        name="finish",
    )(parts)


def unpack_centers(packed, cen, nrm):
    for pair in range(OWN_LISTS // 2):
        for half in range(2):
            blocks = [packed[4 * pair + 2 * i + half].astype(f32) for i in range(2)]
            cen[pair * 16 : pair * 16 + 16, half * HALF_D : (half + 1) * HALF_D] = jnp.concatenate(
                [b[:, :HALF_D] for b in blocks], axis=0
            ).astype(bf16)
        for i in range(2):
            name = 2 * pair + i
            tails = packed[2 * name][:, HALF_D:].astype(f32) + packed[2 * name + 1][:, HALF_D:].astype(f32)
            nrm[name * K : (name + 1) * K, :] = jnp.broadcast_to(
                jnp.sum(tails, axis=1, keepdims=True), (K, LANES)
            )


def dots_of(tile, cen, members):
    return lax.dot_general(
        cen[...], members[at_tile(tile), :], (((1,), (1,)), ((), ())), preferred_element_type=f32
    )


def soft_weights(dots, slot, nrm, names, offset):
    dot = jnp.zeros((K, TILE), f32)
    norm = jnp.zeros((K, TILE), f32)
    for name in range(OWN_LISTS):
        here = names == name + offset
        rows = slice(name * K, (name + 1) * K)
        dot = jnp.where(here, dots[slot, rows, :], dot)
        norm = jnp.where(here, jnp.concatenate([nrm[rows, :]] * (TILE // LANES), axis=1), norm)
    logits = (2.0 * dot - norm) / 2.0
    exps = jnp.exp(logits - jnp.max(logits, axis=0, keepdims=True))
    return exps / jnp.sum(exps, axis=0, keepdims=True)


def add_members(near_ids, far_ids, held, ids, cen, nrm, acc, tot, dots, arrive):
    half = near_ids.shape[1]
    ids[:, :half] = near_ids[...]
    ids[:, half:] = far_ids[...] ^ OWN_LISTS
    acc[...] = jnp.zeros_like(acc)
    tot[...] = jnp.zeros_like(tot)

    def work(turn, carry):
        arrive(turn)
        for part in range(UNROLL):
            dots[part] = dots_of(turn * UNROLL + part, cen, held)
        for part in range(UNROLL):
            spot = at_tile(turn * UNROLL + part)
            names = jnp.broadcast_to(ids[:, spot], (K, TILE))
            weights = soft_weights(dots, part, nrm, names, 0).astype(bf16).astype(f32)
            rows = []
            for name in range(OWN_LISTS):
                here = jnp.where(names == name, weights, 0.0)
                tot[name * K : (name + 1) * K, :] += lane_fold(here)
                rows.append(here)
            spread = jnp.concatenate(rows, axis=0).astype(bf16)
            acc[...] += jnp.dot(spread, held[spot, :], preferred_element_type=f32)
        return carry

    lax.fori_loop(0, held.shape[0] // TILE // UNROLL, work, 0)


def first_kernel(packed, near_ids, other, far_ids, before, out, held, cen, nrm, acc, tot, ids, dots, sems):
    rows = other.shape[0] // COPIES

    def copy_of(number):
        place = pl.ds(number * rows, rows)
        target = pl.ds(other.shape[0] + number * rows, rows)
        return pltpu.make_async_copy(other.at[place, :], held.at[target, :], sems.at[number])

    for number in range(COPIES):
        copy_of(number).start()
    unpack_centers(packed, cen, nrm)

    def arrive(turn):
        @pl.when(turn == other.shape[0] // TILE // UNROLL)
        def _():
            for number in range(COPIES):
                copy_of(number).wait()

    add_members(near_ids, far_ids, held, ids, cen, nrm, acc, tot, dots, arrive)
    store_sums(out, acc, tot, 0)


def later_kernel(packed, near_ids, held, far_ids, out, cen, nrm, acc, tot, ids, dots):
    unpack_centers(packed, cen, nrm)
    add_members(near_ids, far_ids, held, ids, cen, nrm, acc, tot, dots, lambda turn: None)
    store_sums(out, acc, tot, 0)


def round_scratch(rows):
    return [
        pltpu.VMEM((OWN_LISTS * K, D), bf16),
        pltpu.VMEM((OWN_LISTS * K, LANES), f32),
        pltpu.VMEM((OWN_LISTS * K, D), f32),
        pltpu.VMEM((OWN_LISTS * K, LANES), f32),
        pltpu.VMEM((1, 2 * rows), jnp.int32),
        pltpu.VMEM((UNROLL, OWN_LISTS * K, TILE), f32),
    ]


def first_round(packed, near_ids, other, far_ids, held):
    rows = other.shape[0]
    return pl.pallas_call(
        first_kernel,
        in_specs=[IN_VMEM, IN_VMEM, IN_PLACE, IN_VMEM, IN_VMEM],
        out_specs=[IN_VMEM, IN_VMEM],
        out_shape=[jax.ShapeDtypeStruct((SEATS, K, CHUNK), f32), pltpu.VMEM((2 * rows, D), bf16)],
        input_output_aliases={4: 1},
        scratch_shapes=round_scratch(rows) + [pltpu.SemaphoreType.DMA((COPIES,))],
        compiler_params=pltpu.CompilerParams(vmem_limit_bytes=24 << 20),
        name="first_round",
    )(packed, near_ids, other, far_ids, held)


def later_round(packed, near_ids, held, far_ids):
    return pl.pallas_call(
        later_kernel,
        in_specs=[IN_VMEM] * 4,
        out_specs=IN_VMEM,
        out_shape=jax.ShapeDtypeStruct((SEATS, K, CHUNK), f32),
        scratch_shapes=round_scratch(held.shape[0] // 2),
        compiler_params=pltpu.CompilerParams(vmem_limit_bytes=24 << 20),
        name="later_round",
    )(packed, near_ids, held, far_ids)


def assign_kernel(
    place, packed, own, near_ids, other, far_ids, mine, near, far, wide,
    kept, given, held, cen, nrm, dots, blocks, buf, sems,
):
    start_copies([own, other], buf, sems, COPIES)
    unpack_centers(packed, cen, nrm)
    for shift, block in enumerate((mine, near, far, wide)):
        blocks[shift] = block[...]
    for seat in range(4):
        held[seat // 2, :, seat % 2 * HALF_D : (seat % 2 + 1) * HALF_D] = blocks[(place[1] - seat) & 3]
    half = own.shape[0] // TILE
    group = half // COPIES

    def work_on(out, ids, side):
        def work(turn, carry):
            wait_copy(own, buf, sems, COPIES, side * COPIES + turn)
            for part in range(group):
                dots[part] = dots_of(side * half + turn * group + part, cen, buf)
            for part in range(group):
                spot = at_tile(turn * group + part)
                names = jnp.broadcast_to(ids[:, spot], (K, TILE))
                weights = soft_weights(dots, part, nrm, names, side * OWN_LISTS)
                there = (names < OWN_LISTS) if side == 0 else (names >= OWN_LISTS)
                out[:, spot] = jnp.where(there, weights, 0.0)
            return carry

        lax.fori_loop(0, COPIES, work, 0)

    work_on(kept, near_ids, 0)
    work_on(given, far_ids, 1)


def assign(place, packed, own, near_ids, other, far_ids, *blocks):
    rows = own.shape[0]
    part = jax.ShapeDtypeStruct((K, rows), f32)
    return pl.pallas_call(
        assign_kernel,
        in_specs=[IN_SMEM, IN_VMEM, IN_PLACE, IN_VMEM, IN_PLACE, IN_VMEM] + [IN_VMEM] * 4,
        out_specs=[IN_VMEM, IN_VMEM, IN_VMEM],
        out_shape=[part, part, jax.ShapeDtypeStruct((2, K, D), f32)],
        scratch_shapes=[
            pltpu.VMEM((OWN_LISTS * K, D), bf16),
            pltpu.VMEM((OWN_LISTS * K, LANES), f32),
            pltpu.VMEM((rows // TILE // COPIES, OWN_LISTS * K, TILE), f32),
            pltpu.VMEM((4, K, HALF_D), f32),
            pltpu.VMEM((2 * rows, D), bf16),
            pltpu.SemaphoreType.DMA((2 * COPIES,)),
        ],
        compiler_params=pltpu.CompilerParams(vmem_limit_bytes=24 << 20),
        name="assign",
    )(place, packed, own, near_ids, other, far_ids, *blocks)


SWAP = [(0, 1), (1, 0)]
SEAT_AXES = ("x", "z", "y")


def local(members, owner, seed_label):
    place = jnp.stack([lax.axis_index("c"), lax.axis_index("y")]).astype(jnp.int32)
    swap = lambda value: lax.ppermute(value, "c", SWAP)
    members, other, owner, seeds = (
        pltpu.with_memory_space_constraint(v, pltpu.HBM)
        for v in (members, swap(members), owner.reshape(1, -1), seed_label.reshape(1, -1))
    )

    def exchange(parts):
        return lax.all_to_all(parts, SEAT_AXES, split_axis=0, concat_axis=0, tiled=True)

    mine, theirs, near_ids, held = seed_sums(place, members, owner, seeds)
    parts, far_ids = lax.optimization_barrier((mine + swap(theirs), swap(near_ids)))
    packed = exchange(finish(exchange(parts))[0])
    parts, held = first_round(packed, near_ids, other, far_ids, held)
    for turn in range(ITERS - 1):
        packed = exchange(finish(exchange(parts))[0])
        parts = later_round(packed, near_ids, held, far_ids)
    packed, exact = finish(exchange(parts))
    blocks = [exact] + [
        lax.ppermute(exact, "y", [(seat, (seat + shift) % 4) for seat in range(4)]) for shift in (1, 2, 3)
    ]
    kept, given, centers = assign(place, exchange(packed), members, near_ids, other, far_ids, *blocks)
    return kept + swap(given), centers


def solution(mesh):
    fine = Mesh(mesh.devices.reshape(4, 4, 2, 4), ("x", "z", "c", "y"))
    every = ("x", "z", "c", "y")
    return jax.shard_map(
        local,
        mesh=fine,
        in_specs=(P(every, None), P(every, None), P(every)),
        out_specs=(P(None, every), P(("x", "z", "c"), None, None)),
        check_vma=False,
    )
```

time: 226 us -> 206 us (0.912)
  blocking collectives: 118 us -> 134 us
  Pallas kernels: 54.8 us -> 40 us
  waiting for transfers between devices: 20.7 us -> 11.6 us
  starting transfers between devices: 25.5 us -> 18.8 us
  other arithmetic: 3.59 us -> 0.95 us
    all_to_all x6 -> x7, blocking collectives: 118 us -> 134 us  [exchange(): lax.all_to_all(parts, SEAT_AXES, split_axis=0, concat_axis=0, tiled=True)]
    pallas_call x4, Pallas kernels: 43.3 us -> 29.6 us  [the longest x2 14.7 us: later_round(): pl.pallas_call(later_kernel, in_specs=[IN_VMEM] * 4, out_specs=IN_VMEM, o...]
    all_to_all x2 -> x1, waiting for transfers between devices: 11.7 us -> 3.41 us  [exchange(): lax.all_to_all(parts, SEAT_AXES, split_axis=0, concat_axis=0, tiled=True)]
    all_to_all x2 -> x1, starting transfers between devices: 10.2 us -> 4.63 us  [exchange(): lax.all_to_all(parts, SEAT_AXES, split_axis=0, concat_axis=0, tiled=True)]
  transfers between devices with their start and end apart: 9 -> 8, of which waited for: 7 -> 5; matrix products, arithmetic and copies ran while one was open for 1% -> 0% of each run, Pallas kernels for 4% -> 4%
where the time goes in v4:
time: 206 us
  blocking collectives  134 us (65%)
  Pallas kernels  40 us (19%)
  starting transfers between devices  18.8 us (9%)
  waiting for transfers between devices  11.6 us (6%)
    all_to_all x7, blocking collectives, exchange(): lax.all_to_all(parts, SEAT_AXES, split_axis=0, concat_axis=0, tiled=True)  134 us
    pallas_call x2, Pallas kernels, later_round(): pl.pallas_call(later_kernel, in_specs=[IN_VMEM] * 4, out_specs=IN_VMEM, o...  14.7 us
    ppermute x4, starting transfers between devices, local(): swap = lambda value: lax.ppermute(value, 'c', SWAP)  10.8 us
    pallas_call x1, Pallas kernels, seed_sums(): pl.pallas_call(seed_kernel, in_specs=[IN_SMEM, IN_PLACE, IN_PLACE, IN_PLA...  7.44 us
    pallas_call x1, Pallas kernels, first_round(): pl.pallas_call(first_kernel, in_specs=[IN_VMEM, IN_VMEM, IN_PLACE, IN_VME...  7.42 us
    pallas_call x1, Pallas kernels, assign(): pl.pallas_call(assign_kernel, in_specs=[IN_SMEM, IN_VMEM, IN_PLACE, IN_VM...  7.13 us
    all_to_all x1, starting transfers between devices, exchange(): lax.all_to_all(parts, SEAT_AXES, split_axis=0, concat_axis=0, tiled=True)  4.63 us
    ppermute x4, waiting for transfers between devices, local(): swap = lambda value: lax.ppermute(value, 'c', SWAP)  4.37 us
  transfers between devices with their start and end apart: 8, of which 5 were waited for; matrix products, arithmetic and copies ran while one was open for 0% of the time, Pallas kernels for 4%

profile of v4, /device:TPU:1, one launch (start us, length us, event | category | flops | bytes accessed | tf_op | source)
XLA Modules:
  0.0 205.6 jit_solution(8972243417852901727)
XLA Ops:
  0.6 1.5 collective-permute-start.2
  2.1 0.1 pad_add_fusion.core.place
  2.2 7.4 %seed_sums.1 = (f32[64,8,512]{2,1,0:T(8,128)S(1)}, f32[64,8,512]{2,1,0:T(8,128)S(1)}, s32[1,4096]{1,0:T(1,128)S(1)}, bf16[8192,768]{1,0:T(8,128)(2,1)S(1)}) custom-call(s32[2]{0:T(128)S(1)} %pad_add_fusion.core.place, bf16[4096,768]{1,0:T(8,128)(2,1)} %own.1, s32[1,4096]{1,0:T(1,128)} %bitcast.4, s32[1,4096]{1,0:T(1,128)} %bitcast.5), custom_call_target="tpu_custom_call" | custom-call | tf_op jit(solution)/shard_map/seed_sums/pallas_call | solution.py:101
  9.6 0.1 collective-permute-start
  9.7 0.5 collective-permute-start.1
  10.2 3.4 %collective-permute-done = f32[64,8,512]{2,1,0:T(8,128)S(1)} collective-permute-done((f32[64,8,512]{2,1,0:T(8,128)S(1)}, f32[64,8,512]{2,1,0:T(8,128)S(1)}, u32[]{:S(2)}, u32[]{:S(2)}) %collective-permute-start) | collective-permute-done | bytes 1048608 | tf_op jit(solution)/shard_map/ppermute | solution.py:342
  13.6 0.2 add.6
  13.8 28.1 %all_to_all.40.parts = f32[64,8,512]{2,1,0:T(8,128)S(1)} all-to-all(f32[64,8,512]{2,1,0:T(8,128)S(1)} %add.6), channel_id=1, replica_groups=mesh['x'=4,'z'=4,'c'=2,'y'=4] {'x','z','y'}, dimensions={0} | all-to-all | bytes 2097152 | tf_op jit(solution)/shard_map/all_to_all | solution.py:349
  41.9 0.8 finish.4
  42.7 16.3 %all_to_all.41.packed = bf16[64,8,512]{2,1,0:T(8,128)(2,1)S(1)} all-to-all(bf16[64,8,512]{2,1,0:T(8,128)(2,1)S(1)} %get-tuple-element.22), channel_id=1, replica_groups=mesh['x'=4,'z'=4,'c'=2,'y'=4] {'x','z','y'}, dimensions={0} | all-to-all | bytes 1048576 | tf_op jit(solution)/shard_map/all_to_all | solution.py:349
  59.0 7.4 %first_round.1 = (f32[64,8,512]{2,1,0:T(8,128)S(1)}, bf16[8192,768]{1,0:T(8,128)(2,1)S(1)}) custom-call(bf16[64,8,512]{2,1,0:T(8,128)(2,1)S(1)} %all_to_all.41.packed, s32[1,4096]{1,0:T(1,128)S(1)} %get-tuple-element.20.near_ids, bf16[4096,768]{1,0:T(8,128)(2,1)} %collective-permute-done.2.other, ...), custom_call_target="tpu_custom_call", output_to_operand_aliasing={{1}: (4, {})} | custom-call | tf_op jit(solution)/shard_map/first_round/pallas_call | solution.py:259
  66.4 21.9 %all_to_all.42.parts = f32[64,8,512]{2,1,0:T(8,128)S(1)} all-to-all(f32[64,8,512]{2,1,0:T(8,128)S(1)} %get-tuple-element.25), channel_id=1, replica_groups=mesh['x'=4,'z'=4,'c'=2,'y'=4] {'x','z','y'}, dimensions={0} | all-to-all | bytes 2097152 | tf_op jit(solution)/shard_map/all_to_all | solution.py:349
  88.3 0.8 finish.5
  89.0 15.2 %all_to_all.43.packed = bf16[64,8,512]{2,1,0:T(8,128)(2,1)S(1)} all-to-all(bf16[64,8,512]{2,1,0:T(8,128)(2,1)S(1)} %get-tuple-element.26), channel_id=1, replica_groups=mesh['x'=4,'z'=4,'c'=2,'y'=4] {'x','z','y'}, dimensions={0} | all-to-all | bytes 1048576 | tf_op jit(solution)/shard_map/all_to_all | solution.py:349
  104.2 7.4 %later_round.2 = f32[64,8,512]{2,1,0:T(8,128)S(1)} custom-call(bf16[64,8,512]{2,1,0:T(8,128)(2,1)S(1)} %all_to_all.43.packed, s32[1,4096]{1,0:T(1,128)S(1)} %get-tuple-element.20.near_ids, bf16[8192,768]{1,0:T(8,128)(2,1)S(1)} %get-tuple-element.27.held, s32[1,4096]{1,0:T(1,128)S(1)} %collective-permute-done.1.far_ids), custom_call_target="tpu_custom_call" | custom-call | tf_op jit(solution)/shard_map/later_round/pallas_call | solution.py:272
  111.6 18.7 %all_to_all.44.parts = f32[64,8,512]{2,1,0:T(8,128)S(1)} all-to-all(f32[64,8,512]{2,1,0:T(8,128)S(1)} %later_round.2), channel_id=1, replica_groups=mesh['x'=4,'z'=4,'c'=2,'y'=4] {'x','z','y'}, dimensions={0} | all-to-all | bytes 2097152 | tf_op jit(solution)/shard_map/all_to_all | solution.py:349
  130.3 0.8 finish.6
  131.0 15.3 %all_to_all.45.packed = bf16[64,8,512]{2,1,0:T(8,128)(2,1)S(1)} all-to-all(bf16[64,8,512]{2,1,0:T(8,128)(2,1)S(1)} %get-tuple-element.28), channel_id=1, replica_groups=mesh['x'=4,'z'=4,'c'=2,'y'=4] {'x','z','y'}, dimensions={0} | all-to-all | bytes 1048576 | tf_op jit(solution)/shard_map/all_to_all | solution.py:349
  146.3 7.4 %later_round.3 = f32[64,8,512]{2,1,0:T(8,128)S(1)} custom-call(bf16[64,8,512]{2,1,0:T(8,128)(2,1)S(1)} %all_to_all.45.packed, s32[1,4096]{1,0:T(1,128)S(1)} %get-tuple-element.20.near_ids, bf16[8192,768]{1,0:T(8,128)(2,1)S(1)} %get-tuple-element.27.held, s32[1,4096]{1,0:T(1,128)S(1)} %collective-permute-done.1.far_ids), custom_call_target="tpu_custom_call" | custom-call | tf_op jit(solution)/shard_map/later_round/pallas_call | solution.py:272
  153.6 18.2 %all_to_all.46.parts = f32[64,8,512]{2,1,0:T(8,128)S(1)} all-to-all(f32[64,8,512]{2,1,0:T(8,128)S(1)} %later_round.3), channel_id=1, replica_groups=mesh['x'=4,'z'=4,'c'=2,'y'=4] {'x','z','y'}, dimensions={0} | all-to-all | bytes 2097152 | tf_op jit(solution)/shard_map/all_to_all | solution.py:349
  171.8 1.1 finish.7
  172.9 4.6 %all-to-all-start.7 = ((bf16[64,8,512]{2,1,0:T(8,128)(2,1)}), bf16[64,8,512]{2,1,0:T(8,128)(2,1)S(1)}, u32[]{:S(2)}, u32[]{:S(2)}) async-start(bf16[64,8,512]{2,1,0:T(8,128)(2,1)} %get-tuple-element.29), calls=%async_computation.7 | async-start | bytes 1048576 | tf_op jit(solution)/shard_map/all_to_all | solution.py:349
  177.5 2.2 %collective-permute-start.5 = (f32[8,384]{1,0:T(8,128)S(1)}, f32[8,384]{1,0:T(8,128)S(1)}, u32[]{:S(2)}, u32[]{:S(2)}) collective-permute-start(f32[8,384]{1,0:T(8,128)S(1)} %get-tuple-element.30.mine), channel_id=1, source_target_pairs={{0,3},{1,0},{2,1},{3,2},{4,7},{5,4},{6,5},{7,6},{8,11},{9,8},{10,9... | collective-permute-start | bytes 36872 | tf_op jit(solution)/shard_map/ppermute | solution.py:360
  179.7 0.6 collective-permute-start.4
  180.3 0.6 collective-permute-start.3
  180.8 3.4 %collective-permute-done.4.far = f32[8,384]{1,0:T(8,128)S(1)} collective-permute-done((f32[8,384]{1,0:T(8,128)S(1)}, f32[8,384]{1,0:T(8,128)S(1)}, u32[]{:S(2)}, u32[]{:S(2)}) %collective-permute-start.4) | collective-permute-done | bytes 12320 | tf_op jit(solution)/shard_map/ppermute | solution.py:360
  184.2 0.4 collective-permute-done.3.near
  184.6 3.4 %all-to-all-done.7.packed = bf16[64,8,512]{2,1,0:T(8,128)(2,1)S(1)} async-done(((bf16[64,8,512]{2,1,0:T(8,128)(2,1)}), bf16[64,8,512]{2,1,0:T(8,128)(2,1)S(1)}, u32[]{:S(2)}, u32[]{:S(2)}) %all-to-all-start.7) | async-done | bytes 524320 | tf_op jit(solution)/shard_map/all_to_all | solution.py:349
  188.0 7.1 %assign.1 = (f32[8,4096]{1,0:T(8,128)S(1)}, f32[8,4096]{1,0:T(8,128)S(1)}, f32[2,8,768]{2,1,0:T(8,128)}) custom-call(s32[2]{0:T(128)S(1)} %pad_add_fusion.core.place, bf16[64,8,512]{2,1,0:T(8,128)(2,1)S(1)} %all-to-all-done.7.packed, bf16[4096,768]{1,0:T(8,128)(2,1)} %own.1, s32[1,4096]{1,0:T(1,128)S(1)} %get-tuple-element.20.near_ids, ...), custom_call_target="tpu_custom_call" | custom-call | tf_op jit(solution)/shard_map/assign/pallas_call | solution.py:318
  195.2 8.8 %collective-permute-start.6 = (f32[8,4096]{1,0:T(8,128)S(1)}, f32[8,4096]{1,0:T(8,128)S(1)}, u32[]{:S(2)}, u32[]{:S(2)}) collective-permute-start(f32[8,4096]{1,0:T(8,128)S(1)} %get-tuple-element.32), channel_id=1, source_target_pairs={{0,4},{4,0},{1,5},{5,1},{2,6},{6,2},{3,7},{7,3},{8,12},{12,8},{9,1... | collective-permute-start | bytes 393224 | tf_op jit(solution)/shard_map/ppermute | solution.py:342
  204.0 1.0 collective-permute-done.6
  205.0 0.7 add.7
  (3 shorter events, 0.0 us)
Async XLA Ops:
  0.6 58.3 %collective-permute-start.2 = (bf16[4096,768]{1,0:T(8,128)(2,1)}, bf16[4096,768]{1,0:T(8,128)(2,1)}, u32[]{:S(2)}, u32[]{:S(2)}) collective-permute-start(bf16[4096,768]{1,0:T(8,128)(2,1)} %own.1), channel_id=1, source_target_pairs={{0,4},{4,0},{1,5},{5,1},{2,6},{6,2},{3,7},{7,3},{8,12},{12,8},{9,1... | collective-permute-start | bytes 18874376 | tf_op jit(solution)/shard_map/ppermute | solution.py:342
  9.6 4.0 %collective-permute-start = (f32[64,8,512]{2,1,0:T(8,128)S(1)}, f32[64,8,512]{2,1,0:T(8,128)S(1)}, u32[]{:S(2)}, u32[]{:S(2)}) collective-permute-start(f32[64,8,512]{2,1,0:T(8,128)S(1)} %get-tuple-element.19), channel_id=1, source_target_pairs={{0,4},{4,0},{1,5},{5,1},{2,6},{6,2},{3,7},{7,3},{8,12},{12,8},{9,1... | collective-permute-start | bytes 3145736 | tf_op jit(solution)/shard_map/ppermute | solution.py:342
  9.7 4.1 %collective-permute-start.1 = (s32[1,4096]{1,0:T(1,128)S(1)}, s32[1,4096]{1,0:T(1,128)S(1)}, u32[]{:S(2)}, u32[]{:S(2)}) collective-permute-start(s32[1,4096]{1,0:T(1,128)S(1)} %get-tuple-element.20.near_ids), channel_id=1, source_target_pairs={{0,4},{4,0},{1,5},{5,1},{2,6},{6,2},{3,7},{7,3},{8,12},{12,8},{9,1... | collective-permute-start | bytes 49160 | tf_op jit(solution)/shard_map/ppermute | solution.py:342
  172.9 15.2 %all-to-all-start.7 = ((bf16[64,8,512]{2,1,0:T(8,128)(2,1)}), bf16[64,8,512]{2,1,0:T(8,128)(2,1)S(1)}, u32[]{:S(2)}, u32[]{:S(2)}) async-start(bf16[64,8,512]{2,1,0:T(8,128)(2,1)} %get-tuple-element.29), calls=%async_computation.7 | async-start | bytes 1048576 | tf_op jit(solution)/shard_map/all_to_all | solution.py:349
  177.5 3.3 %collective-permute-start.5 = (f32[8,384]{1,0:T(8,128)S(1)}, f32[8,384]{1,0:T(8,128)S(1)}, u32[]{:S(2)}, u32[]{:S(2)}) collective-permute-start(f32[8,384]{1,0:T(8,128)S(1)} %get-tuple-element.30.mine), channel_id=1, source_target_pairs={{0,3},{1,0},{2,1},{3,2},{4,7},{5,4},{6,5},{7,6},{8,11},{9,8},{10,9... | collective-permute-start | bytes 36872 | tf_op jit(solution)/shard_map/ppermute | solution.py:360
  179.7 4.5 %collective-permute-start.4 = (f32[8,384]{1,0:T(8,128)S(1)}, f32[8,384]{1,0:T(8,128)S(1)}, u32[]{:S(2)}, u32[]{:S(2)}) collective-permute-start(f32[8,384]{1,0:T(8,128)S(1)} %get-tuple-element.30.mine), channel_id=1, source_target_pairs={{0,2},{1,3},{2,0},{3,1},{4,6},{5,7},{6,4},{7,5},{8,10},{9,11},{10,... | collective-permute-start | bytes 36872 | tf_op jit(solution)/shard_map/ppermute | solution.py:360
  180.3 4.4 %collective-permute-start.3 = (f32[8,384]{1,0:T(8,128)S(1)}, f32[8,384]{1,0:T(8,128)S(1)}, u32[]{:S(2)}, u32[]{:S(2)}) collective-permute-start(f32[8,384]{1,0:T(8,128)S(1)} %get-tuple-element.30.mine), channel_id=1, source_target_pairs={{0,1},{1,2},{2,3},{3,0},{4,5},{5,6},{6,7},{7,4},{8,9},{9,10},{10,1... | collective-permute-start | bytes 36872 | tf_op jit(solution)/shard_map/ppermute | solution.py:360
  195.2 9.8 %collective-permute-start.6 = (f32[8,4096]{1,0:T(8,128)S(1)}, f32[8,4096]{1,0:T(8,128)S(1)}, u32[]{:S(2)}, u32[]{:S(2)}) collective-permute-start(f32[8,4096]{1,0:T(8,128)S(1)} %get-tuple-element.32), channel_id=1, source_target_pairs={{0,4},{4,0},{1,5},{5,1},{2,6},{6,2},{3,7},{7,3},{8,12},{12,8},{9,1... | collective-permute-start | bytes 393224 | tf_op jit(solution)/shard_map/ppermute | solution.py:342

commit v5 on v4

--- a/solution.py
+++ b/solution.py
@@ -8,9 +8,9 @@
 K = 8
 D = 768
 ITERS = 3
-HALF_D = D // 2
+HALF = K // 2
 LANES = 128
-CHUNK = HALF_D + LANES
+CHUNK = D + LANES
 OWN_LISTS = 32
 SEATS = 64
 TILE = 512
@@ -30,9 +30,9 @@
 
 def store_sums(out, acc, tot, base):
     for seat in range(SEATS):
-        row, half = base + (seat // 2) * K, seat % 2
-        out[seat, :, :HALF_D] = acc[row : row + K, half * HALF_D : (half + 1) * HALF_D]
-        out[seat, :, HALF_D:] = tot[row : row + K, :]
+        row = base + seat * HALF
+        out[seat, :, :D] = acc[row : row + HALF, :]
+        out[seat, :, D:] = tot[row : row + HALF, :]
 
 
 def relative(names, core):
@@ -96,7 +96,7 @@
 
 
 def seed_sums(core, members, owner, seeds):
-    part = jax.ShapeDtypeStruct((SEATS, K, CHUNK), f32)
+    part = jax.ShapeDtypeStruct((SEATS, HALF, CHUNK), f32)
     rows = members.shape[0]
     return pl.pallas_call(
         seed_kernel,
@@ -125,12 +125,12 @@
     total = parts[0]
     for seat in range(1, SEATS):
         total = total + parts[seat]
-    count = jnp.sum(total[:, HALF_D:], axis=1, keepdims=True)
-    centers = total[:, :HALF_D] / (count + 1.0)
+    count = jnp.sum(total[:, D:], axis=1, keepdims=True)
+    centers = total[:, :D] / (count + 1.0)
     exact[...] = centers
     norm = jnp.sum(centers * centers, axis=1, keepdims=True)
-    lane = lax.broadcasted_iota(jnp.int32, (K, LANES), 1)
-    norms = jnp.broadcast_to(norm, (K, LANES))
+    lane = lax.broadcasted_iota(jnp.int32, (HALF, LANES), 1)
+    norms = jnp.broadcast_to(norm, (HALF, LANES))
     high = norms.astype(bf16).astype(f32)
     middle = (norms - high).astype(bf16).astype(f32)
     low = norms - high - middle
@@ -146,8 +146,8 @@
         in_specs=[IN_VMEM],
         out_specs=[IN_VMEM, IN_VMEM],
         out_shape=[
-            jax.ShapeDtypeStruct((SEATS, K, CHUNK), bf16),
-            jax.ShapeDtypeStruct((K, HALF_D), f32),
+            jax.ShapeDtypeStruct((SEATS, HALF, CHUNK), bf16),
+            jax.ShapeDtypeStruct((HALF, D), f32),
         ],
         compiler_params=pltpu.CompilerParams(vmem_limit_bytes=4 << 20),
         name="finish",
@@ -155,18 +155,12 @@
 
 
 def unpack_centers(packed, cen, nrm):
-    for pair in range(OWN_LISTS // 2):
-        for half in range(2):
-            blocks = [packed[4 * pair + 2 * i + half].astype(f32) for i in range(2)]
-            cen[pair * 16 : pair * 16 + 16, half * HALF_D : (half + 1) * HALF_D] = jnp.concatenate(
-                [b[:, :HALF_D] for b in blocks], axis=0
-            ).astype(bf16)
-        for i in range(2):
-            name = 2 * pair + i
-            tails = packed[2 * name][:, HALF_D:].astype(f32) + packed[2 * name + 1][:, HALF_D:].astype(f32)
-            nrm[name * K : (name + 1) * K, :] = jnp.broadcast_to(
-                jnp.sum(tails, axis=1, keepdims=True), (K, LANES)
-            )
+    for group in range(OWN_LISTS // 2):
+        blocks = [packed[4 * group + part].astype(f32) for part in range(4)]
+        rows = slice(group * 2 * K, (group + 1) * 2 * K)
+        cen[rows, :] = jnp.concatenate([b[:, :D] for b in blocks], axis=0).astype(bf16)
+        tails = jnp.concatenate([b[:, D:] for b in blocks], axis=0)
+        nrm[rows, :] = jnp.broadcast_to(jnp.sum(tails, axis=1, keepdims=True), (2 * K, LANES))
 
 
 def dots_of(tile, cen, members):
@@ -260,7 +254,7 @@
         first_kernel,
         in_specs=[IN_VMEM, IN_VMEM, IN_PLACE, IN_VMEM, IN_VMEM],
         out_specs=[IN_VMEM, IN_VMEM],
-        out_shape=[jax.ShapeDtypeStruct((SEATS, K, CHUNK), f32), pltpu.VMEM((2 * rows, D), bf16)],
+        out_shape=[jax.ShapeDtypeStruct((SEATS, HALF, CHUNK), f32), pltpu.VMEM((2 * rows, D), bf16)],
         input_output_aliases={4: 1},
         scratch_shapes=round_scratch(rows) + [pltpu.SemaphoreType.DMA((COPIES,))],
         compiler_params=pltpu.CompilerParams(vmem_limit_bytes=24 << 20),
@@ -273,7 +267,7 @@
         later_kernel,
         in_specs=[IN_VMEM] * 4,
         out_specs=IN_VMEM,
-        out_shape=jax.ShapeDtypeStruct((SEATS, K, CHUNK), f32),
+        out_shape=jax.ShapeDtypeStruct((SEATS, HALF, CHUNK), f32),
         scratch_shapes=round_scratch(held.shape[0] // 2),
         compiler_params=pltpu.CompilerParams(vmem_limit_bytes=24 << 20),
         name="later_round",
@@ -289,7 +283,7 @@
     for shift, block in enumerate((mine, near, far, wide)):
         blocks[shift] = block[...]
     for seat in range(4):
-        held[seat // 2, :, seat % 2 * HALF_D : (seat % 2 + 1) * HALF_D] = blocks[(place[1] - seat) & 3]
+        held[seat // 2, seat % 2 * HALF : (seat % 2 + 1) * HALF, :] = blocks[(place[1] - seat) & 3]
     half = own.shape[0] // TILE
     group = half // COPIES
 
@@ -324,7 +318,7 @@
             pltpu.VMEM((OWN_LISTS * K, D), bf16),
             pltpu.VMEM((OWN_LISTS * K, LANES), f32),
             pltpu.VMEM((rows // TILE // COPIES, OWN_LISTS * K, TILE), f32),
-            pltpu.VMEM((4, K, HALF_D), f32),
+            pltpu.VMEM((4, HALF, D), f32),
             pltpu.VMEM((2 * rows, D), bf16),
             pltpu.SemaphoreType.DMA((2 * COPIES,)),
         ],

time: 206 us -> 199 us (0.966)
  blocking collectives: 134 us -> 125 us
    all_to_all x7, blocking collectives: 134 us -> 125 us  [exchange(): lax.all_to_all(parts, SEAT_AXES, split_axis=0, concat_axis=0, tiled=True)]
where the time goes in v5:
time: 199 us; the launch traced here: 198 us
  blocking collectives  125 us (63%)
  Pallas kernels  40.2 us (20%)
  starting transfers between devices  20.6 us (10%)
  waiting for transfers between devices  11 us (6%)
    all_to_all x7, blocking collectives, exchange(): lax.all_to_all(parts, SEAT_AXES, split_axis=0, concat_axis=0, tiled=True)  125 us
    pallas_call x2, Pallas kernels, later_round(): pl.pallas_call(later_kernel, in_specs=[IN_VMEM] * 4, out_specs=IN_VMEM, o...  14.8 us
    ppermute x4, starting transfers between devices, local(): swap = lambda value: lax.ppermute(value, 'c', SWAP)  12.6 us
    pallas_call x1, Pallas kernels, seed_sums(): pl.pallas_call(seed_kernel, in_specs=[IN_SMEM, IN_PLACE, IN_PLACE, IN_PLA...  7.48 us
    pallas_call x1, Pallas kernels, first_round(): pl.pallas_call(first_kernel, in_specs=[IN_VMEM, IN_VMEM, IN_PLACE, IN_VME...  7.46 us
    pallas_call x1, Pallas kernels, assign(): pl.pallas_call(assign_kernel, in_specs=[IN_SMEM, IN_VMEM, IN_PLACE, IN_VM...  7.13 us
    all_to_all x1, starting transfers between devices, exchange(): lax.all_to_all(parts, SEAT_AXES, split_axis=0, concat_axis=0, tiled=True)  4.63 us
    ppermute x4, waiting for transfers between devices, local(): swap = lambda value: lax.ppermute(value, 'c', SWAP)  4.15 us
  transfers between devices with their start and end apart: 8, of which 5 were waited for; matrix products, arithmetic and copies ran while one was open for 0% of the time, Pallas kernels for 4%

profile of v5, /device:TPU:1, one launch (start us, length us, event | category | flops | bytes accessed | tf_op | source)
XLA Modules:
  0.0 198.1 jit_solution(3302951363413366986)
XLA Ops:
  0.6 1.5 collective-permute-start.2
  2.1 0.1 pad_add_fusion.core.place
  2.2 7.5 %seed_sums.1 = (f32[64,4,896]{2,1,0:T(4,128)S(1)}, f32[64,4,896]{2,1,0:T(4,128)S(1)}, s32[1,4096]{1,0:T(1,128)S(1)}, bf16[8192,768]{1,0:T(8,128)(2,1)S(1)}) custom-call(s32[2]{0:T(128)S(1)} %pad_add_fusion.core.place, bf16[4096,768]{1,0:T(8,128)(2,1)} %own.1, s32[1,4096]{1,0:T(1,128)} %bitcast.4, s32[1,4096]{1,0:T(1,128)} %bitcast.5), custom_call_target="tpu_custom_call" | custom-call | tf_op jit(solution)/shard_map/seed_sums/pallas_call | solution.py:101
  9.6 0.1 collective-permute-start
  9.7 0.5 collective-permute-start.1
  10.2 3.2 %collective-permute-done = f32[64,4,896]{2,1,0:T(4,128)S(1)} collective-permute-done((f32[64,4,896]{2,1,0:T(4,128)S(1)}, f32[64,4,896]{2,1,0:T(4,128)S(1)}, u32[]{:S(2)}, u32[]{:S(2)}) %collective-permute-start) | collective-permute-done | bytes 917536 | tf_op jit(solution)/shard_map/ppermute | solution.py:336
  13.4 0.2 add.6
  13.6 27.0 %all_to_all.40.parts = f32[64,4,896]{2,1,0:T(4,128)S(1)} all-to-all(f32[64,4,896]{2,1,0:T(4,128)S(1)} %add.6), channel_id=1, replica_groups=mesh['x'=4,'z'=4,'c'=2,'y'=4] {'x','z','y'}, dimensions={0} | all-to-all | bytes 1835008 | tf_op jit(solution)/shard_map/all_to_all | solution.py:343
  40.6 0.8 finish.4
  41.4 15.2 %all_to_all.41.packed = bf16[64,4,896]{2,1,0:T(4,128)(2,1)S(1)} all-to-all(bf16[64,4,896]{2,1,0:T(4,128)(2,1)S(1)} %get-tuple-element.22), channel_id=1, replica_groups=mesh['x'=4,'z'=4,'c'=2,'y'=4] {'x','z','y'}, dimensions={0} | all-to-all | bytes 917504 | tf_op jit(solution)/shard_map/all_to_all | solution.py:343
  56.5 7.5 %first_round.1 = (f32[64,4,896]{2,1,0:T(4,128)S(1)}, bf16[8192,768]{1,0:T(8,128)(2,1)S(1)}) custom-call(bf16[64,4,896]{2,1,0:T(4,128)(2,1)S(1)} %all_to_all.41.packed, s32[1,4096]{1,0:T(1,128)S(1)} %get-tuple-element.20.near_ids, bf16[4096,768]{1,0:T(8,128)(2,1)} %collective-permute-done.2.other, ...), custom_call_target="tpu_custom_call", output_to_operand_aliasing={{1}: (4, {})} | custom-call | tf_op jit(solution)/shard_map/first_round/pallas_call | solution.py:253
  64.0 18.9 %all_to_all.42.parts = f32[64,4,896]{2,1,0:T(4,128)S(1)} all-to-all(f32[64,4,896]{2,1,0:T(4,128)S(1)} %get-tuple-element.25), channel_id=1, replica_groups=mesh['x'=4,'z'=4,'c'=2,'y'=4] {'x','z','y'}, dimensions={0} | all-to-all | bytes 1835008 | tf_op jit(solution)/shard_map/all_to_all | solution.py:343
  82.9 0.8 finish.5
  83.6 14.7 %all_to_all.43.packed = bf16[64,4,896]{2,1,0:T(4,128)(2,1)S(1)} all-to-all(bf16[64,4,896]{2,1,0:T(4,128)(2,1)S(1)} %get-tuple-element.26), channel_id=1, replica_groups=mesh['x'=4,'z'=4,'c'=2,'y'=4] {'x','z','y'}, dimensions={0} | all-to-all | bytes 917504 | tf_op jit(solution)/shard_map/all_to_all | solution.py:343
  98.3 7.4 %later_round.2 = f32[64,4,896]{2,1,0:T(4,128)S(1)} custom-call(bf16[64,4,896]{2,1,0:T(4,128)(2,1)S(1)} %all_to_all.43.packed, s32[1,4096]{1,0:T(1,128)S(1)} %get-tuple-element.20.near_ids, bf16[8192,768]{1,0:T(8,128)(2,1)S(1)} %get-tuple-element.27.held, s32[1,4096]{1,0:T(1,128)S(1)} %collective-permute-done.1.far_ids), custom_call_target="tpu_custom_call" | custom-call | tf_op jit(solution)/shard_map/later_round/pallas_call | solution.py:266
  105.8 17.9 %all_to_all.44.parts = f32[64,4,896]{2,1,0:T(4,128)S(1)} all-to-all(f32[64,4,896]{2,1,0:T(4,128)S(1)} %later_round.2), channel_id=1, replica_groups=mesh['x'=4,'z'=4,'c'=2,'y'=4] {'x','z','y'}, dimensions={0} | all-to-all | bytes 1835008 | tf_op jit(solution)/shard_map/all_to_all | solution.py:343
  123.6 0.8 finish.6
  124.4 14.0 %all_to_all.45.packed = bf16[64,4,896]{2,1,0:T(4,128)(2,1)S(1)} all-to-all(bf16[64,4,896]{2,1,0:T(4,128)(2,1)S(1)} %get-tuple-element.28), channel_id=1, replica_groups=mesh['x'=4,'z'=4,'c'=2,'y'=4] {'x','z','y'}, dimensions={0} | all-to-all | bytes 917504 | tf_op jit(solution)/shard_map/all_to_all | solution.py:343
  138.4 7.4 %later_round.3 = f32[64,4,896]{2,1,0:T(4,128)S(1)} custom-call(bf16[64,4,896]{2,1,0:T(4,128)(2,1)S(1)} %all_to_all.45.packed, s32[1,4096]{1,0:T(1,128)S(1)} %get-tuple-element.20.near_ids, bf16[8192,768]{1,0:T(8,128)(2,1)S(1)} %get-tuple-element.27.held, s32[1,4096]{1,0:T(1,128)S(1)} %collective-permute-done.1.far_ids), custom_call_target="tpu_custom_call" | custom-call | tf_op jit(solution)/shard_map/later_round/pallas_call | solution.py:266
  145.9 17.0 %all_to_all.46.parts = f32[64,4,896]{2,1,0:T(4,128)S(1)} all-to-all(f32[64,4,896]{2,1,0:T(4,128)S(1)} %later_round.3), channel_id=1, replica_groups=mesh['x'=4,'z'=4,'c'=2,'y'=4] {'x','z','y'}, dimensions={0} | all-to-all | bytes 1835008 | tf_op jit(solution)/shard_map/all_to_all | solution.py:343
  162.9 1.0 finish.7
  163.9 4.6 %all-to-all-start.7 = ((bf16[64,4,896]{2,1,0:T(4,128)(2,1)}), bf16[64,4,896]{2,1,0:T(4,128)(2,1)S(1)}, u32[]{:S(2)}, u32[]{:S(2)}) async-start(bf16[64,4,896]{2,1,0:T(4,128)(2,1)} %get-tuple-element.29), calls=%async_computation.7 | async-start | bytes 917504 | tf_op jit(solution)/shard_map/all_to_all | solution.py:343
  168.5 2.2 %collective-permute-start.5 = (f32[4,768]{1,0:T(4,128)S(1)}, f32[4,768]{1,0:T(4,128)S(1)}, u32[]{:S(2)}, u32[]{:S(2)}) collective-permute-start(f32[4,768]{1,0:T(4,128)S(1)} %get-tuple-element.30.mine), channel_id=1, source_target_pairs={{0,3},{1,0},{2,1},{3,2},{4,7},{5,4},{6,5},{7,6},{8,11},{9,8},{10,9... | collective-permute-start | bytes 36872 | tf_op jit(solution)/shard_map/ppermute | solution.py:354
  170.7 0.6 collective-permute-start.4
  171.3 0.6 collective-permute-start.3
  171.9 3.3 %collective-permute-done.4.far = f32[4,768]{1,0:T(4,128)S(1)} collective-permute-done((f32[4,768]{1,0:T(4,128)S(1)}, f32[4,768]{1,0:T(4,128)S(1)}, u32[]{:S(2)}, u32[]{:S(2)}) %collective-permute-start.4) | collective-permute-done | bytes 12320 | tf_op jit(solution)/shard_map/ppermute | solution.py:354
  175.2 0.3 collective-permute-done.3.near
  175.5 3.3 %all-to-all-done.7.packed = bf16[64,4,896]{2,1,0:T(4,128)(2,1)S(1)} async-done(((bf16[64,4,896]{2,1,0:T(4,128)(2,1)}), bf16[64,4,896]{2,1,0:T(4,128)(2,1)S(1)}, u32[]{:S(2)}, u32[]{:S(2)}) %all-to-all-start.7) | async-done | bytes 458784 | tf_op jit(solution)/shard_map/all_to_all | solution.py:343
  178.8 7.1 %assign.1 = (f32[8,4096]{1,0:T(8,128)S(1)}, f32[8,4096]{1,0:T(8,128)S(1)}, f32[2,8,768]{2,1,0:T(8,128)}) custom-call(s32[2]{0:T(128)S(1)} %pad_add_fusion.core.place, bf16[64,4,896]{2,1,0:T(4,128)(2,1)S(1)} %all-to-all-done.7.packed, bf16[4096,768]{1,0:T(8,128)(2,1)} %own.1, s32[1,4096]{1,0:T(1,128)S(1)} %get-tuple-element.20.near_ids, ...), custom_call_target="tpu_custom_call" | custom-call | tf_op jit(solution)/shard_map/assign/pallas_call | solution.py:312
  185.9 10.5 %collective-permute-start.6 = (f32[8,4096]{1,0:T(8,128)S(1)}, f32[8,4096]{1,0:T(8,128)S(1)}, u32[]{:S(2)}, u32[]{:S(2)}) collective-permute-start(f32[8,4096]{1,0:T(8,128)S(1)} %get-tuple-element.32), channel_id=1, source_target_pairs={{0,4},{4,0},{1,5},{5,1},{2,6},{6,2},{3,7},{7,3},{8,12},{12,8},{9,1... | collective-permute-start | bytes 393224 | tf_op jit(solution)/shard_map/ppermute | solution.py:336
  196.5 1.0 collective-permute-done.6
  197.4 0.7 add.7
  (3 shorter events, 0.0 us)
Async XLA Ops:
  0.6 55.9 %collective-permute-start.2 = (bf16[4096,768]{1,0:T(8,128)(2,1)}, bf16[4096,768]{1,0:T(8,128)(2,1)}, u32[]{:S(2)}, u32[]{:S(2)}) collective-permute-start(bf16[4096,768]{1,0:T(8,128)(2,1)} %own.1), channel_id=1, source_target_pairs={{0,4},{4,0},{1,5},{5,1},{2,6},{6,2},{3,7},{7,3},{8,12},{12,8},{9,1... | collective-permute-start | bytes 18874376 | tf_op jit(solution)/shard_map/ppermute | solution.py:336
  9.6 3.7 %collective-permute-start = (f32[64,4,896]{2,1,0:T(4,128)S(1)}, f32[64,4,896]{2,1,0:T(4,128)S(1)}, u32[]{:S(2)}, u32[]{:S(2)}) collective-permute-start(f32[64,4,896]{2,1,0:T(4,128)S(1)} %get-tuple-element.19), channel_id=1, source_target_pairs={{0,4},{4,0},{1,5},{5,1},{2,6},{6,2},{3,7},{7,3},{8,12},{12,8},{9,1... | collective-permute-start | bytes 2752520 | tf_op jit(solution)/shard_map/ppermute | solution.py:336
  9.7 3.9 %collective-permute-start.1 = (s32[1,4096]{1,0:T(1,128)S(1)}, s32[1,4096]{1,0:T(1,128)S(1)}, u32[]{:S(2)}, u32[]{:S(2)}) collective-permute-start(s32[1,4096]{1,0:T(1,128)S(1)} %get-tuple-element.20.near_ids), channel_id=1, source_target_pairs={{0,4},{4,0},{1,5},{5,1},{2,6},{6,2},{3,7},{7,3},{8,12},{12,8},{9,1... | collective-permute-start | bytes 49160 | tf_op jit(solution)/shard_map/ppermute | solution.py:336
  163.9 14.9 %all-to-all-start.7 = ((bf16[64,4,896]{2,1,0:T(4,128)(2,1)}), bf16[64,4,896]{2,1,0:T(4,128)(2,1)S(1)}, u32[]{:S(2)}, u32[]{:S(2)}) async-start(bf16[64,4,896]{2,1,0:T(4,128)(2,1)} %get-tuple-element.29), calls=%async_computation.7 | async-start | bytes 917504 | tf_op jit(solution)/shard_map/all_to_all | solution.py:343
  168.5 3.4 %collective-permute-start.5 = (f32[4,768]{1,0:T(4,128)S(1)}, f32[4,768]{1,0:T(4,128)S(1)}, u32[]{:S(2)}, u32[]{:S(2)}) collective-permute-start(f32[4,768]{1,0:T(4,128)S(1)} %get-tuple-element.30.mine), channel_id=1, source_target_pairs={{0,3},{1,0},{2,1},{3,2},{4,7},{5,4},{6,5},{7,6},{8,11},{9,8},{10,9... | collective-permute-start | bytes 36872 | tf_op jit(solution)/shard_map/ppermute | solution.py:354
  170.7 4.4 %collective-permute-start.4 = (f32[4,768]{1,0:T(4,128)S(1)}, f32[4,768]{1,0:T(4,128)S(1)}, u32[]{:S(2)}, u32[]{:S(2)}) collective-permute-start(f32[4,768]{1,0:T(4,128)S(1)} %get-tuple-element.30.mine), channel_id=1, source_target_pairs={{0,2},{1,3},{2,0},{3,1},{4,6},{5,7},{6,4},{7,5},{8,10},{9,11},{10,... | collective-permute-start | bytes 36872 | tf_op jit(solution)/shard_map/ppermute | solution.py:354
  171.3 4.2 %collective-permute-start.3 = (f32[4,768]{1,0:T(4,128)S(1)}, f32[4,768]{1,0:T(4,128)S(1)}, u32[]{:S(2)}, u32[]{:S(2)}) collective-permute-start(f32[4,768]{1,0:T(4,128)S(1)} %get-tuple-element.30.mine), channel_id=1, source_target_pairs={{0,1},{1,2},{2,3},{3,0},{4,5},{5,6},{6,7},{7,4},{8,9},{9,10},{10,1... | collective-permute-start | bytes 36872 | tf_op jit(solution)/shard_map/ppermute | solution.py:354
  185.9 11.5 %collective-permute-start.6 = (f32[8,4096]{1,0:T(8,128)S(1)}, f32[8,4096]{1,0:T(8,128)S(1)}, u32[]{:S(2)}, u32[]{:S(2)}) collective-permute-start(f32[8,4096]{1,0:T(8,128)S(1)} %get-tuple-element.32), channel_id=1, source_target_pairs={{0,4},{4,0},{1,5},{5,1},{2,6},{6,2},{3,7},{7,3},{8,12},{12,8},{9,1... | collective-permute-start | bytes 393224 | tf_op jit(solution)/shard_map/ppermute | solution.py:336

commit v6 on v5

--- a/solution.py
+++ b/solution.py
@@ -58,7 +58,20 @@
     return pl.ds(pl.multiple_of(tile * TILE, TILE), TILE)
 
 
-def seed_kernel(core, members, owner, seeds, mine, theirs, ids, held, acc, tot, code, buf, sems, pair):
+def add_seeds(code, held, acc, tot, base, tile):
+    spot = at_tile(tile)
+    groups = lax.broadcasted_iota(jnp.int32, (K, TILE), 0)
+    shifted = jnp.broadcast_to(code[:, spot], (K, TILE)) - groups
+    rows = []
+    for name in range(OWN_LISTS):
+        hot = jnp.where(shifted == base + name * K, 1.0, 0.0).astype(f32)
+        tot[name * K : (name + 1) * K, :] += lane_fold(hot)
+        rows.append(hot)
+    hots = jnp.concatenate(rows, axis=0).astype(bf16)
+    acc[...] += jnp.dot(hots, held[spot, :], preferred_element_type=f32)
+
+
+def seed_away_kernel(core, members, owner, seeds, theirs, ids, code, held, acc, tot, buf, sems, pair):
     start_copies([members], held, sems, SEED_COPIES)
     pltpu.make_async_copy(owner, ids, pair.at[0]).start()
     pltpu.make_async_copy(seeds, buf, pair.at[1]).start()
@@ -68,26 +81,24 @@
     pltpu.make_async_copy(seeds, buf, pair.at[1]).wait()
     ids[...] = relative(ids[...], core[0])
     code[...] = ids[...] * K + buf[...]
-    groups = lax.broadcasted_iota(jnp.int32, (K, TILE), 0)
     unroll = members.shape[0] // TILE // SEED_COPIES
 
     def work(turn, carry):
         wait_copy(members, held, sems, SEED_COPIES, turn)
         for part in range(unroll):
-            spot = at_tile(turn * unroll + part)
-            shifted = jnp.broadcast_to(code[:, spot], (K, TILE)) - groups
-            rows = []
-            for name in range(2 * OWN_LISTS):
-                hot = jnp.where(shifted == name * K, 1.0, 0.0).astype(f32)
-                tot[name * K : (name + 1) * K, :] += lane_fold(hot)
-                rows.append(hot)
-            hots = jnp.concatenate(rows, axis=0).astype(bf16)
-            acc[...] += jnp.dot(hots, held[spot, :], preferred_element_type=f32)
+            add_seeds(code, held, acc, tot, OWN_LISTS * K, turn * unroll + part)
         return carry
 
     lax.fori_loop(0, SEED_COPIES, work, 0)
+    store_sums(theirs, acc, tot, 0)
+
+
+def seed_own_kernel(code, held, mine, acc, tot):
+    acc[...] = jnp.zeros_like(acc)
+    tot[...] = jnp.zeros_like(tot)
+    for tile in range(code.shape[1] // TILE):
+        add_seeds(code, held, acc, tot, 0, tile)
     store_sums(mine, acc, tot, 0)
-    store_sums(theirs, acc, tot, OWN_LISTS * K)
 
 
 IN_VMEM = pl.BlockSpec(memory_space=pltpu.VMEM)
@@ -95,30 +106,40 @@
 IN_PLACE = pl.BlockSpec(memory_space=pltpu.HBM)
 
 
-def seed_sums(core, members, owner, seeds):
-    part = jax.ShapeDtypeStruct((SEATS, HALF, CHUNK), f32)
+PART = jax.ShapeDtypeStruct((SEATS, HALF, CHUNK), f32)
+SUM_SCRATCH = [pltpu.VMEM((OWN_LISTS * K, D), f32), pltpu.VMEM((OWN_LISTS * K, LANES), f32)]
+ROOM = pltpu.CompilerParams(vmem_limit_bytes=24 << 20)
+
+
+def seed_away(core, members, owner, seeds):
     rows = members.shape[0]
-    return pl.pallas_call(
-        seed_kernel,
+    names = jax.ShapeDtypeStruct((1, rows), jnp.int32)
+    return pl.pallas_call(
+        seed_away_kernel,
         in_specs=[IN_SMEM, IN_PLACE, IN_PLACE, IN_PLACE],
         out_specs=[IN_VMEM] * 4,
-        out_shape=[
-            part,
-            part,
-            jax.ShapeDtypeStruct((1, rows), jnp.int32),
-            pltpu.VMEM((2 * rows, D), bf16),
-        ],
-        scratch_shapes=[
-            pltpu.VMEM((2 * OWN_LISTS * K, D), f32),
-            pltpu.VMEM((2 * OWN_LISTS * K, LANES), f32),
-            pltpu.VMEM((1, rows), jnp.int32),
+        out_shape=[PART, names, names, pltpu.VMEM((2 * rows, D), bf16)],
+        scratch_shapes=SUM_SCRATCH
+        + [
             pltpu.VMEM((1, rows), jnp.int32),
             pltpu.SemaphoreType.DMA((SEED_COPIES,)),
             pltpu.SemaphoreType.DMA((2,)),
         ],
-        compiler_params=pltpu.CompilerParams(vmem_limit_bytes=24 << 20),
-        name="seed_sums",
+        compiler_params=ROOM,
+        name="seed_away",
     )(core, members, owner, seeds)
+
+
+def seed_own(code, held):
+    return pl.pallas_call(
+        seed_own_kernel,
+        in_specs=[IN_VMEM, IN_VMEM],
+        out_specs=IN_VMEM,
+        out_shape=PART,
+        scratch_shapes=SUM_SCRATCH,
+        compiler_params=ROOM,
+        name="seed_own",
+    )(code, held)
 
 
 def finish_kernel(parts, out, exact):
@@ -274,57 +295,74 @@
     )(packed, near_ids, held, far_ids)
 
 
-def assign_kernel(
-    place, packed, own, near_ids, other, far_ids, mine, near, far, wide,
-    kept, given, held, cen, nrm, dots, blocks, buf, sems,
+def assign_members(packed, members, ids, out, cen, nrm, dots, buf, sems, side):
+    start_copies([members], buf, sems, COPIES)
+    unpack_centers(packed, cen, nrm)
+    group = members.shape[0] // TILE // COPIES
+
+    def work(turn, carry):
+        wait_copy(members, buf, sems, COPIES, turn)
+        for part in range(group):
+            dots[part] = dots_of(turn * group + part, cen, buf)
+        for part in range(group):
+            spot = at_tile(turn * group + part)
+            names = jnp.broadcast_to(ids[:, spot], (K, TILE))
+            weights = soft_weights(dots, part, nrm, names, side * OWN_LISTS)
+            there = (names < OWN_LISTS) if side == 0 else (names >= OWN_LISTS)
+            out[:, spot] = jnp.where(there, weights, 0.0)
+        return carry
+
+    lax.fori_loop(0, COPIES, work, 0)
+
+
+def assign_away_kernel(
+    place, packed, members, ids, mine, near, far, wide, out, held, blocks, *scratch
 ):
-    start_copies([own, other], buf, sems, COPIES)
-    unpack_centers(packed, cen, nrm)
     for shift, block in enumerate((mine, near, far, wide)):
         blocks[shift] = block[...]
     for seat in range(4):
         held[seat // 2, seat % 2 * HALF : (seat % 2 + 1) * HALF, :] = blocks[(place[1] - seat) & 3]
-    half = own.shape[0] // TILE
-    group = half // COPIES
-
-    def work_on(out, ids, side):
-        def work(turn, carry):
-            wait_copy(own, buf, sems, COPIES, side * COPIES + turn)
-            for part in range(group):
-                dots[part] = dots_of(side * half + turn * group + part, cen, buf)
-            for part in range(group):
-                spot = at_tile(turn * group + part)
-                names = jnp.broadcast_to(ids[:, spot], (K, TILE))
-                weights = soft_weights(dots, part, nrm, names, side * OWN_LISTS)
-                there = (names < OWN_LISTS) if side == 0 else (names >= OWN_LISTS)
-                out[:, spot] = jnp.where(there, weights, 0.0)
-            return carry
-
-        lax.fori_loop(0, COPIES, work, 0)
-
-    work_on(kept, near_ids, 0)
-    work_on(given, far_ids, 1)
-
-
-def assign(place, packed, own, near_ids, other, far_ids, *blocks):
-    rows = own.shape[0]
-    part = jax.ShapeDtypeStruct((K, rows), f32)
-    return pl.pallas_call(
-        assign_kernel,
-        in_specs=[IN_SMEM, IN_VMEM, IN_PLACE, IN_VMEM, IN_PLACE, IN_VMEM] + [IN_VMEM] * 4,
-        out_specs=[IN_VMEM, IN_VMEM, IN_VMEM],
-        out_shape=[part, part, jax.ShapeDtypeStruct((2, K, D), f32)],
-        scratch_shapes=[
-            pltpu.VMEM((OWN_LISTS * K, D), bf16),
-            pltpu.VMEM((OWN_LISTS * K, LANES), f32),
-            pltpu.VMEM((rows // TILE // COPIES, OWN_LISTS * K, TILE), f32),
-            pltpu.VMEM((4, HALF, D), f32),
-            pltpu.VMEM((2 * rows, D), bf16),
-            pltpu.SemaphoreType.DMA((2 * COPIES,)),
-        ],
-        compiler_params=pltpu.CompilerParams(vmem_limit_bytes=24 << 20),
-        name="assign",
-    )(place, packed, own, near_ids, other, far_ids, *blocks)
+    assign_members(packed, members, ids, out, *scratch, 1)
+
+
+def assign_own_kernel(packed, members, ids, out, *scratch):
+    assign_members(packed, members, ids, out, *scratch, 0)
+
+
+def assign_scratch(rows):
+    return [
+        pltpu.VMEM((OWN_LISTS * K, D), bf16),
+        pltpu.VMEM((OWN_LISTS * K, LANES), f32),
+        pltpu.VMEM((rows // TILE // COPIES, OWN_LISTS * K, TILE), f32),
+        pltpu.VMEM((rows, D), bf16),
+        pltpu.SemaphoreType.DMA((COPIES,)),
+    ]
+
+
+def assign_away(place, packed, members, ids, *blocks):
+    rows = members.shape[0]
+    return pl.pallas_call(
+        assign_away_kernel,
+        in_specs=[IN_SMEM, IN_VMEM, IN_PLACE, IN_VMEM] + [IN_VMEM] * 4,
+        out_specs=[IN_VMEM, IN_VMEM],
+        out_shape=[jax.ShapeDtypeStruct((K, rows), f32), jax.ShapeDtypeStruct((2, K, D), f32)],
+        scratch_shapes=[pltpu.VMEM((4, HALF, D), f32)] + assign_scratch(rows),
+        compiler_params=ROOM,
+        name="assign_away",
+    )(place, packed, members, ids, *blocks)
+
+
+def assign_own(packed, members, ids):
+    rows = members.shape[0]
+    return pl.pallas_call(
+        assign_own_kernel,
+        in_specs=[IN_VMEM, IN_PLACE, IN_VMEM],
+        out_specs=IN_VMEM,
+        out_shape=jax.ShapeDtypeStruct((K, rows), f32),
+        scratch_shapes=assign_scratch(rows),
+        compiler_params=ROOM,
+        name="assign_own",
+    )(packed, members, ids)
 
 
 SWAP = [(0, 1), (1, 0)]
@@ -342,8 +380,8 @@
     def exchange(parts):
         return lax.all_to_all(parts, SEAT_AXES, split_axis=0, concat_axis=0, tiled=True)
 
-    mine, theirs, near_ids, held = seed_sums(place, members, owner, seeds)
-    parts, far_ids = lax.optimization_barrier((mine + swap(theirs), swap(near_ids)))
+    theirs, near_ids, code, held = seed_away(place, members, owner, seeds)
+    parts, far_ids = lax.optimization_barrier((seed_own(code, held) + swap(theirs), swap(near_ids)))
     packed = exchange(finish(exchange(parts))[0])
     parts, held = first_round(packed, near_ids, other, far_ids, held)
     for turn in range(ITERS - 1):
@@ -353,7 +391,9 @@
     blocks = [exact] + [
         lax.ppermute(exact, "y", [(seat, (seat + shift) % 4) for seat in range(4)]) for shift in (1, 2, 3)
     ]
-    kept, given, centers = assign(place, exchange(packed), members, near_ids, other, far_ids, *blocks)
+    packed = exchange(packed)
+    given, centers = assign_away(place, packed, other, far_ids, *blocks)
+    kept = assign_own(packed, members, near_ids)
     return kept + swap(given), centers
 
 

time: 199 us -> 199 us (level)
    pallas_call x2 -> x4, Pallas kernels: 14.6 us -> 16.3 us  [the longest x1 5.78 us: seed_away(): pl.pallas_call(seed_away_kernel, in_specs=[IN_SMEM, IN_PLACE, IN_PLACE, I...]
  transfers between devices with their start and end apart: 8 -> 8, of which waited for: 5 -> 4; matrix products, arithmetic and copies ran while one was open for 0% -> 0% of each run, Pallas kernels for 4% -> 6%
where the time goes in v6:
time: 199 us
  blocking collectives  125 us (63%)
  Pallas kernels  41.9 us (21%)
  starting transfers between devices  20.6 us (10%)
  waiting for transfers between devices  9.79 us (5%)
    all_to_all x7, blocking collectives, exchange(): lax.all_to_all(parts, SEAT_AXES, split_axis=0, concat_axis=0, tiled=True)  125 us
    pallas_call x2, Pallas kernels, later_round(): pl.pallas_call(later_kernel, in_specs=[IN_VMEM] * 4, out_specs=IN_VMEM, o...  14.8 us
    ppermute x4, starting transfers between devices, local(): swap = lambda value: lax.ppermute(value, 'c', SWAP)  12.6 us
    pallas_call x1, Pallas kernels, first_round(): pl.pallas_call(first_kernel, in_specs=[IN_VMEM, IN_VMEM, IN_PLACE, IN_VME...  7.46 us
    pallas_call x1, Pallas kernels, seed_away(): pl.pallas_call(seed_away_kernel, in_specs=[IN_SMEM, IN_PLACE, IN_PLACE, I...  5.78 us
    all_to_all x1, starting transfers between devices, exchange(): lax.all_to_all(parts, SEAT_AXES, split_axis=0, concat_axis=0, tiled=True)  4.63 us
    pallas_call x1, Pallas kernels, assign_away(): pl.pallas_call(assign_away_kernel, in_specs=[IN_SMEM, IN_VMEM, IN_PLACE,...  4.58 us
    pallas_call x1, Pallas kernels, assign_own(): pl.pallas_call(assign_own_kernel, in_specs=[IN_VMEM, IN_PLACE, IN_VMEM],...  4 us
  transfers between devices with their start and end apart: 8, of which 4 were waited for; matrix products, arithmetic and copies ran while one was open for 0% of the time, Pallas kernels for 6%

profile of v6, /device:TPU:1, one launch (start us, length us, event | category | flops | bytes accessed | tf_op | source)
XLA Modules:
  0.0 198.6 jit_solution(15183262978359042715)
XLA Ops:
  0.6 1.5 collective-permute-start.2
  2.2 5.8 %seed_away.1 = (f32[64,4,896]{2,1,0:T(4,128)S(1)}, s32[1,4096]{1,0:T(1,128)S(1)}, s32[1,4096]{1,0:T(1,128)S(1)}, bf16[8192,768]{1,0:T(8,128)(2,1)S(1)}) custom-call(s32[2]{0:T(128)S(1)} %pad_add_fusion.core.place, bf16[4096,768]{1,0:T(8,128)(2,1)} %members.3, s32[1,4096]{1,0:T(1,128)} %bitcast.4, s32[1,4096]{1,0:T(1,128)} %bitcast.5), custom_call_target="tpu_custom_call" | custom-call | tf_op jit(solution)/shard_map/seed_away/pallas_call | solution.py:117
  8.0 0.1 collective-permute-start
  8.1 0.5 collective-permute-start.1
  8.5 2.0 seed_own.1
  10.5 2.9 %collective-permute-done = f32[64,4,896]{2,1,0:T(4,128)S(1)} collective-permute-done((f32[64,4,896]{2,1,0:T(4,128)S(1)}, f32[64,4,896]{2,1,0:T(4,128)S(1)}, u32[]{:S(2)}, u32[]{:S(2)}) %collective-permute-start) | collective-permute-done | bytes 917536 | tf_op jit(solution)/shard_map/ppermute | solution.py:374
  13.4 0.2 add.6
  13.6 27.0 %all_to_all.40.parts = f32[64,4,896]{2,1,0:T(4,128)S(1)} all-to-all(f32[64,4,896]{2,1,0:T(4,128)S(1)} %add.6), channel_id=1, replica_groups=mesh['x'=4,'z'=4,'c'=2,'y'=4] {'x','z','y'}, dimensions={0} | all-to-all | bytes 1835008 | tf_op jit(solution)/shard_map/all_to_all | solution.py:381
  40.6 0.8 finish.4
  41.4 15.2 %all_to_all.41.packed = bf16[64,4,896]{2,1,0:T(4,128)(2,1)S(1)} all-to-all(bf16[64,4,896]{2,1,0:T(4,128)(2,1)S(1)} %get-tuple-element.22), channel_id=1, replica_groups=mesh['x'=4,'z'=4,'c'=2,'y'=4] {'x','z','y'}, dimensions={0} | all-to-all | bytes 917504 | tf_op jit(solution)/shard_map/all_to_all | solution.py:381
  56.5 7.5 %first_round.1 = (f32[64,4,896]{2,1,0:T(4,128)S(1)}, bf16[8192,768]{1,0:T(8,128)(2,1)S(1)}) custom-call(bf16[64,4,896]{2,1,0:T(4,128)(2,1)S(1)} %all_to_all.41.packed, s32[1,4096]{1,0:T(1,128)S(1)} %get-tuple-element.20.near_ids.ids, bf16[4096,768]{1,0:T(8,128)(2,1)} %collective-permute-done.2.other.members, ...), custom_call_target="tpu_custom_call", output_to_operand_aliasing={{1}: (4, {})} | custom-call | tf_op jit(solution)/shard_map/first_round/pallas_call | solution.py:274
  64.0 18.9 %all_to_all.42.parts = f32[64,4,896]{2,1,0:T(4,128)S(1)} all-to-all(f32[64,4,896]{2,1,0:T(4,128)S(1)} %get-tuple-element.24), channel_id=1, replica_groups=mesh['x'=4,'z'=4,'c'=2,'y'=4] {'x','z','y'}, dimensions={0} | all-to-all | bytes 1835008 | tf_op jit(solution)/shard_map/all_to_all | solution.py:381
  82.9 0.8 finish.5
  83.6 14.7 %all_to_all.43.packed = bf16[64,4,896]{2,1,0:T(4,128)(2,1)S(1)} all-to-all(bf16[64,4,896]{2,1,0:T(4,128)(2,1)S(1)} %get-tuple-element.25), channel_id=1, replica_groups=mesh['x'=4,'z'=4,'c'=2,'y'=4] {'x','z','y'}, dimensions={0} | all-to-all | bytes 917504 | tf_op jit(solution)/shard_map/all_to_all | solution.py:381
  98.3 7.4 %later_round.2 = f32[64,4,896]{2,1,0:T(4,128)S(1)} custom-call(bf16[64,4,896]{2,1,0:T(4,128)(2,1)S(1)} %all_to_all.43.packed, s32[1,4096]{1,0:T(1,128)S(1)} %get-tuple-element.20.near_ids.ids, bf16[8192,768]{1,0:T(8,128)(2,1)S(1)} %get-tuple-element.26.held, s32[1,4096]{1,0:T(1,128)S(1)} %collective-permute-done.1.far_ids.ids), custom_call_target="tpu_custom_call" | custom-call | tf_op jit(solution)/shard_map/later_round/pallas_call | solution.py:287
  105.8 17.9 %all_to_all.44.parts = f32[64,4,896]{2,1,0:T(4,128)S(1)} all-to-all(f32[64,4,896]{2,1,0:T(4,128)S(1)} %later_round.2), channel_id=1, replica_groups=mesh['x'=4,'z'=4,'c'=2,'y'=4] {'x','z','y'}, dimensions={0} | all-to-all | bytes 1835008 | tf_op jit(solution)/shard_map/all_to_all | solution.py:381
  123.6 0.8 finish.6
  124.4 14.0 %all_to_all.45.packed = bf16[64,4,896]{2,1,0:T(4,128)(2,1)S(1)} all-to-all(bf16[64,4,896]{2,1,0:T(4,128)(2,1)S(1)} %get-tuple-element.27), channel_id=1, replica_groups=mesh['x'=4,'z'=4,'c'=2,'y'=4] {'x','z','y'}, dimensions={0} | all-to-all | bytes 917504 | tf_op jit(solution)/shard_map/all_to_all | solution.py:381
  138.4 7.4 %later_round.3 = f32[64,4,896]{2,1,0:T(4,128)S(1)} custom-call(bf16[64,4,896]{2,1,0:T(4,128)(2,1)S(1)} %all_to_all.45.packed, s32[1,4096]{1,0:T(1,128)S(1)} %get-tuple-element.20.near_ids.ids, bf16[8192,768]{1,0:T(8,128)(2,1)S(1)} %get-tuple-element.26.held, s32[1,4096]{1,0:T(1,128)S(1)} %collective-permute-done.1.far_ids.ids), custom_call_target="tpu_custom_call" | custom-call | tf_op jit(solution)/shard_map/later_round/pallas_call | solution.py:287
  145.9 17.0 %all_to_all.46.parts = f32[64,4,896]{2,1,0:T(4,128)S(1)} all-to-all(f32[64,4,896]{2,1,0:T(4,128)S(1)} %later_round.3), channel_id=1, replica_groups=mesh['x'=4,'z'=4,'c'=2,'y'=4] {'x','z','y'}, dimensions={0} | all-to-all | bytes 1835008 | tf_op jit(solution)/shard_map/all_to_all | solution.py:381
  162.9 1.0 finish.7
  163.9 4.6 %all-to-all-start.7 = ((bf16[64,4,896]{2,1,0:T(4,128)(2,1)}), bf16[64,4,896]{2,1,0:T(4,128)(2,1)S(1)}, u32[]{:S(2)}, u32[]{:S(2)}) async-start(bf16[64,4,896]{2,1,0:T(4,128)(2,1)} %get-tuple-element.28), calls=%async_computation.7 | async-start | bytes 917504 | tf_op jit(solution)/shard_map/all_to_all | solution.py:381
  168.5 2.2 %collective-permute-start.5 = (f32[4,768]{1,0:T(4,128)S(1)}, f32[4,768]{1,0:T(4,128)S(1)}, u32[]{:S(2)}, u32[]{:S(2)}) collective-permute-start(f32[4,768]{1,0:T(4,128)S(1)} %get-tuple-element.29.mine), channel_id=1, source_target_pairs={{0,3},{1,0},{2,1},{3,2},{4,7},{5,4},{6,5},{7,6},{8,11},{9,8},{10,9... | collective-permute-start | bytes 36872 | tf_op jit(solution)/shard_map/ppermute | solution.py:392
  170.7 0.6 collective-permute-start.4
  171.3 0.6 collective-permute-start.3
  171.9 3.3 %collective-permute-done.4.far = f32[4,768]{1,0:T(4,128)S(1)} collective-permute-done((f32[4,768]{1,0:T(4,128)S(1)}, f32[4,768]{1,0:T(4,128)S(1)}, u32[]{:S(2)}, u32[]{:S(2)}) %collective-permute-start.4) | collective-permute-done | bytes 12320 | tf_op jit(solution)/shard_map/ppermute | solution.py:392
  175.2 0.3 collective-permute-done.3.near
  175.5 3.3 %all-to-all-done.7.packed = bf16[64,4,896]{2,1,0:T(4,128)(2,1)S(1)} async-done(((bf16[64,4,896]{2,1,0:T(4,128)(2,1)}), bf16[64,4,896]{2,1,0:T(4,128)(2,1)S(1)}, u32[]{:S(2)}, u32[]{:S(2)}) %all-to-all-start.7) | async-done | bytes 458784 | tf_op jit(solution)/shard_map/all_to_all | solution.py:381
  178.8 4.6 %assign_away.1 = (f32[8,4096]{1,0:T(8,128)S(1)}, f32[2,8,768]{2,1,0:T(8,128)}) custom-call(s32[2]{0:T(128)S(1)} %pad_add_fusion.core.place, bf16[64,4,896]{2,1,0:T(4,128)(2,1)S(1)} %all-to-all-done.7.packed, bf16[4096,768]{1,0:T(8,128)(2,1)} %collective-permute-done.2.other.members, s32[1,4096]{1,0:T(1,128)S(1)} %collective-permute-done.1.far_ids.ids, ...), custom_call_target="tpu_custom_call" | custom-call | tf_op jit(solution)/shard_map/assign_away/pallas_call | solution.py:344
  183.4 10.5 %collective-permute-start.6 = (f32[8,4096]{1,0:T(8,128)S(1)}, f32[8,4096]{1,0:T(8,128)S(1)}, u32[]{:S(2)}, u32[]{:S(2)}) collective-permute-start(f32[8,4096]{1,0:T(8,128)S(1)} %get-tuple-element.30), channel_id=1, source_target_pairs={{0,4},{4,0},{1,5},{5,1},{2,6},{6,2},{3,7},{7,3},{8,12},{12,8},{9,1... | collective-permute-start | bytes 393224 | tf_op jit(solution)/shard_map/ppermute | solution.py:374
  193.9 4.0 %assign_own.1 = f32[8,4096]{1,0:T(8,128)S(1)} custom-call(bf16[64,4,896]{2,1,0:T(4,128)(2,1)S(1)} %all-to-all-done.7.packed, bf16[4096,768]{1,0:T(8,128)(2,1)} %members.3, s32[1,4096]{1,0:T(1,128)S(1)} %get-tuple-element.20.near_ids.ids), custom_call_target="tpu_custom_call" | custom-call | tf_op jit(solution)/shard_map/assign_own/pallas_call | solution.py:357
  197.9 0.7 add.7
  (5 shorter events, 0.1 us)
Async XLA Ops:
  0.6 55.9 %collective-permute-start.2 = (bf16[4096,768]{1,0:T(8,128)(2,1)}, bf16[4096,768]{1,0:T(8,128)(2,1)}, u32[]{:S(2)}, u32[]{:S(2)}) collective-permute-start(bf16[4096,768]{1,0:T(8,128)(2,1)} %members.3), channel_id=1, source_target_pairs={{0,4},{4,0},{1,5},{5,1},{2,6},{6,2},{3,7},{7,3},{8,12},{12,8},{9,1... | collective-permute-start | bytes 18874376 | tf_op jit(solution)/shard_map/ppermute | solution.py:374
  8.0 5.4 %collective-permute-start = (f32[64,4,896]{2,1,0:T(4,128)S(1)}, f32[64,4,896]{2,1,0:T(4,128)S(1)}, u32[]{:S(2)}, u32[]{:S(2)}) collective-permute-start(f32[64,4,896]{2,1,0:T(4,128)S(1)} %get-tuple-element.19), channel_id=1, source_target_pairs={{0,4},{4,0},{1,5},{5,1},{2,6},{6,2},{3,7},{7,3},{8,12},{12,8},{9,1... | collective-permute-start | bytes 2752520 | tf_op jit(solution)/shard_map/ppermute | solution.py:374
  8.1 5.6 %collective-permute-start.1 = (s32[1,4096]{1,0:T(1,128)S(1)}, s32[1,4096]{1,0:T(1,128)S(1)}, u32[]{:S(2)}, u32[]{:S(2)}) collective-permute-start(s32[1,4096]{1,0:T(1,128)S(1)} %get-tuple-element.20.near_ids.ids), channel_id=1, source_target_pairs={{0,4},{4,0},{1,5},{5,1},{2,6},{6,2},{3,7},{7,3},{8,12},{12,8},{9,1... | collective-permute-start | bytes 49160 | tf_op jit(solution)/shard_map/ppermute | solution.py:374
  163.9 14.9 %all-to-all-start.7 = ((bf16[64,4,896]{2,1,0:T(4,128)(2,1)}), bf16[64,4,896]{2,1,0:T(4,128)(2,1)S(1)}, u32[]{:S(2)}, u32[]{:S(2)}) async-start(bf16[64,4,896]{2,1,0:T(4,128)(2,1)} %get-tuple-element.28), calls=%async_computation.7 | async-start | bytes 917504 | tf_op jit(solution)/shard_map/all_to_all | solution.py:381
  168.5 3.4 %collective-permute-start.5 = (f32[4,768]{1,0:T(4,128)S(1)}, f32[4,768]{1,0:T(4,128)S(1)}, u32[]{:S(2)}, u32[]{:S(2)}) collective-permute-start(f32[4,768]{1,0:T(4,128)S(1)} %get-tuple-element.29.mine), channel_id=1, source_target_pairs={{0,3},{1,0},{2,1},{3,2},{4,7},{5,4},{6,5},{7,6},{8,11},{9,8},{10,9... | collective-permute-start | bytes 36872 | tf_op jit(solution)/shard_map/ppermute | solution.py:392
  170.7 4.4 %collective-permute-start.4 = (f32[4,768]{1,0:T(4,128)S(1)}, f32[4,768]{1,0:T(4,128)S(1)}, u32[]{:S(2)}, u32[]{:S(2)}) collective-permute-start(f32[4,768]{1,0:T(4,128)S(1)} %get-tuple-element.29.mine), channel_id=1, source_target_pairs={{0,2},{1,3},{2,0},{3,1},{4,6},{5,7},{6,4},{7,5},{8,10},{9,11},{10,... | collective-permute-start | bytes 36872 | tf_op jit(solution)/shard_map/ppermute | solution.py:392
  171.3 4.2 %collective-permute-start.3 = (f32[4,768]{1,0:T(4,128)S(1)}, f32[4,768]{1,0:T(4,128)S(1)}, u32[]{:S(2)}, u32[]{:S(2)}) collective-permute-start(f32[4,768]{1,0:T(4,128)S(1)} %get-tuple-element.29.mine), channel_id=1, source_target_pairs={{0,1},{1,2},{2,3},{3,0},{4,5},{5,6},{6,7},{7,4},{8,9},{9,10},{10,1... | collective-permute-start | bytes 36872 | tf_op jit(solution)/shard_map/ppermute | solution.py:392
  183.4 14.5 %collective-permute-start.6 = (f32[8,4096]{1,0:T(8,128)S(1)}, f32[8,4096]{1,0:T(8,128)S(1)}, u32[]{:S(2)}, u32[]{:S(2)}) collective-permute-start(f32[8,4096]{1,0:T(8,128)S(1)} %get-tuple-element.30), channel_id=1, source_target_pairs={{0,4},{4,0},{1,5},{5,1},{2,6},{6,2},{3,7},{7,3},{8,12},{12,8},{9,1... | collective-permute-start | bytes 393224 | tf_op jit(solution)/shard_map/ppermute | solution.py:374

commit v7 on v6

--- a/solution.py
+++ b/solution.py
@@ -108,7 +108,7 @@
 
 PART = jax.ShapeDtypeStruct((SEATS, HALF, CHUNK), f32)
 SUM_SCRATCH = [pltpu.VMEM((OWN_LISTS * K, D), f32), pltpu.VMEM((OWN_LISTS * K, LANES), f32)]
-ROOM = pltpu.CompilerParams(vmem_limit_bytes=24 << 20)
+ROOM = pltpu.CompilerParams(vmem_limit_bytes=36 << 20)
 
 
 def seed_away(core, members, owner, seeds):
@@ -278,7 +278,7 @@
         out_shape=[jax.ShapeDtypeStruct((SEATS, HALF, CHUNK), f32), pltpu.VMEM((2 * rows, D), bf16)],
         input_output_aliases={4: 1},
         scratch_shapes=round_scratch(rows) + [pltpu.SemaphoreType.DMA((COPIES,))],
-        compiler_params=pltpu.CompilerParams(vmem_limit_bytes=24 << 20),
+        compiler_params=pltpu.CompilerParams(vmem_limit_bytes=36 << 20),
         name="first_round",
     )(packed, near_ids, other, far_ids, held)
 
@@ -290,7 +290,7 @@
         out_specs=IN_VMEM,
         out_shape=jax.ShapeDtypeStruct((SEATS, HALF, CHUNK), f32),
         scratch_shapes=round_scratch(held.shape[0] // 2),
-        compiler_params=pltpu.CompilerParams(vmem_limit_bytes=24 << 20),
+        compiler_params=pltpu.CompilerParams(vmem_limit_bytes=36 << 20),
         name="later_round",
     )(packed, near_ids, held, far_ids)
 
@@ -372,16 +372,17 @@
 def local(members, owner, seed_label):
     place = jnp.stack([lax.axis_index("c"), lax.axis_index("y")]).astype(jnp.int32)
     swap = lambda value: lax.ppermute(value, "c", SWAP)
-    members, other, owner, seeds = (
-        pltpu.with_memory_space_constraint(v, pltpu.HBM)
-        for v in (members, swap(members), owner.reshape(1, -1), seed_label.reshape(1, -1))
-    )
+    place_in_hbm = lambda value: pltpu.with_memory_space_constraint(value, pltpu.HBM)
+    members, owner, seeds = map(place_in_hbm, (members, owner.reshape(1, -1), seed_label.reshape(1, -1)))
 
     def exchange(parts):
         return lax.all_to_all(parts, SEAT_AXES, split_axis=0, concat_axis=0, tiled=True)
 
     theirs, near_ids, code, held = seed_away(place, members, owner, seeds)
-    parts, far_ids = lax.optimization_barrier((seed_own(code, held) + swap(theirs), swap(near_ids)))
+    parts, far_ids, later = lax.optimization_barrier(
+        (seed_own(code, held) + swap(theirs), swap(near_ids), members)
+    )
+    other = place_in_hbm(swap(later))
     packed = exchange(finish(exchange(parts))[0])
     parts, held = first_round(packed, near_ids, other, far_ids, held)
     for turn in range(ITERS - 1):

time: 199 us -> 197 us (0.990)
  waiting for transfers between devices: 9.79 us -> 6.94 us
    ppermute x4, waiting for transfers between devices: 2.9 us -> 0.04 us  [local(): swap = lambda value: lax.ppermute(value, 'c', SWAP)]
  transfers between devices with their start and end apart: 8 -> 8, of which waited for: 4 -> 3; matrix products, arithmetic and copies ran while one was open for 0% -> 0% of each run, Pallas kernels for 6% -> 3%
where the time goes in v7:
time: 197 us
  blocking collectives  125 us (63%)
  Pallas kernels  42.1 us (21%)
  starting transfers between devices  20.3 us (10%)
  waiting for transfers between devices  6.94 us (4%)
    all_to_all x7, blocking collectives, exchange(): lax.all_to_all(parts, SEAT_AXES, split_axis=0, concat_axis=0, tiled=True)  125 us
    pallas_call x2, Pallas kernels, later_round(): pl.pallas_call(later_kernel, in_specs=[IN_VMEM] * 4, out_specs=IN_VMEM, o...  14.8 us
    ppermute x4, starting transfers between devices, local(): swap = lambda value: lax.ppermute(value, 'c', SWAP)  12.4 us
    pallas_call x1, Pallas kernels, first_round(): pl.pallas_call(first_kernel, in_specs=[IN_VMEM, IN_VMEM, IN_PLACE, IN_VME...  7.46 us
    pallas_call x1, Pallas kernels, seed_away(): pl.pallas_call(seed_away_kernel, in_specs=[IN_SMEM, IN_PLACE, IN_PLACE, I...  6 us
    all_to_all x1, starting transfers between devices, exchange(): lax.all_to_all(parts, SEAT_AXES, split_axis=0, concat_axis=0, tiled=True)  4.63 us
    pallas_call x1, Pallas kernels, assign_away(): pl.pallas_call(assign_away_kernel, in_specs=[IN_SMEM, IN_VMEM, IN_PLACE,...  4.58 us
    pallas_call x1, Pallas kernels, assign_own(): pl.pallas_call(assign_own_kernel, in_specs=[IN_VMEM, IN_PLACE, IN_VMEM],...  4 us
  transfers between devices with their start and end apart: 8, of which 3 were waited for; matrix products, arithmetic and copies ran while one was open for 0% of the time, Pallas kernels for 3%

profile of v7, /device:TPU:1, one launch (start us, length us, event | category | flops | bytes accessed | tf_op | source)
XLA Modules:
  0.0 196.6 jit_solution(8590582400115351082)
XLA Ops:
  0.6 0.1 pad_add_fusion.core.place
  0.7 6.0 %seed_away.1 = (f32[64,4,896]{2,1,0:T(4,128)S(1)}, s32[1,4096]{1,0:T(1,128)S(1)}, s32[1,4096]{1,0:T(1,128)S(1)}, bf16[8192,768]{1,0:T(8,128)(2,1)S(1)}) custom-call(s32[2]{0:T(128)S(1)} %pad_add_fusion.core.place, bf16[4096,768]{1,0:T(8,128)(2,1)} %members.3, s32[1,4096]{1,0:T(1,128)} %bitcast.6, s32[1,4096]{1,0:T(1,128)} %bitcast.7), custom_call_target="tpu_custom_call" | custom-call | tf_op jit(solution)/shard_map/seed_away/pallas_call | solution.py:117
  6.7 1.5 collective-permute-start
  8.2 0.1 collective-permute-start.1
  8.3 2.0 %seed_own.1 = f32[64,4,896]{2,1,0:T(4,128)S(1)} custom-call(s32[1,4096]{1,0:T(1,128)S(1)} %get-tuple-element.18.code, bf16[8192,768]{1,0:T(8,128)(2,1)S(1)} %get-tuple-element.19.held.before), custom_call_target="tpu_custom_call" | custom-call | tf_op jit(solution)/shard_map/seed_own/pallas_call | solution.py:134
  10.3 0.2 add.6
  10.6 0.5 collective-permute-start.2
  11.1 27.0 %all_to_all.40.parts = f32[64,4,896]{2,1,0:T(4,128)S(1)} all-to-all(f32[64,4,896]{2,1,0:T(4,128)S(1)} %add.6), channel_id=1, replica_groups=mesh['x'=4,'z'=4,'c'=2,'y'=4] {'x','z','y'}, dimensions={0} | all-to-all | bytes 1835008 | tf_op jit(solution)/shard_map/all_to_all | solution.py:379
  38.1 0.8 finish.4
  38.8 15.6 %all_to_all.41.packed = bf16[64,4,896]{2,1,0:T(4,128)(2,1)S(1)} all-to-all(bf16[64,4,896]{2,1,0:T(4,128)(2,1)S(1)} %get-tuple-element.23), channel_id=1, replica_groups=mesh['x'=4,'z'=4,'c'=2,'y'=4] {'x','z','y'}, dimensions={0} | all-to-all | bytes 917504 | tf_op jit(solution)/shard_map/all_to_all | solution.py:379
  54.4 7.5 %first_round.1 = (f32[64,4,896]{2,1,0:T(4,128)S(1)}, bf16[8192,768]{1,0:T(8,128)(2,1)S(1)}) custom-call(bf16[64,4,896]{2,1,0:T(4,128)(2,1)S(1)} %all_to_all.41.packed, s32[1,4096]{1,0:T(1,128)S(1)} %get-tuple-element.21.near_ids.ids, bf16[4096,768]{1,0:T(8,128)(2,1)} %collective-permute-done.2.other.members, ...), custom_call_target="tpu_custom_call", output_to_operand_aliasing={{1}: (4, {})} | custom-call | tf_op jit(solution)/shard_map/first_round/pallas_call | solution.py:274
  61.9 19.4 %all_to_all.42.parts = f32[64,4,896]{2,1,0:T(4,128)S(1)} all-to-all(f32[64,4,896]{2,1,0:T(4,128)S(1)} %get-tuple-element.26), channel_id=1, replica_groups=mesh['x'=4,'z'=4,'c'=2,'y'=4] {'x','z','y'}, dimensions={0} | all-to-all | bytes 1835008 | tf_op jit(solution)/shard_map/all_to_all | solution.py:379
  81.3 0.8 finish.5
  82.0 14.8 %all_to_all.43.packed = bf16[64,4,896]{2,1,0:T(4,128)(2,1)S(1)} all-to-all(bf16[64,4,896]{2,1,0:T(4,128)(2,1)S(1)} %get-tuple-element.27), channel_id=1, replica_groups=mesh['x'=4,'z'=4,'c'=2,'y'=4] {'x','z','y'}, dimensions={0} | all-to-all | bytes 917504 | tf_op jit(solution)/shard_map/all_to_all | solution.py:379
  96.9 7.4 %later_round.2 = f32[64,4,896]{2,1,0:T(4,128)S(1)} custom-call(bf16[64,4,896]{2,1,0:T(4,128)(2,1)S(1)} %all_to_all.43.packed, s32[1,4096]{1,0:T(1,128)S(1)} %get-tuple-element.21.near_ids.ids, bf16[8192,768]{1,0:T(8,128)(2,1)S(1)} %get-tuple-element.28.held, s32[1,4096]{1,0:T(1,128)S(1)} %collective-permute-done.1.far_ids.ids), custom_call_target="tpu_custom_call" | custom-call | tf_op jit(solution)/shard_map/later_round/pallas_call | solution.py:287
  104.3 17.4 %all_to_all.44.parts = f32[64,4,896]{2,1,0:T(4,128)S(1)} all-to-all(f32[64,4,896]{2,1,0:T(4,128)S(1)} %later_round.2), channel_id=1, replica_groups=mesh['x'=4,'z'=4,'c'=2,'y'=4] {'x','z','y'}, dimensions={0} | all-to-all | bytes 1835008 | tf_op jit(solution)/shard_map/all_to_all | solution.py:379
  121.7 0.8 finish.6
  122.5 14.2 %all_to_all.45.packed = bf16[64,4,896]{2,1,0:T(4,128)(2,1)S(1)} all-to-all(bf16[64,4,896]{2,1,0:T(4,128)(2,1)S(1)} %get-tuple-element.29), channel_id=1, replica_groups=mesh['x'=4,'z'=4,'c'=2,'y'=4] {'x','z','y'}, dimensions={0} | all-to-all | bytes 917504 | tf_op jit(solution)/shard_map/all_to_all | solution.py:379
  136.6 7.4 %later_round.3 = f32[64,4,896]{2,1,0:T(4,128)S(1)} custom-call(bf16[64,4,896]{2,1,0:T(4,128)(2,1)S(1)} %all_to_all.45.packed, s32[1,4096]{1,0:T(1,128)S(1)} %get-tuple-element.21.near_ids.ids, bf16[8192,768]{1,0:T(8,128)(2,1)S(1)} %get-tuple-element.28.held, s32[1,4096]{1,0:T(1,128)S(1)} %collective-permute-done.1.far_ids.ids), custom_call_target="tpu_custom_call" | custom-call | tf_op jit(solution)/shard_map/later_round/pallas_call | solution.py:287
  144.1 17.0 %all_to_all.46.parts = f32[64,4,896]{2,1,0:T(4,128)S(1)} all-to-all(f32[64,4,896]{2,1,0:T(4,128)S(1)} %later_round.3), channel_id=1, replica_groups=mesh['x'=4,'z'=4,'c'=2,'y'=4] {'x','z','y'}, dimensions={0} | all-to-all | bytes 1835008 | tf_op jit(solution)/shard_map/all_to_all | solution.py:379
  161.1 1.0 finish.7
  162.1 4.6 %all-to-all-start.7 = ((bf16[64,4,896]{2,1,0:T(4,128)(2,1)}), bf16[64,4,896]{2,1,0:T(4,128)(2,1)S(1)}, u32[]{:S(2)}, u32[]{:S(2)}) async-start(bf16[64,4,896]{2,1,0:T(4,128)(2,1)} %get-tuple-element.30), calls=%async_computation.7 | async-start | bytes 917504 | tf_op jit(solution)/shard_map/all_to_all | solution.py:379
  166.7 2.2 %collective-permute-start.5 = (f32[4,768]{1,0:T(4,128)S(1)}, f32[4,768]{1,0:T(4,128)S(1)}, u32[]{:S(2)}, u32[]{:S(2)}) collective-permute-start(f32[4,768]{1,0:T(4,128)S(1)} %get-tuple-element.31.mine), channel_id=1, source_target_pairs={{0,3},{1,0},{2,1},{3,2},{4,7},{5,4},{6,5},{7,6},{8,11},{9,8},{10,9... | collective-permute-start | bytes 36872 | tf_op jit(solution)/shard_map/ppermute | solution.py:393
  168.9 0.6 collective-permute-start.4
  169.5 0.6 collective-permute-start.3
  170.1 3.3 %collective-permute-done.4.far = f32[4,768]{1,0:T(4,128)S(1)} collective-permute-done((f32[4,768]{1,0:T(4,128)S(1)}, f32[4,768]{1,0:T(4,128)S(1)}, u32[]{:S(2)}, u32[]{:S(2)}) %collective-permute-start.4) | collective-permute-done | bytes 12320 | tf_op jit(solution)/shard_map/ppermute | solution.py:393
  173.3 0.3 collective-permute-done.3.near
  173.7 3.3 %all-to-all-done.7.packed = bf16[64,4,896]{2,1,0:T(4,128)(2,1)S(1)} async-done(((bf16[64,4,896]{2,1,0:T(4,128)(2,1)}), bf16[64,4,896]{2,1,0:T(4,128)(2,1)S(1)}, u32[]{:S(2)}, u32[]{:S(2)}) %all-to-all-start.7) | async-done | bytes 458784 | tf_op jit(solution)/shard_map/all_to_all | solution.py:379
  177.0 4.6 %assign_away.1 = (f32[8,4096]{1,0:T(8,128)S(1)}, f32[2,8,768]{2,1,0:T(8,128)}) custom-call(s32[2]{0:T(128)S(1)} %pad_add_fusion.core.place, bf16[64,4,896]{2,1,0:T(4,128)(2,1)S(1)} %all-to-all-done.7.packed, bf16[4096,768]{1,0:T(8,128)(2,1)} %collective-permute-done.2.other.members, s32[1,4096]{1,0:T(1,128)S(1)} %collective-permute-done.1.far_ids.ids, ...), custom_call_target="tpu_custom_call" | custom-call | tf_op jit(solution)/shard_map/assign_away/pallas_call | solution.py:344
  181.6 10.3 %collective-permute-start.6 = (f32[8,4096]{1,0:T(8,128)S(1)}, f32[8,4096]{1,0:T(8,128)S(1)}, u32[]{:S(2)}, u32[]{:S(2)}) collective-permute-start(f32[8,4096]{1,0:T(8,128)S(1)} %get-tuple-element.32), channel_id=1, source_target_pairs={{0,4},{4,0},{1,5},{5,1},{2,6},{6,2},{3,7},{7,3},{8,12},{12,8},{9,1... | collective-permute-start | bytes 393224 | tf_op jit(solution)/shard_map/ppermute | solution.py:374
  191.9 4.0 %assign_own.1 = f32[8,4096]{1,0:T(8,128)S(1)} custom-call(bf16[64,4,896]{2,1,0:T(4,128)(2,1)S(1)} %all-to-all-done.7.packed, bf16[4096,768]{1,0:T(8,128)(2,1)} %members.3, s32[1,4096]{1,0:T(1,128)S(1)} %get-tuple-element.21.near_ids.ids), custom_call_target="tpu_custom_call" | custom-call | tf_op jit(solution)/shard_map/assign_own/pallas_call | solution.py:357
  195.9 0.7 add.7
  (10 shorter events, 0.1 us)
Async XLA Ops:
  0.6 9.9 %slice-start = ((s8[6291456]{0:T(1024)(128)(4,1)}), s8[4194304]{0:T(1024)(128)(4,1)S(1)}, s32[]{:S(2)}) async-start(s8[6291456]{0:T(1024)(128)(4,1)} %bitcast.4), calls=%async_computation.8 | async-start | bytes 8388608
  6.7 3.6 %collective-permute-start = (f32[64,4,896]{2,1,0:T(4,128)S(1)}, f32[64,4,896]{2,1,0:T(4,128)S(1)}, u32[]{:S(2)}, u32[]{:S(2)}) collective-permute-start(f32[64,4,896]{2,1,0:T(4,128)S(1)} %get-tuple-element.20), channel_id=1, source_target_pairs={{0,4},{4,0},{1,5},{5,1},{2,6},{6,2},{3,7},{7,3},{8,12},{12,8},{9,1... | collective-permute-start | bytes 2752520 | tf_op jit(solution)/shard_map/ppermute | solution.py:374
  8.2 2.3 %collective-permute-start.1 = (s32[1,4096]{1,0:T(1,128)S(1)}, s32[1,4096]{1,0:T(1,128)S(1)}, u32[]{:S(2)}, u32[]{:S(2)}) collective-permute-start(s32[1,4096]{1,0:T(1,128)S(1)} %get-tuple-element.21.near_ids.ids), channel_id=1, source_target_pairs={{0,4},{4,0},{1,5},{5,1},{2,6},{6,2},{3,7},{7,3},{8,12},{12,8},{9,1... | collective-permute-start | bytes 49160 | tf_op jit(solution)/shard_map/ppermute | solution.py:374
  8.3 2.3 %slice-start.1 = ((s8[6291456]{0:T(1024)(128)(4,1)}), s8[2097152]{0:T(1024)(128)(4,1)S(1)}, s32[]{:S(2)}) async-start(s8[6291456]{0:T(1024)(128)(4,1)} %bitcast.4), calls=%async_computation.9 | async-start | bytes 4194304
  10.6 43.8 %collective-permute-start.2 = (bf16[4096,768]{1,0:T(8,128)(2,1)S(1)}, bf16[4096,768]{1,0:T(8,128)(2,1)}, u32[]{:S(2)}, u32[]{:S(2)}) collective-permute-start(bf16[4096,768]{1,0:T(8,128)(2,1)S(1)} %bitcast.5), channel_id=1, source_target_pairs={{0,4},{4,0},{1,5},{5,1},{2,6},{6,2},{3,7},{7,3},{8,12},{12,8},{9,1... | collective-permute-start | bytes 18874376 | tf_op jit(solution)/shard_map/ppermute | solution.py:374
  162.1 14.9 %all-to-all-start.7 = ((bf16[64,4,896]{2,1,0:T(4,128)(2,1)}), bf16[64,4,896]{2,1,0:T(4,128)(2,1)S(1)}, u32[]{:S(2)}, u32[]{:S(2)}) async-start(bf16[64,4,896]{2,1,0:T(4,128)(2,1)} %get-tuple-element.30), calls=%async_computation.7 | async-start | bytes 917504 | tf_op jit(solution)/shard_map/all_to_all | solution.py:379
  166.7 3.3 %collective-permute-start.5 = (f32[4,768]{1,0:T(4,128)S(1)}, f32[4,768]{1,0:T(4,128)S(1)}, u32[]{:S(2)}, u32[]{:S(2)}) collective-permute-start(f32[4,768]{1,0:T(4,128)S(1)} %get-tuple-element.31.mine), channel_id=1, source_target_pairs={{0,3},{1,0},{2,1},{3,2},{4,7},{5,4},{6,5},{7,6},{8,11},{9,8},{10,9... | collective-permute-start | bytes 36872 | tf_op jit(solution)/shard_map/ppermute | solution.py:393
  168.9 4.4 %collective-permute-start.4 = (f32[4,768]{1,0:T(4,128)S(1)}, f32[4,768]{1,0:T(4,128)S(1)}, u32[]{:S(2)}, u32[]{:S(2)}) collective-permute-start(f32[4,768]{1,0:T(4,128)S(1)} %get-tuple-element.31.mine), channel_id=1, source_target_pairs={{0,2},{1,3},{2,0},{3,1},{4,6},{5,7},{6,4},{7,5},{8,10},{9,11},{10,... | collective-permute-start | bytes 36872 | tf_op jit(solution)/shard_map/ppermute | solution.py:393
  169.5 4.2 %collective-permute-start.3 = (f32[4,768]{1,0:T(4,128)S(1)}, f32[4,768]{1,0:T(4,128)S(1)}, u32[]{:S(2)}, u32[]{:S(2)}) collective-permute-start(f32[4,768]{1,0:T(4,128)S(1)} %get-tuple-element.31.mine), channel_id=1, source_target_pairs={{0,1},{1,2},{2,3},{3,0},{4,5},{5,6},{6,7},{7,4},{8,9},{9,10},{10,1... | collective-permute-start | bytes 36872 | tf_op jit(solution)/shard_map/ppermute | solution.py:393
  181.6 14.3 %collective-permute-start.6 = (f32[8,4096]{1,0:T(8,128)S(1)}, f32[8,4096]{1,0:T(8,128)S(1)}, u32[]{:S(2)}, u32[]{:S(2)}) collective-permute-start(f32[8,4096]{1,0:T(8,128)S(1)} %get-tuple-element.32), channel_id=1, source_target_pairs={{0,4},{4,0},{1,5},{5,1},{2,6},{6,2},{3,7},{7,3},{8,12},{12,8},{9,1... | collective-permute-start | bytes 393224 | tf_op jit(solution)/shard_map/ppermute | solution.py:374

commit v8 on v7

--- a/solution.py
+++ b/solution.py
@@ -203,17 +203,19 @@
     return exps / jnp.sum(exps, axis=0, keepdims=True)
 
 
-def add_members(near_ids, far_ids, held, ids, cen, nrm, acc, tot, dots, arrive):
+def add_members(near_ids, far_ids, held, ids, cen, nrm, acc, tot, dots, flat, arrive):
     half = near_ids.shape[1]
     ids[:, :half] = near_ids[...]
     ids[:, half:] = far_ids[...] ^ OWN_LISTS
+    flat[...] = cen[...].T
     acc[...] = jnp.zeros_like(acc)
     tot[...] = jnp.zeros_like(tot)
 
     def work(turn, carry):
         arrive(turn)
         for part in range(UNROLL):
-            dots[part] = dots_of(turn * UNROLL + part, cen, held)
+            tile = held[at_tile(turn * UNROLL + part), :]
+            dots[part] = jnp.dot(tile, flat[...], preferred_element_type=f32).T
         for part in range(UNROLL):
             spot = at_tile(turn * UNROLL + part)
             names = jnp.broadcast_to(ids[:, spot], (K, TILE))
@@ -230,7 +232,7 @@
     lax.fori_loop(0, held.shape[0] // TILE // UNROLL, work, 0)
 
 
-def first_kernel(packed, near_ids, other, far_ids, before, out, held, cen, nrm, acc, tot, ids, dots, sems):
+def first_kernel(packed, near_ids, other, far_ids, before, out, held, cen, nrm, acc, tot, ids, dots, flat, sems):
     rows = other.shape[0] // COPIES
 
     def copy_of(number):
@@ -248,13 +250,13 @@
             for number in range(COPIES):
                 copy_of(number).wait()
 
-    add_members(near_ids, far_ids, held, ids, cen, nrm, acc, tot, dots, arrive)
+    add_members(near_ids, far_ids, held, ids, cen, nrm, acc, tot, dots, flat, arrive)
     store_sums(out, acc, tot, 0)
 
 
-def later_kernel(packed, near_ids, held, far_ids, out, cen, nrm, acc, tot, ids, dots):
+def later_kernel(packed, near_ids, held, far_ids, out, cen, nrm, acc, tot, ids, dots, flat):
     unpack_centers(packed, cen, nrm)
-    add_members(near_ids, far_ids, held, ids, cen, nrm, acc, tot, dots, lambda turn: None)
+    add_members(near_ids, far_ids, held, ids, cen, nrm, acc, tot, dots, flat, lambda turn: None)
     store_sums(out, acc, tot, 0)
 
 
@@ -266,6 +268,7 @@
         pltpu.VMEM((OWN_LISTS * K, LANES), f32),
         pltpu.VMEM((1, 2 * rows), jnp.int32),
         pltpu.VMEM((UNROLL, OWN_LISTS * K, TILE), f32),
+        pltpu.VMEM((D, OWN_LISTS * K), bf16),
     ]
 
 

time: 197 us -> 198 us (level)
  no operation moved by 1% of the time
where the time goes in v8:
time: 198 us; the launch traced here: 197 us
  blocking collectives  125 us (63%)
  Pallas kernels  42.8 us (22%)
  starting transfers between devices  20.3 us (10%)
  waiting for transfers between devices  6.94 us (4%)
    all_to_all x7, blocking collectives, exchange(): lax.all_to_all(parts, SEAT_AXES, split_axis=0, concat_axis=0, tiled=True)  125 us
    pallas_call x2, Pallas kernels, later_round(): pl.pallas_call(later_kernel, in_specs=[IN_VMEM] * 4, out_specs=IN_VMEM, o...  15.2 us
    ppermute x4, starting transfers between devices, local(): swap = lambda value: lax.ppermute(value, 'c', SWAP)  12.4 us
    pallas_call x1, Pallas kernels, first_round(): pl.pallas_call(first_kernel, in_specs=[IN_VMEM, IN_VMEM, IN_PLACE, IN_VME...  7.66 us
    pallas_call x1, Pallas kernels, seed_away(): pl.pallas_call(seed_away_kernel, in_specs=[IN_SMEM, IN_PLACE, IN_PLACE, I...  6 us
    all_to_all x1, starting transfers between devices, exchange(): lax.all_to_all(parts, SEAT_AXES, split_axis=0, concat_axis=0, tiled=True)  4.63 us
    pallas_call x1, Pallas kernels, assign_away(): pl.pallas_call(assign_away_kernel, in_specs=[IN_SMEM, IN_VMEM, IN_PLACE,...  4.59 us
    pallas_call x1, Pallas kernels, assign_own(): pl.pallas_call(assign_own_kernel, in_specs=[IN_VMEM, IN_PLACE, IN_VMEM],...  4 us
  transfers between devices with their start and end apart: 8, of which 3 were waited for; matrix products, arithmetic and copies ran while one was open for 0% of the time, Pallas kernels for 3%

profile of v8, /device:TPU:1, one launch (start us, length us, event | category | flops | bytes accessed | tf_op | source)
XLA Modules:
  0.0 197.2 jit_solution(14438250871763928463)
XLA Ops:
  0.6 0.1 pad_add_fusion.core.place
  0.7 6.0 %seed_away.1 = (f32[64,4,896]{2,1,0:T(4,128)S(1)}, s32[1,4096]{1,0:T(1,128)S(1)}, s32[1,4096]{1,0:T(1,128)S(1)}, bf16[8192,768]{1,0:T(8,128)(2,1)S(1)}) custom-call(s32[2]{0:T(128)S(1)} %pad_add_fusion.core.place, bf16[4096,768]{1,0:T(8,128)(2,1)} %members.3, s32[1,4096]{1,0:T(1,128)} %bitcast.6, s32[1,4096]{1,0:T(1,128)} %bitcast.7), custom_call_target="tpu_custom_call" | custom-call | tf_op jit(solution)/shard_map/seed_away/pallas_call | solution.py:117
  6.7 1.5 collective-permute-start
  8.2 0.1 collective-permute-start.1
  8.3 2.0 seed_own.1
  10.3 0.2 add.6
  10.6 0.5 collective-permute-start.2
  11.1 27.0 %all_to_all.40.parts = f32[64,4,896]{2,1,0:T(4,128)S(1)} all-to-all(f32[64,4,896]{2,1,0:T(4,128)S(1)} %add.6), channel_id=1, replica_groups=mesh['x'=4,'z'=4,'c'=2,'y'=4] {'x','z','y'}, dimensions={0} | all-to-all | bytes 1835008 | tf_op jit(solution)/shard_map/all_to_all | solution.py:382
  38.1 0.8 finish.4
  38.8 15.6 %all_to_all.41.packed = bf16[64,4,896]{2,1,0:T(4,128)(2,1)S(1)} all-to-all(bf16[64,4,896]{2,1,0:T(4,128)(2,1)S(1)} %get-tuple-element.23), channel_id=1, replica_groups=mesh['x'=4,'z'=4,'c'=2,'y'=4] {'x','z','y'}, dimensions={0} | all-to-all | bytes 917504 | tf_op jit(solution)/shard_map/all_to_all | solution.py:382
  54.4 7.7 %first_round.1 = (f32[64,4,896]{2,1,0:T(4,128)S(1)}, bf16[8192,768]{1,0:T(8,128)(2,1)S(1)}) custom-call(bf16[64,4,896]{2,1,0:T(4,128)(2,1)S(1)} %all_to_all.41.packed, s32[1,4096]{1,0:T(1,128)S(1)} %get-tuple-element.21.near_ids.ids, bf16[4096,768]{1,0:T(8,128)(2,1)} %collective-permute-done.2.other.members, ...), custom_call_target="tpu_custom_call", output_to_operand_aliasing={{1}: (4, {})} | custom-call | tf_op jit(solution)/shard_map/first_round/pallas_call | solution.py:277
  62.1 19.4 %all_to_all.42.parts = f32[64,4,896]{2,1,0:T(4,128)S(1)} all-to-all(f32[64,4,896]{2,1,0:T(4,128)S(1)} %get-tuple-element.26), channel_id=1, replica_groups=mesh['x'=4,'z'=4,'c'=2,'y'=4] {'x','z','y'}, dimensions={0} | all-to-all | bytes 1835008 | tf_op jit(solution)/shard_map/all_to_all | solution.py:382
  81.5 0.8 finish.5
  82.2 14.8 %all_to_all.43.packed = bf16[64,4,896]{2,1,0:T(4,128)(2,1)S(1)} all-to-all(bf16[64,4,896]{2,1,0:T(4,128)(2,1)S(1)} %get-tuple-element.27), channel_id=1, replica_groups=mesh['x'=4,'z'=4,'c'=2,'y'=4] {'x','z','y'}, dimensions={0} | all-to-all | bytes 917504 | tf_op jit(solution)/shard_map/all_to_all | solution.py:382
  97.1 7.6 %later_round.2 = f32[64,4,896]{2,1,0:T(4,128)S(1)} custom-call(bf16[64,4,896]{2,1,0:T(4,128)(2,1)S(1)} %all_to_all.43.packed, s32[1,4096]{1,0:T(1,128)S(1)} %get-tuple-element.21.near_ids.ids, bf16[8192,768]{1,0:T(8,128)(2,1)S(1)} %get-tuple-element.28.held, s32[1,4096]{1,0:T(1,128)S(1)} %collective-permute-done.1.far_ids.ids), custom_call_target="tpu_custom_call" | custom-call | tf_op jit(solution)/shard_map/later_round/pallas_call | solution.py:290
  104.7 17.4 %all_to_all.44.parts = f32[64,4,896]{2,1,0:T(4,128)S(1)} all-to-all(f32[64,4,896]{2,1,0:T(4,128)S(1)} %later_round.2), channel_id=1, replica_groups=mesh['x'=4,'z'=4,'c'=2,'y'=4] {'x','z','y'}, dimensions={0} | all-to-all | bytes 1835008 | tf_op jit(solution)/shard_map/all_to_all | solution.py:382
  122.1 0.8 finish.6
  122.9 14.2 %all_to_all.45.packed = bf16[64,4,896]{2,1,0:T(4,128)(2,1)S(1)} all-to-all(bf16[64,4,896]{2,1,0:T(4,128)(2,1)S(1)} %get-tuple-element.29), channel_id=1, replica_groups=mesh['x'=4,'z'=4,'c'=2,'y'=4] {'x','z','y'}, dimensions={0} | all-to-all | bytes 917504 | tf_op jit(solution)/shard_map/all_to_all | solution.py:382
  137.0 7.6 %later_round.3 = f32[64,4,896]{2,1,0:T(4,128)S(1)} custom-call(bf16[64,4,896]{2,1,0:T(4,128)(2,1)S(1)} %all_to_all.45.packed, s32[1,4096]{1,0:T(1,128)S(1)} %get-tuple-element.21.near_ids.ids, bf16[8192,768]{1,0:T(8,128)(2,1)S(1)} %get-tuple-element.28.held, s32[1,4096]{1,0:T(1,128)S(1)} %collective-permute-done.1.far_ids.ids), custom_call_target="tpu_custom_call" | custom-call | tf_op jit(solution)/shard_map/later_round/pallas_call | solution.py:290
  144.7 17.0 %all_to_all.46.parts = f32[64,4,896]{2,1,0:T(4,128)S(1)} all-to-all(f32[64,4,896]{2,1,0:T(4,128)S(1)} %later_round.3), channel_id=1, replica_groups=mesh['x'=4,'z'=4,'c'=2,'y'=4] {'x','z','y'}, dimensions={0} | all-to-all | bytes 1835008 | tf_op jit(solution)/shard_map/all_to_all | solution.py:382
  161.7 1.0 finish.7
  162.7 4.6 %all-to-all-start.7 = ((bf16[64,4,896]{2,1,0:T(4,128)(2,1)}), bf16[64,4,896]{2,1,0:T(4,128)(2,1)S(1)}, u32[]{:S(2)}, u32[]{:S(2)}) async-start(bf16[64,4,896]{2,1,0:T(4,128)(2,1)} %get-tuple-element.30), calls=%async_computation.7 | async-start | bytes 917504 | tf_op jit(solution)/shard_map/all_to_all | solution.py:382
  167.4 2.2 %collective-permute-start.5 = (f32[4,768]{1,0:T(4,128)S(1)}, f32[4,768]{1,0:T(4,128)S(1)}, u32[]{:S(2)}, u32[]{:S(2)}) collective-permute-start(f32[4,768]{1,0:T(4,128)S(1)} %get-tuple-element.31.mine), channel_id=1, source_target_pairs={{0,3},{1,0},{2,1},{3,2},{4,7},{5,4},{6,5},{7,6},{8,11},{9,8},{10,9... | collective-permute-start | bytes 36872 | tf_op jit(solution)/shard_map/ppermute | solution.py:396
  169.5 0.6 collective-permute-start.4
  170.1 0.6 collective-permute-start.3
  170.7 3.3 %collective-permute-done.4.far = f32[4,768]{1,0:T(4,128)S(1)} collective-permute-done((f32[4,768]{1,0:T(4,128)S(1)}, f32[4,768]{1,0:T(4,128)S(1)}, u32[]{:S(2)}, u32[]{:S(2)}) %collective-permute-start.4) | collective-permute-done | bytes 12320 | tf_op jit(solution)/shard_map/ppermute | solution.py:396
  174.0 0.3 collective-permute-done.3.near
  174.3 3.3 %all-to-all-done.7.packed = bf16[64,4,896]{2,1,0:T(4,128)(2,1)S(1)} async-done(((bf16[64,4,896]{2,1,0:T(4,128)(2,1)}), bf16[64,4,896]{2,1,0:T(4,128)(2,1)S(1)}, u32[]{:S(2)}, u32[]{:S(2)}) %all-to-all-start.7) | async-done | bytes 458784 | tf_op jit(solution)/shard_map/all_to_all | solution.py:382
  177.6 4.6 %assign_away.1 = (f32[8,4096]{1,0:T(8,128)S(1)}, f32[2,8,768]{2,1,0:T(8,128)}) custom-call(s32[2]{0:T(128)S(1)} %pad_add_fusion.core.place, bf16[64,4,896]{2,1,0:T(4,128)(2,1)S(1)} %all-to-all-done.7.packed, bf16[4096,768]{1,0:T(8,128)(2,1)} %collective-permute-done.2.other.members, s32[1,4096]{1,0:T(1,128)S(1)} %collective-permute-done.1.far_ids.ids, ...), custom_call_target="tpu_custom_call" | custom-call | tf_op jit(solution)/shard_map/assign_away/pallas_call | solution.py:347
  182.2 10.3 %collective-permute-start.6 = (f32[8,4096]{1,0:T(8,128)S(1)}, f32[8,4096]{1,0:T(8,128)S(1)}, u32[]{:S(2)}, u32[]{:S(2)}) collective-permute-start(f32[8,4096]{1,0:T(8,128)S(1)} %get-tuple-element.32), channel_id=1, source_target_pairs={{0,4},{4,0},{1,5},{5,1},{2,6},{6,2},{3,7},{7,3},{8,12},{12,8},{9,1... | collective-permute-start | bytes 393224 | tf_op jit(solution)/shard_map/ppermute | solution.py:377
  192.5 4.0 %assign_own.1 = f32[8,4096]{1,0:T(8,128)S(1)} custom-call(bf16[64,4,896]{2,1,0:T(4,128)(2,1)S(1)} %all-to-all-done.7.packed, bf16[4096,768]{1,0:T(8,128)(2,1)} %members.3, s32[1,4096]{1,0:T(1,128)S(1)} %get-tuple-element.21.near_ids.ids), custom_call_target="tpu_custom_call" | custom-call | tf_op jit(solution)/shard_map/assign_own/pallas_call | solution.py:360
  196.5 0.7 add.7
  (10 shorter events, 0.1 us)
Async XLA Ops:
  0.6 9.9 %slice-start = ((s8[6291456]{0:T(1024)(128)(4,1)}), s8[4194304]{0:T(1024)(128)(4,1)S(1)}, s32[]{:S(2)}) async-start(s8[6291456]{0:T(1024)(128)(4,1)} %bitcast.4), calls=%async_computation.8 | async-start | bytes 8388608
  6.7 3.6 %collective-permute-start = (f32[64,4,896]{2,1,0:T(4,128)S(1)}, f32[64,4,896]{2,1,0:T(4,128)S(1)}, u32[]{:S(2)}, u32[]{:S(2)}) collective-permute-start(f32[64,4,896]{2,1,0:T(4,128)S(1)} %get-tuple-element.20), channel_id=1, source_target_pairs={{0,4},{4,0},{1,5},{5,1},{2,6},{6,2},{3,7},{7,3},{8,12},{12,8},{9,1... | collective-permute-start | bytes 2752520 | tf_op jit(solution)/shard_map/ppermute | solution.py:377
  8.2 2.3 %collective-permute-start.1 = (s32[1,4096]{1,0:T(1,128)S(1)}, s32[1,4096]{1,0:T(1,128)S(1)}, u32[]{:S(2)}, u32[]{:S(2)}) collective-permute-start(s32[1,4096]{1,0:T(1,128)S(1)} %get-tuple-element.21.near_ids.ids), channel_id=1, source_target_pairs={{0,4},{4,0},{1,5},{5,1},{2,6},{6,2},{3,7},{7,3},{8,12},{12,8},{9,1... | collective-permute-start | bytes 49160 | tf_op jit(solution)/shard_map/ppermute | solution.py:377
  8.3 2.3 %slice-start.1 = ((s8[6291456]{0:T(1024)(128)(4,1)}), s8[2097152]{0:T(1024)(128)(4,1)S(1)}, s32[]{:S(2)}) async-start(s8[6291456]{0:T(1024)(128)(4,1)} %bitcast.4), calls=%async_computation.9 | async-start | bytes 4194304
  10.6 43.8 %collective-permute-start.2 = (bf16[4096,768]{1,0:T(8,128)(2,1)S(1)}, bf16[4096,768]{1,0:T(8,128)(2,1)}, u32[]{:S(2)}, u32[]{:S(2)}) collective-permute-start(bf16[4096,768]{1,0:T(8,128)(2,1)S(1)} %bitcast.5), channel_id=1, source_target_pairs={{0,4},{4,0},{1,5},{5,1},{2,6},{6,2},{3,7},{7,3},{8,12},{12,8},{9,1... | collective-permute-start | bytes 18874376 | tf_op jit(solution)/shard_map/ppermute | solution.py:377
  162.7 14.9 %all-to-all-start.7 = ((bf16[64,4,896]{2,1,0:T(4,128)(2,1)}), bf16[64,4,896]{2,1,0:T(4,128)(2,1)S(1)}, u32[]{:S(2)}, u32[]{:S(2)}) async-start(bf16[64,4,896]{2,1,0:T(4,128)(2,1)} %get-tuple-element.30), calls=%async_computation.7 | async-start | bytes 917504 | tf_op jit(solution)/shard_map/all_to_all | solution.py:382
  167.4 3.3 %collective-permute-start.5 = (f32[4,768]{1,0:T(4,128)S(1)}, f32[4,768]{1,0:T(4,128)S(1)}, u32[]{:S(2)}, u32[]{:S(2)}) collective-permute-start(f32[4,768]{1,0:T(4,128)S(1)} %get-tuple-element.31.mine), channel_id=1, source_target_pairs={{0,3},{1,0},{2,1},{3,2},{4,7},{5,4},{6,5},{7,6},{8,11},{9,8},{10,9... | collective-permute-start | bytes 36872 | tf_op jit(solution)/shard_map/ppermute | solution.py:396
  169.5 4.4 %collective-permute-start.4 = (f32[4,768]{1,0:T(4,128)S(1)}, f32[4,768]{1,0:T(4,128)S(1)}, u32[]{:S(2)}, u32[]{:S(2)}) collective-permute-start(f32[4,768]{1,0:T(4,128)S(1)} %get-tuple-element.31.mine), channel_id=1, source_target_pairs={{0,2},{1,3},{2,0},{3,1},{4,6},{5,7},{6,4},{7,5},{8,10},{9,11},{10,... | collective-permute-start | bytes 36872 | tf_op jit(solution)/shard_map/ppermute | solution.py:396
  170.1 4.2 %collective-permute-start.3 = (f32[4,768]{1,0:T(4,128)S(1)}, f32[4,768]{1,0:T(4,128)S(1)}, u32[]{:S(2)}, u32[]{:S(2)}) collective-permute-start(f32[4,768]{1,0:T(4,128)S(1)} %get-tuple-element.31.mine), channel_id=1, source_target_pairs={{0,1},{1,2},{2,3},{3,0},{4,5},{5,6},{6,7},{7,4},{8,9},{9,10},{10,1... | collective-permute-start | bytes 36872 | tf_op jit(solution)/shard_map/ppermute | solution.py:396
  182.2 14.3 %collective-permute-start.6 = (f32[8,4096]{1,0:T(8,128)S(1)}, f32[8,4096]{1,0:T(8,128)S(1)}, u32[]{:S(2)}, u32[]{:S(2)}) collective-permute-start(f32[8,4096]{1,0:T(8,128)S(1)} %get-tuple-element.32), channel_id=1, source_target_pairs={{0,4},{4,0},{1,5},{5,1},{2,6},{6,2},{3,7},{7,3},{8,12},{12,8},{9,1... | collective-permute-start | bytes 393224 | tf_op jit(solution)/shard_map/ppermute | solution.py:377

commit v9 on v7

--- a/solution.py
+++ b/solution.py
@@ -15,7 +15,7 @@
 SEATS = 64
 TILE = 512
 UNROLL = 8
-COPIES = 4
+COPIES = 2
 SEED_COPIES = 4
 f32 = jnp.float32
 bf16 = jnp.bfloat16

time: 197 us -> 197 us (level)
  no operation moved by 1% of the time
where the time goes in v9:
time: 197 us
  blocking collectives  125 us (63%)
  Pallas kernels  42.3 us (21%)
  starting transfers between devices  20.3 us (10%)
  waiting for transfers between devices  6.94 us (4%)
    all_to_all x7, blocking collectives, exchange(): lax.all_to_all(parts, SEAT_AXES, split_axis=0, concat_axis=0, tiled=True)  125 us
    pallas_call x2, Pallas kernels, later_round(): pl.pallas_call(later_kernel, in_specs=[IN_VMEM] * 4, out_specs=IN_VMEM, o...  14.8 us
    ppermute x4, starting transfers between devices, local(): swap = lambda value: lax.ppermute(value, 'c', SWAP)  12.4 us
    pallas_call x1, Pallas kernels, first_round(): pl.pallas_call(first_kernel, in_specs=[IN_VMEM, IN_VMEM, IN_PLACE, IN_VME...  7.43 us
    pallas_call x1, Pallas kernels, seed_away(): pl.pallas_call(seed_away_kernel, in_specs=[IN_SMEM, IN_PLACE, IN_PLACE, I...  6 us
    pallas_call x1, Pallas kernels, assign_away(): pl.pallas_call(assign_away_kernel, in_specs=[IN_SMEM, IN_VMEM, IN_PLACE,...  4.78 us
    all_to_all x1, starting transfers between devices, exchange(): lax.all_to_all(parts, SEAT_AXES, split_axis=0, concat_axis=0, tiled=True)  4.63 us
    pallas_call x1, Pallas kernels, assign_own(): pl.pallas_call(assign_own_kernel, in_specs=[IN_VMEM, IN_PLACE, IN_VMEM],...  4 us
  transfers between devices with their start and end apart: 8, of which 3 were waited for; matrix products, arithmetic and copies ran while one was open for 0% of the time, Pallas kernels for 3%

profile of v9, /device:TPU:1, one launch (start us, length us, event | category | flops | bytes accessed | tf_op | source)
XLA Modules:
  0.0 196.8 jit_solution(2803907332530211636)
XLA Ops:
  0.6 0.1 pad_add_fusion.core.place
  0.7 6.0 %seed_away.1 = (f32[64,4,896]{2,1,0:T(4,128)S(1)}, s32[1,4096]{1,0:T(1,128)S(1)}, s32[1,4096]{1,0:T(1,128)S(1)}, bf16[8192,768]{1,0:T(8,128)(2,1)S(1)}) custom-call(s32[2]{0:T(128)S(1)} %pad_add_fusion.core.place, bf16[4096,768]{1,0:T(8,128)(2,1)} %members.3, s32[1,4096]{1,0:T(1,128)} %bitcast.6, s32[1,4096]{1,0:T(1,128)} %bitcast.7), custom_call_target="tpu_custom_call" | custom-call | tf_op jit(solution)/shard_map/seed_away/pallas_call | solution.py:117
  6.7 1.5 collective-permute-start
  8.2 0.1 collective-permute-start.1
  8.3 2.0 %seed_own.1 = f32[64,4,896]{2,1,0:T(4,128)S(1)} custom-call(s32[1,4096]{1,0:T(1,128)S(1)} %get-tuple-element.18.code, bf16[8192,768]{1,0:T(8,128)(2,1)S(1)} %get-tuple-element.19.held.before), custom_call_target="tpu_custom_call" | custom-call | tf_op jit(solution)/shard_map/seed_own/pallas_call | solution.py:134
  10.3 0.2 add.6
  10.6 0.5 collective-permute-start.2
  11.1 27.0 %all_to_all.40.parts = f32[64,4,896]{2,1,0:T(4,128)S(1)} all-to-all(f32[64,4,896]{2,1,0:T(4,128)S(1)} %add.6), channel_id=1, replica_groups=mesh['x'=4,'z'=4,'c'=2,'y'=4] {'x','z','y'}, dimensions={0} | all-to-all | bytes 1835008 | tf_op jit(solution)/shard_map/all_to_all | solution.py:379
  38.1 0.8 finish.4
  38.8 15.6 %all_to_all.41.packed = bf16[64,4,896]{2,1,0:T(4,128)(2,1)S(1)} all-to-all(bf16[64,4,896]{2,1,0:T(4,128)(2,1)S(1)} %get-tuple-element.23), channel_id=1, replica_groups=mesh['x'=4,'z'=4,'c'=2,'y'=4] {'x','z','y'}, dimensions={0} | all-to-all | bytes 917504 | tf_op jit(solution)/shard_map/all_to_all | solution.py:379
  54.4 7.4 %first_round.1 = (f32[64,4,896]{2,1,0:T(4,128)S(1)}, bf16[8192,768]{1,0:T(8,128)(2,1)S(1)}) custom-call(bf16[64,4,896]{2,1,0:T(4,128)(2,1)S(1)} %all_to_all.41.packed, s32[1,4096]{1,0:T(1,128)S(1)} %get-tuple-element.21.near_ids.ids, bf16[4096,768]{1,0:T(8,128)(2,1)} %collective-permute-done.2.other.members, ...), custom_call_target="tpu_custom_call", output_to_operand_aliasing={{1}: (4, {})} | custom-call | tf_op jit(solution)/shard_map/first_round/pallas_call | solution.py:274
  61.8 19.4 %all_to_all.42.parts = f32[64,4,896]{2,1,0:T(4,128)S(1)} all-to-all(f32[64,4,896]{2,1,0:T(4,128)S(1)} %get-tuple-element.26), channel_id=1, replica_groups=mesh['x'=4,'z'=4,'c'=2,'y'=4] {'x','z','y'}, dimensions={0} | all-to-all | bytes 1835008 | tf_op jit(solution)/shard_map/all_to_all | solution.py:379
  81.2 0.8 finish.5
  82.0 14.8 %all_to_all.43.packed = bf16[64,4,896]{2,1,0:T(4,128)(2,1)S(1)} all-to-all(bf16[64,4,896]{2,1,0:T(4,128)(2,1)S(1)} %get-tuple-element.27), channel_id=1, replica_groups=mesh['x'=4,'z'=4,'c'=2,'y'=4] {'x','z','y'}, dimensions={0} | all-to-all | bytes 917504 | tf_op jit(solution)/shard_map/all_to_all | solution.py:379
  96.8 7.4 %later_round.2 = f32[64,4,896]{2,1,0:T(4,128)S(1)} custom-call(bf16[64,4,896]{2,1,0:T(4,128)(2,1)S(1)} %all_to_all.43.packed, s32[1,4096]{1,0:T(1,128)S(1)} %get-tuple-element.21.near_ids.ids, bf16[8192,768]{1,0:T(8,128)(2,1)S(1)} %get-tuple-element.28.held, s32[1,4096]{1,0:T(1,128)S(1)} %collective-permute-done.1.far_ids.ids), custom_call_target="tpu_custom_call" | custom-call | tf_op jit(solution)/shard_map/later_round/pallas_call | solution.py:287
  104.3 17.4 %all_to_all.44.parts = f32[64,4,896]{2,1,0:T(4,128)S(1)} all-to-all(f32[64,4,896]{2,1,0:T(4,128)S(1)} %later_round.2), channel_id=1, replica_groups=mesh['x'=4,'z'=4,'c'=2,'y'=4] {'x','z','y'}, dimensions={0} | all-to-all | bytes 1835008 | tf_op jit(solution)/shard_map/all_to_all | solution.py:379
  121.7 0.8 finish.6
  122.5 14.2 %all_to_all.45.packed = bf16[64,4,896]{2,1,0:T(4,128)(2,1)S(1)} all-to-all(bf16[64,4,896]{2,1,0:T(4,128)(2,1)S(1)} %get-tuple-element.29), channel_id=1, replica_groups=mesh['x'=4,'z'=4,'c'=2,'y'=4] {'x','z','y'}, dimensions={0} | all-to-all | bytes 917504 | tf_op jit(solution)/shard_map/all_to_all | solution.py:379
  136.6 7.4 %later_round.3 = f32[64,4,896]{2,1,0:T(4,128)S(1)} custom-call(bf16[64,4,896]{2,1,0:T(4,128)(2,1)S(1)} %all_to_all.45.packed, s32[1,4096]{1,0:T(1,128)S(1)} %get-tuple-element.21.near_ids.ids, bf16[8192,768]{1,0:T(8,128)(2,1)S(1)} %get-tuple-element.28.held, s32[1,4096]{1,0:T(1,128)S(1)} %collective-permute-done.1.far_ids.ids), custom_call_target="tpu_custom_call" | custom-call | tf_op jit(solution)/shard_map/later_round/pallas_call | solution.py:287
  144.0 17.0 %all_to_all.46.parts = f32[64,4,896]{2,1,0:T(4,128)S(1)} all-to-all(f32[64,4,896]{2,1,0:T(4,128)S(1)} %later_round.3), channel_id=1, replica_groups=mesh['x'=4,'z'=4,'c'=2,'y'=4] {'x','z','y'}, dimensions={0} | all-to-all | bytes 1835008 | tf_op jit(solution)/shard_map/all_to_all | solution.py:379
  161.0 1.0 finish.7
  162.1 4.6 %all-to-all-start.7 = ((bf16[64,4,896]{2,1,0:T(4,128)(2,1)}), bf16[64,4,896]{2,1,0:T(4,128)(2,1)S(1)}, u32[]{:S(2)}, u32[]{:S(2)}) async-start(bf16[64,4,896]{2,1,0:T(4,128)(2,1)} %get-tuple-element.30), calls=%async_computation.7 | async-start | bytes 917504 | tf_op jit(solution)/shard_map/all_to_all | solution.py:379
  166.7 2.2 %collective-permute-start.5 = (f32[4,768]{1,0:T(4,128)S(1)}, f32[4,768]{1,0:T(4,128)S(1)}, u32[]{:S(2)}, u32[]{:S(2)}) collective-permute-start(f32[4,768]{1,0:T(4,128)S(1)} %get-tuple-element.31.mine), channel_id=1, source_target_pairs={{0,3},{1,0},{2,1},{3,2},{4,7},{5,4},{6,5},{7,6},{8,11},{9,8},{10,9... | collective-permute-start | bytes 36872 | tf_op jit(solution)/shard_map/ppermute | solution.py:393
  168.9 0.6 collective-permute-start.4
  169.5 0.6 collective-permute-start.3
  170.1 3.3 %collective-permute-done.4.far = f32[4,768]{1,0:T(4,128)S(1)} collective-permute-done((f32[4,768]{1,0:T(4,128)S(1)}, f32[4,768]{1,0:T(4,128)S(1)}, u32[]{:S(2)}, u32[]{:S(2)}) %collective-permute-start.4) | collective-permute-done | bytes 12320 | tf_op jit(solution)/shard_map/ppermute | solution.py:393
  173.3 0.3 collective-permute-done.3.near
  173.6 3.3 %all-to-all-done.7.packed = bf16[64,4,896]{2,1,0:T(4,128)(2,1)S(1)} async-done(((bf16[64,4,896]{2,1,0:T(4,128)(2,1)}), bf16[64,4,896]{2,1,0:T(4,128)(2,1)S(1)}, u32[]{:S(2)}, u32[]{:S(2)}) %all-to-all-start.7) | async-done | bytes 458784 | tf_op jit(solution)/shard_map/all_to_all | solution.py:379
  177.0 4.8 %assign_away.1 = (f32[8,4096]{1,0:T(8,128)S(1)}, f32[2,8,768]{2,1,0:T(8,128)}) custom-call(s32[2]{0:T(128)S(1)} %pad_add_fusion.core.place, bf16[64,4,896]{2,1,0:T(4,128)(2,1)S(1)} %all-to-all-done.7.packed, bf16[4096,768]{1,0:T(8,128)(2,1)} %collective-permute-done.2.other.members, s32[1,4096]{1,0:T(1,128)S(1)} %collective-permute-done.1.far_ids.ids, ...), custom_call_target="tpu_custom_call" | custom-call | tf_op jit(solution)/shard_map/assign_away/pallas_call | solution.py:344
  181.7 10.3 %collective-permute-start.6 = (f32[8,4096]{1,0:T(8,128)S(1)}, f32[8,4096]{1,0:T(8,128)S(1)}, u32[]{:S(2)}, u32[]{:S(2)}) collective-permute-start(f32[8,4096]{1,0:T(8,128)S(1)} %get-tuple-element.32), channel_id=1, source_target_pairs={{0,4},{4,0},{1,5},{5,1},{2,6},{6,2},{3,7},{7,3},{8,12},{12,8},{9,1... | collective-permute-start | bytes 393224 | tf_op jit(solution)/shard_map/ppermute | solution.py:374
  192.1 4.0 %assign_own.1 = f32[8,4096]{1,0:T(8,128)S(1)} custom-call(bf16[64,4,896]{2,1,0:T(4,128)(2,1)S(1)} %all-to-all-done.7.packed, bf16[4096,768]{1,0:T(8,128)(2,1)} %members.3, s32[1,4096]{1,0:T(1,128)S(1)} %get-tuple-element.21.near_ids.ids), custom_call_target="tpu_custom_call" | custom-call | tf_op jit(solution)/shard_map/assign_own/pallas_call | solution.py:357
  196.1 0.7 add.7
  (10 shorter events, 0.1 us)
Async XLA Ops:
  0.6 9.9 %slice-start = ((s8[6291456]{0:T(1024)(128)(4,1)}), s8[4194304]{0:T(1024)(128)(4,1)S(1)}, s32[]{:S(2)}) async-start(s8[6291456]{0:T(1024)(128)(4,1)} %bitcast.4), calls=%async_computation.8 | async-start | bytes 8388608
  6.7 3.6 %collective-permute-start = (f32[64,4,896]{2,1,0:T(4,128)S(1)}, f32[64,4,896]{2,1,0:T(4,128)S(1)}, u32[]{:S(2)}, u32[]{:S(2)}) collective-permute-start(f32[64,4,896]{2,1,0:T(4,128)S(1)} %get-tuple-element.20), channel_id=1, source_target_pairs={{0,4},{4,0},{1,5},{5,1},{2,6},{6,2},{3,7},{7,3},{8,12},{12,8},{9,1... | collective-permute-start | bytes 2752520 | tf_op jit(solution)/shard_map/ppermute | solution.py:374
  8.2 2.3 %collective-permute-start.1 = (s32[1,4096]{1,0:T(1,128)S(1)}, s32[1,4096]{1,0:T(1,128)S(1)}, u32[]{:S(2)}, u32[]{:S(2)}) collective-permute-start(s32[1,4096]{1,0:T(1,128)S(1)} %get-tuple-element.21.near_ids.ids), channel_id=1, source_target_pairs={{0,4},{4,0},{1,5},{5,1},{2,6},{6,2},{3,7},{7,3},{8,12},{12,8},{9,1... | collective-permute-start | bytes 49160 | tf_op jit(solution)/shard_map/ppermute | solution.py:374
  8.3 2.3 %slice-start.1 = ((s8[6291456]{0:T(1024)(128)(4,1)}), s8[2097152]{0:T(1024)(128)(4,1)S(1)}, s32[]{:S(2)}) async-start(s8[6291456]{0:T(1024)(128)(4,1)} %bitcast.4), calls=%async_computation.9 | async-start | bytes 4194304
  10.6 43.8 %collective-permute-start.2 = (bf16[4096,768]{1,0:T(8,128)(2,1)S(1)}, bf16[4096,768]{1,0:T(8,128)(2,1)}, u32[]{:S(2)}, u32[]{:S(2)}) collective-permute-start(bf16[4096,768]{1,0:T(8,128)(2,1)S(1)} %bitcast.5), channel_id=1, source_target_pairs={{0,4},{4,0},{1,5},{5,1},{2,6},{6,2},{3,7},{7,3},{8,12},{12,8},{9,1... | collective-permute-start | bytes 18874376 | tf_op jit(solution)/shard_map/ppermute | solution.py:374
  162.1 14.9 %all-to-all-start.7 = ((bf16[64,4,896]{2,1,0:T(4,128)(2,1)}), bf16[64,4,896]{2,1,0:T(4,128)(2,1)S(1)}, u32[]{:S(2)}, u32[]{:S(2)}) async-start(bf16[64,4,896]{2,1,0:T(4,128)(2,1)} %get-tuple-element.30), calls=%async_computation.7 | async-start | bytes 917504 | tf_op jit(solution)/shard_map/all_to_all | solution.py:379
  166.7 3.3 %collective-permute-start.5 = (f32[4,768]{1,0:T(4,128)S(1)}, f32[4,768]{1,0:T(4,128)S(1)}, u32[]{:S(2)}, u32[]{:S(2)}) collective-permute-start(f32[4,768]{1,0:T(4,128)S(1)} %get-tuple-element.31.mine), channel_id=1, source_target_pairs={{0,3},{1,0},{2,1},{3,2},{4,7},{5,4},{6,5},{7,6},{8,11},{9,8},{10,9... | collective-permute-start | bytes 36872 | tf_op jit(solution)/shard_map/ppermute | solution.py:393
  168.9 4.4 %collective-permute-start.4 = (f32[4,768]{1,0:T(4,128)S(1)}, f32[4,768]{1,0:T(4,128)S(1)}, u32[]{:S(2)}, u32[]{:S(2)}) collective-permute-start(f32[4,768]{1,0:T(4,128)S(1)} %get-tuple-element.31.mine), channel_id=1, source_target_pairs={{0,2},{1,3},{2,0},{3,1},{4,6},{5,7},{6,4},{7,5},{8,10},{9,11},{10,... | collective-permute-start | bytes 36872 | tf_op jit(solution)/shard_map/ppermute | solution.py:393
  169.5 4.2 %collective-permute-start.3 = (f32[4,768]{1,0:T(4,128)S(1)}, f32[4,768]{1,0:T(4,128)S(1)}, u32[]{:S(2)}, u32[]{:S(2)}) collective-permute-start(f32[4,768]{1,0:T(4,128)S(1)} %get-tuple-element.31.mine), channel_id=1, source_target_pairs={{0,1},{1,2},{2,3},{3,0},{4,5},{5,6},{6,7},{7,4},{8,9},{9,10},{10,1... | collective-permute-start | bytes 36872 | tf_op jit(solution)/shard_map/ppermute | solution.py:393
  181.7 14.3 %collective-permute-start.6 = (f32[8,4096]{1,0:T(8,128)S(1)}, f32[8,4096]{1,0:T(8,128)S(1)}, u32[]{:S(2)}, u32[]{:S(2)}) collective-permute-start(f32[8,4096]{1,0:T(8,128)S(1)} %get-tuple-element.32), channel_id=1, source_target_pairs={{0,4},{4,0},{1,5},{5,1},{2,6},{6,2},{3,7},{7,3},{8,12},{12,8},{9,1... | collective-permute-start | bytes 393224 | tf_op jit(solution)/shard_map/ppermute | solution.py:374
